TPU v7x, 32 devices: a whole 2x2x4 slice. The times are simulated.
32 devices in a mesh: section: 2 (over x), dp: 16 (over z, y, core).
Axes of the slice: x: 2, y: 2, z: 4, core: 2. Of those that a mesh axis runs over, the one named last changes fastest.
Arguments:
- section_rows: bfloat16 [2, 2048, 1024], P('section', 'dp'), may hold values from -6 to 6
- lang_ids: int32 [2048], P('dp'), may hold values from 0 to 199, as said below
- lang_table: int32 [200], replicated, may hold values from 0 to 7, as said below
- lang_counts: int32 [16, 200], P('dp'), may hold values from 4 to 210
- temp_num: int32 [200], replicated, may hold values from 1 to 16
- weights: bfloat16 [2, 1024, 32768], P('section', None, 'dp'), may hold values from -0.1875 to 0.1875
Outputs:
- grads: float32 [2, 1024, 32768], P('section', None, 'dp')
- input_grad: bfloat16 [2048, 1024], P('dp', 'section')
Inputs may be any that keep to these rules, and one draw needn't show every extreme that they name: `lang_table`: every block is named by at least one language. `lang_ids`: on each replica (each aligned block of 128 rows) at most 32 rows map to any one block through lang_table, and one block receives exactly 32 rows from every replica.
All inputs are finite; a program needn't handle non-finite values.
Results may differ from a plain program's by a relative error of at most 0.0058.
Values may be sent and summed in bfloat16 or wider, within the bound.
No kernel may reach another device: no remote copies, remote signals or barrier semaphores. Data moves between devices by JAX's collectives and lax.ppermute only.
A program may use at most 64 MiB of HBM per device.

v0:
```python
import jax
import jax.numpy as jnp
from jax import lax
from jax.sharding import PartitionSpec as P


def partner(value, axis, bit):
    mask = 2**bit
    pairs = [(source, source ^ mask) for source in range(lax.axis_size(axis))]
    return lax.ppermute(value, axis, pairs)


def shifted(value, axis, steps):
    count = lax.axis_size(axis)
    first, last = (max(0, -steps), min(count, count - steps))
    return lax.ppermute(value, axis, [(source, source + steps) for source in range(first, last)])


def on_device(section_rows, lang_ids, lang_table, lang_counts, temp_num, weights):
    section_pos = lax.axis_index("section")
    replicas = lax.axis_size("dp")
    blocks_all = replicas // 2
    rows_dev = lang_ids.shape[0]
    capacity = 2 * rows_dev // blocks_all
    row_width = section_rows.shape[2]
    half_width = row_width // 2
    languages = lang_table.shape[0]
    own_weight = weights[0]
    lang_hot = lang_ids[:, None] == jnp.arange(languages, dtype=jnp.int32)[None, :]
    row_block = jnp.sum(jnp.where(lang_hot, lang_table[None, :], 0), axis=1)
    block_hot = (row_block[:, None] == jnp.arange(blocks_all, dtype=jnp.int32)[None, :]).astype(
        jnp.int32
    )
    running = jnp.cumsum(block_hot, axis=0) - 1
    slot_index = jnp.sum(running * block_hot, axis=1)
    target = row_block * capacity + slot_index
    placing = target[None, :] == jnp.arange(blocks_all * capacity, dtype=jnp.int32)[:, None]
    totals = lax.psum(lang_counts[0].astype(jnp.float32), "dp")
    lang_scale = 2.0 * replicas * temp_num.astype(jnp.float32) / totals
    row_scale = jnp.sum(jnp.where(lang_hot, lang_scale[None, :], 0.0), axis=1)
    local_rows = section_rows[0]
    weighted = (local_rows * row_scale[:, None]).astype(jnp.bfloat16)
    outgoing = jnp.where(section_pos == 1, weighted, local_rows)
    packed = jnp.dot(
        placing.astype(jnp.bfloat16), outgoing, preferred_element_type=jnp.float32
    ).astype(jnp.bfloat16)
    packed = packed.reshape(blocks_all, capacity, row_width)
    doubled = jnp.repeat(packed, 2, axis=0)
    arrived = lax.all_to_all(doubled, "dp", split_axis=0, concat_axis=0, tiled=True)
    projected = jnp.einsum("skd,df->skf", arrived, own_weight, preferred_element_type=jnp.float32)
    routed_flat = arrived.reshape(-1, row_width)
    projected = projected.reshape(routed_flat.shape[0], -1)
    handed = jnp.where(section_pos == 0, jnp.maximum(projected, 0.0), projected).astype(
        jnp.bfloat16
    )
    received = partner(handed, "section", 0)
    partner_term = jnp.where(
        (section_pos == 0) & (projected <= 0.0), jnp.zeros_like(received), received
    )
    weight_grad = lax.dot_general(
        routed_flat, partner_term, (((0,), (0,)), ((), ())), preferred_element_type=jnp.float32
    )

    def input_terms():
        return lax.dot_general(
            partner_term, own_weight, (((1,), (1,)), ((), ())), preferred_element_type=jnp.float32
        )

    def no_terms():
        return jnp.zeros((routed_flat.shape[0], row_width), jnp.float32)

    partial_rows = lax.cond(section_pos == 0, input_terms, no_terms)
    unplace = placing.astype(jnp.float32)
    came_back = lax.all_to_all(
        partial_rows.reshape(replicas, capacity, row_width),
        "dp",
        split_axis=0,
        concat_axis=0,
        tiled=True,
    )
    summed = (
        came_back.reshape(blocks_all, 2, capacity, row_width)
        .sum(axis=1)
        .reshape(blocks_all * capacity, row_width)
    )
    full_rows = lax.dot_general(
        unplace,
        summed,
        (((0,), (0,)), ((), ())),
        precision=lax.Precision.HIGHEST,
        preferred_element_type=jnp.float32,
    ).astype(jnp.bfloat16)
    right_cols = shifted(full_rows[:, half_width:], "section", 1)
    input_grad = jnp.where(section_pos == 0, full_rows[:, :half_width], right_cols)
    return (weight_grad[None], input_grad)


def solution(mesh):
    return jax.shard_map(
        on_device,
        mesh=mesh,
        in_specs=(
            P("section", "dp", None),
            P("dp"),
            P(),
            P("dp", None),
            P(),
            P("section", None, "dp"),
        ),
        out_specs=(P("section", None, "dp"), P("dp", "section")),
        check_vma=False,
    )
```

profile of v0, /device:TPU:0, one launch (start us, length us, event | category | flops | bytes accessed | tf_op | source)
XLA Modules:
  0.0 195.4 jit_solution(13366520089438789141)
XLA Ops:
  0.6 0.7 convert_element_type.35
  1.3 34.9 %psum.7 = f32[200]{0:T(256)S(1)} all-reduce(f32[200]{0:T(256)S(1)} %bitcast.31), channel_id=1, replica_groups=mesh['section'=2,'dp'=16] {'dp'}, use_global_device_ids=true, to_apply=%region_3.4 | all-reduce | flops 200 | bytes 1600 | tf_op jit(solution)/shard_map/psum | solution.py:38
  36.2 0.8 select_reduce_fusion.1
  37.0 0.7 multiply_divide_fusion
  37.7 0.8 select_reduce_fusion
  38.5 0.1 fusion.8
  38.5 0.2 reduce_window_sum.11
  38.7 0.2 select_reduce_fusion.2
  38.9 1.3 convolution_convert_fusion
  40.2 1.1 broadcast_in_dim.46
  41.4 3.7 %all-to-all-start = ((bf16[16,32,1024]{2,1,0:T(8,128)(2,1)}), bf16[16,32,1024]{2,1,0:T(8,128)(2,1)S(1)}, u32[]{:S(2)}, u32[]{:S(2)}) async-start(bf16[16,32,1024]{2,1,0:T(8,128)(2,1)} %bitcast.3), calls=%async_computation | async-start | bytes 2097152 | tf_op jit(solution)/shard_map/all_to_all | solution.py:49
  45.0 22.9 %all-to-all-done = bf16[16,32,1024]{2,1,0:T(8,128)(2,1)S(1)} async-done(((bf16[16,32,1024]{2,1,0:T(8,128)(2,1)}), bf16[16,32,1024]{2,1,0:T(8,128)(2,1)S(1)}, u32[]{:S(2)}, u32[]{:S(2)}) %all-to-all-start) | async-done | bytes 1048608 | tf_op jit(solution)/shard_map/all_to_all | solution.py:49
  67.9 7.3 %fusion = (bf16[512,2048]{1,0:T(8,128)(2,1)}, f32[512,2048]{1,0:T(8,128)}) fusion(pred[]{:T(512)S(6)} %eq.58, bf16[512,1024]{1,0:T(8,128)(2,1)S(1)} %bitcast.29, bf16[1,1024,2048]{2,1,0:T(8,128)(2,1)} %param.13), kind=kOutput, calls=%fused_computation.2 | convolution fusion | flops 2150629376 | bytes 11534337 | tf_op jit(solution)/shard_map/skd,df->skf/dot_general | solution.py:50
  75.2 1.5 collective-permute-start
  76.7 46.8 %collective-permute-done = bf16[512,2048]{1,0:T(8,128)(2,1)S(1)} collective-permute-done((bf16[512,2048]{1,0:T(8,128)(2,1)}, bf16[512,2048]{1,0:T(8,128)(2,1)S(1)}, u32[]{:S(2)}, u32[]{:S(2)}) %collective-permute-start) | collective-permute-done | bytes 2097184 | tf_op jit(solution)/shard_map/ppermute | solution.py:10
  123.5 4.5 %and_select_fusion = bf16[512,2048]{1,0:T(8,128)(2,1)} fusion(bf16[512,2048]{1,0:T(8,128)(2,1)S(1)} %collective-permute-done, f32[512,2048]{1,0:T(8,128)} %get-tuple-element.12, pred[]{:T(512)S(6)} %eq.58), kind=kLoop, calls=%fused_computation.3 | loop fusion | flops 3145728 | bytes 8388609 | tf_op jit(solution)/shard_map/jit(_where)/select_n | solution.py:57
  128.0 5.2 %conditional.1 = (f32[512,1024]{1,0:T(8,128)S(1)}) conditional(s32[]{:T(128)} %convert_element_type.40, () %tuple.14, (bf16[512,2048]{1,0:T(8,128)(2,1)}, bf16[1024,2048]{1,0:T(8,128)(2,1)}) %tuple.20), branch_computations={%region_5.6_spmd, %region_6.7_spmd} | conditional | flops 2147483648 | bytes 8388616 | solution.py:72
  128.0 5.2 %fusion.11 = f32[512,1024]{1,0:T(8,128)S(1)} fusion(bf16[512,2048]{1,0:T(8,128)(2,1)} %get-tuple-element.4, bf16[1024,2048]{1,0:T(8,128)(2,1)} %get-tuple-element.8), kind=kOutput, calls=%fused_computation.26 | convolution fusion | flops 2147483648 | bytes 8388608 | tf_op jit(solution)/shard_map/cond/branch_1_fun/dot_general | solution.py:65
  133.2 53.7 %all_to_all.10 = f32[16,32,1024]{2,1,0:T(8,128)S(1)} all-to-all(f32[16,32,1024]{2,1,0:T(8,128)S(1)} %bitcast.26), channel_id=1, replica_groups=mesh['section'=2,'dp'=16] {'dp'}, dimensions={0} | all-to-all | bytes 4194304 | tf_op jit(solution)/shard_map/all_to_all | solution.py:74
  186.9 0.0 copy-start
  186.9 0.2 bitcast_reduce_fusion
  187.1 0.5 convolution_convert_fusion.1
  187.6 1.3 collective-permute-start.1
  188.9 0.0 copy-done
  188.9 5.8 %convolution_bitcast_fusion = f32[1,1024,2048]{2,1,0:T(8,128)} fusion(bf16[512,1024]{1,0:T(8,128)(2,1)S(1)} %bitcast.30, bf16[512,2048]{1,0:T(8,128)(2,1)S(1)} %copy-done), kind=kOutput, calls=%fused_computation.1 | convolution fusion | flops 2147483648 | bytes 11534336 | tf_op jit(solution)/shard_map/dot_general | solution.py:60
  194.8 0.0 collective-permute-done.1
  194.8 0.7 slice_select_fusion
  (2 shorter events, 0.0 us)
Async XLA Ops:
  41.4 26.6 %all-to-all-start = ((bf16[16,32,1024]{2,1,0:T(8,128)(2,1)}), bf16[16,32,1024]{2,1,0:T(8,128)(2,1)S(1)}, u32[]{:S(2)}, u32[]{:S(2)}) async-start(bf16[16,32,1024]{2,1,0:T(8,128)(2,1)} %bitcast.3), calls=%async_computation | async-start | bytes 2097152 | tf_op jit(solution)/shard_map/all_to_all | solution.py:49
  75.2 48.3 %collective-permute-start = (bf16[512,2048]{1,0:T(8,128)(2,1)}, bf16[512,2048]{1,0:T(8,128)(2,1)S(1)}, u32[]{:S(2)}, u32[]{:S(2)}) collective-permute-start(bf16[512,2048]{1,0:T(8,128)(2,1)} %get-tuple-element.11), channel_id=1, source_target_pairs={{0,16},{16,0},{1,17},{17,1},{2,18},{18,2},{3,19},{19,3},{4,20},{20... | collective-permute-start | bytes 6291464 | tf_op jit(solution)/shard_map/ppermute | solution.py:10
  186.9 2.1 %copy-start = (bf16[512,2048]{1,0:T(8,128)(2,1)S(1)}, bf16[512,2048]{1,0:T(8,128)(2,1)}, u32[]{:S(2)}) copy-start(bf16[512,2048]{1,0:T(8,128)(2,1)} %and_select_fusion) | copy-start | bytes 6291460
  187.6 7.1 %collective-permute-start.1 = (bf16[128,512]{1,0:T(8,128)(2,1)S(1)}, bf16[128,512]{1,0:T(8,128)(2,1)S(1)}, u32[]{:S(2)}, u32[]{:S(2)}) collective-permute-start(bf16[128,512]{1,0:T(8,128)(2,1)S(1)} %slice.9), channel_id=1, source_target_pairs={{0,16},{1,17},{2,18},{3,19},{4,20},{5,21},{6,22},{7,23},{8,24},{9,... | collective-permute-start | bytes 393224 | tf_op jit(solution)/shard_map/ppermute | solution.py:16
where the time goes:
time: 196 us; the launch traced here: 195 us
  blocking collectives  88.6 us (45%)
  waiting for transfers between devices  69.7 us (36%)
  matrix products  20.1 us (10%)
  other arithmetic  8.72 us (4%)
  starting transfers between devices  6.44 us (3%)
    all_to_all x1, blocking collectives, on_device(): lax.all_to_all(partial_rows.reshape(replicas, capacity, row_width), 'dp',...  53.7 us
    ppermute x1, waiting for transfers between devices, partner(): return lax.ppermute(value, axis, pairs)  46.8 us
    psum x1, blocking collectives, on_device(): totals = lax.psum(lang_counts[0].astype(jnp.float32), 'dp')  34.9 us
    all_to_all x1, waiting for transfers between devices, on_device(): lax.all_to_all(doubled, 'dp', split_axis=0, concat_axis=0, tiled=True)  22.9 us
    dot_general x1, matrix products, on_device(): jnp.einsum('skd,df->skf', arrived, own_weight, preferred_element_type=jnp...  7.29 us
    dot_general x1, matrix products, on_device(): lax.dot_general(routed_flat, partner_term, (((0,), (0,)), ((), ())), pref...  5.82 us
    dot_general x1, matrix products, input_terms(): lax.dot_general(partner_term, own_weight, (((1,), (1,)), ((), ())), prefe...  5.18 us
    select_n x1, other arithmetic, on_device(): jnp.where((section_pos == 0) & (projected <= 0.0), jnp.zeros_like(receive...  4.5 us
  transfers between devices with their start and end apart: 3, of which 2 were waited for; matrix products, arithmetic and copies ran while one was open for 3% of the time, Pallas kernels for 0%

commit v1 on v0

v1 whole, which is shorter than its diff:
```python
import jax
import jax.numpy as jnp
from jax import lax
from jax.sharding import PartitionSpec as P

HALVES = 2
PIECES = 2


def sibling(value):
    count = lax.axis_size("dp")
    return lax.ppermute(value, "dp", [(i, i ^ 1) for i in range(count)])


def across(value):
    return lax.ppermute(value, "section", [(0, 1), (1, 0)])


def same_core_exchange(value):
    count = lax.axis_size("dp")
    groups = [list(range(core, count, 2)) for core in range(2)]
    return lax.all_to_all(
        value, "dp", split_axis=0, concat_axis=0, axis_index_groups=groups, tiled=True
    )


def on_device(section_rows, lang_ids, lang_table, lang_counts, temp_num, weights):
    section_pos = lax.axis_index("section")
    is_up = section_pos == 0
    replicas = lax.axis_size("dp")
    blocks_all = replicas // 2
    rows_dev = lang_ids.shape[0]
    capacity = 2 * rows_dev // blocks_all
    half_cap = capacity // HALVES
    row_width = section_rows.shape[2]
    half_width = row_width // 2
    languages = lang_table.shape[0]
    own_weight = weights[0]
    local_rows = section_rows[0]

    lang_hot = lang_ids[:, None] == jnp.arange(languages, dtype=jnp.int32)[None, :]
    row_block = jnp.sum(jnp.where(lang_hot, lang_table[None, :], 0), axis=1)
    same = row_block[:, None] == row_block[None, :]
    earlier = jnp.arange(rows_dev)[None, :] < jnp.arange(rows_dev)[:, None]
    slot_index = jnp.sum((same & earlier).astype(jnp.int32), axis=1)
    target = (
        (slot_index // half_cap) * (blocks_all * half_cap)
        + row_block * half_cap
        + slot_index % half_cap
    )
    placing = target[None, :] == jnp.arange(blocks_all * capacity, dtype=jnp.int32)[:, None]
    place_hot = placing.astype(jnp.bfloat16)
    packed = jnp.dot(place_hot, local_rows, preferred_element_type=jnp.float32).astype(
        jnp.bfloat16
    )
    packed = packed.reshape(HALVES, blocks_all, half_cap, row_width)

    slot_lang = jnp.sum(jnp.where(placing, lang_ids[None, :], 0), axis=1)
    slot_lang = (
        slot_lang.reshape(HALVES, blocks_all, half_cap)
        .transpose(1, 0, 2)
        .reshape(blocks_all, capacity)
    )
    notes = jnp.concatenate(
        [jnp.broadcast_to(lang_counts, (blocks_all, languages)), slot_lang], axis=1
    )
    notes = jnp.repeat(notes, 2, axis=0)[:, None, :]
    notes = lax.all_to_all(notes, "dp", split_axis=0, concat_axis=0, tiled=True)[:, 0, :]
    totals = jnp.sum(notes[:, :languages].astype(jnp.float32), axis=0)
    lang_scale = 2.0 * replicas * temp_num.astype(jnp.float32) / totals
    core = lax.axis_index("dp") % 2
    came_lang = notes[:, languages:].reshape(blocks_all, 2, HALVES, half_cap)
    came_lang = jnp.where(core == 0, came_lang, came_lang[:, ::-1]).transpose(2, 1, 0, 3)
    came_hot = came_lang[..., None] == jnp.arange(languages, dtype=jnp.int32)
    came_scale = jnp.sum(jnp.where(came_hot, lang_scale, 0.0), axis=-1).reshape(HALVES, -1, 1)

    routed_parts, partner_parts, finals = [], [], []
    for half in range(HALVES):
        own = same_core_exchange(packed[half]).reshape(-1, row_width)
        other = sibling(own)
        routed = jnp.concatenate([own, other], axis=0)
        weighted = (routed * came_scale[half]).astype(jnp.bfloat16)
        routed = jnp.where(is_up, routed, weighted)
        routed_parts.append(routed)
        terms = []
        for piece in jnp.split(routed, PIECES, axis=0):
            projected = jnp.dot(piece, own_weight, preferred_element_type=jnp.float32)
            handed = jnp.where(is_up, jnp.maximum(projected, 0.0), projected).astype(jnp.bfloat16)
            received = across(handed)
            partner = jnp.where(is_up & (handed <= 0), jnp.zeros_like(received), received)
            partner_parts.append(partner)
            terms.append(
                lax.dot_general(
                    partner,
                    own_weight,
                    (((1,), (1,)), ((), ())),
                    preferred_element_type=jnp.float32,
                )
            )
        mine, theirs = terms
        summed = (mine + sibling(theirs)).astype(jnp.bfloat16)
        finals.append(same_core_exchange(summed.reshape(blocks_all, half_cap, row_width)))

    weight_grad = lax.dot_general(
        jnp.concatenate(routed_parts, axis=0),
        jnp.concatenate(partner_parts, axis=0),
        (((0,), (0,)), ((), ())),
        preferred_element_type=jnp.float32,
    )
    full_rows = lax.dot_general(
        place_hot,
        jnp.concatenate([f.reshape(-1, row_width) for f in finals], axis=0),
        (((0,), (0,)), ((), ())),
        preferred_element_type=jnp.float32,
    ).astype(jnp.bfloat16)
    right_cols = lax.ppermute(full_rows[:, half_width:], "section", [(0, 1)])
    input_grad = jnp.where(is_up, full_rows[:, :half_width], right_cols)
    return (weight_grad[None], input_grad)


def solution(mesh):
    return jax.shard_map(
        on_device,
        mesh=mesh,
        in_specs=(
            P("section", "dp", None),
            P("dp"),
            P(),
            P("dp", None),
            P(),
            P("section", None, "dp"),
        ),
        out_specs=(P("section", None, "dp"), P("dp", "section")),
        check_vma=False,
    )
```

time: 196 us -> 128 us (0.65)
  blocking collectives: 88.6 us -> 12.5 us
  starting transfers between devices: 6.44 us -> 26.2 us
  waiting for transfers between devices: 69.7 us -> 54.3 us
  matrix products: 20.1 us -> 23.5 us
  other arithmetic: 8.72 us -> 6.01 us
  local copies, waits for them, and re-layouts: 1.12 us -> 3.43 us
    all_to_all x1, blocking collectives: 53.7 us -> 12.5 us  [same_core_exchange(): lax.all_to_all(value, 'dp', split_axis=0, concat_axis=0, axis_index_group...]
    psum x1 -> x0, blocking collectives: 34.9 us -> none  [on_device(): totals = lax.psum(lang_counts[0].astype(jnp.float32), 'dp')]
    ppermute x2 -> x9, waiting for transfers between devices: 46.8 us -> 30.3 us  [the longest x4 30.3 us: across(): return lax.ppermute(value, 'section', [(0, 1), (1, 0)])]
    all_to_all x1 -> x4, starting transfers between devices: 3.66 us -> 18.4 us  [the longest x3 11 us: same_core_exchange(): lax.all_to_all(value, 'dp', split_axis=0, concat_axis=0, axis_index_group...]
    ppermute x2 -> x9, starting transfers between devices: 2.79 us -> 7.79 us  [the longest x4 4.31 us: across(): return lax.ppermute(value, 'section', [(0, 1), (1, 0)])]
    dot_general x5 -> x11, matrix products: 20.1 us -> 23.5 us  [the longest x4 9.89 us: on_device(): lax.dot_general(partner, own_weight, (((1,), (1,)), ((), ())), preferred_...]
    select_n x2 -> x7, other arithmetic: 5.17 us -> 3.17 us  [the longest x4 2.07 us: on_device(): jnp.where(is_up & (handed <= 0), jnp.zeros_like(received), received)]
    all_to_all x1 -> x4, waiting for transfers between devices: 22.9 us -> 24 us  [the longest x3 18.6 us: same_core_exchange(): lax.all_to_all(value, 'dp', split_axis=0, concat_axis=0, axis_index_group...]
  transfers between devices with their start and end apart: 3 -> 13, of which waited for: 2 -> 7; matrix products, arithmetic and copies ran while one was open for 3% -> 21% of each run, Pallas kernels for 0% -> 0%
where the time goes in v1:
time: 128 us; the launch traced here: 127 us
  waiting for transfers between devices  54.3 us (42%)
  starting transfers between devices  26.2 us (20%)
  matrix products  23.5 us (18%)
  blocking collectives  12.5 us (10%)
  other arithmetic  6.01 us (5%)
  local copies, waits for them, and re-layouts  3.43 us (3%)
    ppermute x4, waiting for transfers between devices, across(): return lax.ppermute(value, 'section', [(0, 1), (1, 0)])  30.3 us
    all_to_all x3, waiting for transfers between devices, same_core_exchange(): lax.all_to_all(value, 'dp', split_axis=0, concat_axis=0, axis_index_group...  18.6 us
    all_to_all x1, blocking collectives, same_core_exchange(): lax.all_to_all(value, 'dp', split_axis=0, concat_axis=0, axis_index_group...  12.5 us
    all_to_all x3, starting transfers between devices, same_core_exchange(): lax.all_to_all(value, 'dp', split_axis=0, concat_axis=0, axis_index_group...  11 us
    dot_general x4, matrix products, on_device(): lax.dot_general(partner, own_weight, (((1,), (1,)), ((), ())), preferred_...  9.89 us
    all_to_all x1, starting transfers between devices, on_device(): lax.all_to_all(notes, 'dp', split_axis=0, concat_axis=0, tiled=True)  7.39 us
    dot_general x1, matrix products, on_device(): lax.dot_general(jnp.concatenate(routed_parts, axis=0), jnp.concatenate(pa...  6.83 us
    all_to_all x1, waiting for transfers between devices, on_device(): lax.all_to_all(notes, 'dp', split_axis=0, concat_axis=0, tiled=True)  5.37 us
  transfers between devices with their start and end apart: 13, of which 7 were waited for; matrix products, arithmetic and copies ran while one was open for 21% of the time, Pallas kernels for 0%

profile of v1, /device:TPU:0, one launch (start us, length us, event | category | flops | bytes accessed | tf_op | source)
XLA Modules:
  0.0 126.8 jit_solution(10299659451875801075)
XLA Ops:
  0.6 0.0 copy-start
  0.6 0.8 select_reduce_fusion.2
  1.5 0.2 convert_reduce_fusion
  1.7 0.8 select_reduce_fusion.1
  2.5 0.1 reshape.84
  2.5 0.1 reshape.85
  2.6 0.7 pad.10.clone
  3.3 0.1 pad_add_fusion
  3.4 0.6 broadcast_in_dim_reshape.3
  4.0 7.4 %all-to-all-start.1 = ((s32[16,1,232]{2,1,0:T(1,128)}), s32[16,1,232]{2,1,0:T(1,128)S(1)}, u32[]{:S(2)}, u32[]{:S(2)}) async-start(s32[16,1,232]{2,1,0:T(1,128)} %broadcast_in_dim_reshape.3), calls=%async_computation.1 | async-start | bytes 32768 | tf_op jit(solution)/shard_map/all_to_all | solution.py:68
  11.4 0.0 copy-done
  11.4 0.3 convolution_convert_fusion
  11.7 0.8 fusion.76
  12.5 5.4 %all-to-all-done.1 = s32[16,1,232]{2,1,0:T(1,128)S(1)} async-done(((s32[16,1,232]{2,1,0:T(1,128)}), s32[16,1,232]{2,1,0:T(1,128)S(1)}, u32[]{:S(2)}, u32[]{:S(2)}) %all-to-all-start.1) | async-done | bytes 14880 | tf_op jit(solution)/shard_map/all_to_all | solution.py:68
  17.9 3.4 %all-to-all-start.2 = ((bf16[8,16,1024]{2,1,0:T(8,128)(2,1)}), bf16[8,16,1024]{2,1,0:T(8,128)(2,1)S(1)}, u32[]{:S(2)}, u32[]{:S(2)}) async-start(bf16[8,16,1024]{2,1,0:T(8,128)(2,1)} %bitcast.6), calls=%async_computation.2 | async-start | bytes 524288 | tf_op jit(solution)/shard_map/all_to_all | solution.py:22
  21.4 0.1 slice.37
  21.4 0.1 reshape.86
  21.6 8.8 %all-to-all-done.2 = bf16[8,16,1024]{2,1,0:T(8,128)(2,1)S(1)} async-done(((bf16[8,16,1024]{2,1,0:T(8,128)(2,1)}), bf16[8,16,1024]{2,1,0:T(8,128)(2,1)S(1)}, u32[]{:S(2)}, u32[]{:S(2)}) %all-to-all-start.2) | async-done | bytes 262176 | tf_op jit(solution)/shard_map/all_to_all | solution.py:22
  30.4 3.6 %all-to-all-start = ((bf16[8,16,1024]{2,1,0:T(8,128)(2,1)}), bf16[8,16,1024]{2,1,0:T(8,128)(2,1)S(1)}, u32[]{:S(2)}, u32[]{:S(2)}) async-start(bf16[8,16,1024]{2,1,0:T(8,128)(2,1)} %bitcast.1), calls=%async_computation | async-start | bytes 524288 | tf_op jit(solution)/shard_map/all_to_all | solution.py:22
  33.9 0.7 multiply_divide_fusion
  34.6 0.0 collective-permute-start.1
  34.6 0.3 select_reduce_fusion
  34.9 0.1 mul.52
  35.0 0.1 mul.49
  35.1 7.5 %all-to-all-done = bf16[8,16,1024]{2,1,0:T(8,128)(2,1)S(1)} async-done(((bf16[8,16,1024]{2,1,0:T(8,128)(2,1)}), bf16[8,16,1024]{2,1,0:T(8,128)(2,1)S(1)}, u32[]{:S(2)}, u32[]{:S(2)}) %all-to-all-start) | async-done | bytes 262176 | tf_op jit(solution)/shard_map/all_to_all | solution.py:22
  42.6 0.0 collective-permute-start
  42.6 0.0 collective-permute-done.1
  42.6 0.2 fusion.59
  42.8 3.1 %fusion.25 = bf16[128,2048]{1,0:T(8,128)(2,1)S(1)} fusion(bf16[1,1024,2048]{2,1,0:T(8,128)(2,1)} %param.11, pred[]{:T(512)S(6)} %eq.32, bf16[256,1024]{1,0:T(8,128)(2,1)S(1)} %fusion.59), kind=kOutput, calls=%fused_computation.25 | convolution fusion | flops 537657344 | bytes 4980737 | tf_op jit(solution)/shard_map/dot_general | solution.py:87
  45.9 1.6 %collective-permute-start.5 = (bf16[128,2048]{1,0:T(8,128)(2,1)S(1)}, bf16[128,2048]{1,0:T(8,128)(2,1)S(1)}, u32[]{:S(2)}, u32[]{:S(2)}) collective-permute-start(bf16[128,2048]{1,0:T(8,128)(2,1)S(1)} %fusion.25), channel_id=1, source_target_pairs={{0,16},{16,0},{1,17},{17,1},{2,18},{18,2},{3,19},{19,3},{4,20},{20... | collective-permute-start | bytes 1572872 | tf_op jit(solution)/shard_map/ppermute | solution.py:16
  47.4 0.0 copy-done.1
  47.4 0.7 fusion.30
  48.2 0.6 collective-permute-start.4
  48.8 0.0 collective-permute-done
  48.8 0.2 fusion.58
  49.0 0.7 fusion.35
  49.8 1.6 %collective-permute-start.3 = (bf16[128,2048]{1,0:T(8,128)(2,1)S(1)}, bf16[128,2048]{1,0:T(8,128)(2,1)S(1)}, u32[]{:S(2)}, u32[]{:S(2)}) collective-permute-start(bf16[128,2048]{1,0:T(8,128)(2,1)S(1)} %fusion.35), channel_id=1, source_target_pairs={{0,16},{16,0},{1,17},{17,1},{2,18},{18,2},{3,19},{19,3},{4,20},{20... | collective-permute-start | bytes 1572872 | tf_op jit(solution)/shard_map/ppermute | solution.py:16
  51.3 0.7 fusion.40
  52.1 0.6 collective-permute-start.2
  52.7 8.0 %collective-permute-done.5 = bf16[128,2048]{1,0:T(8,128)(2,1)S(1)} collective-permute-done((bf16[128,2048]{1,0:T(8,128)(2,1)S(1)}, bf16[128,2048]{1,0:T(8,128)(2,1)S(1)}, u32[]{:S(2)}, u32[]{:S(2)}) %collective-permute-start.5) | collective-permute-done | bytes 524320 | tf_op jit(solution)/shard_map/ppermute | solution.py:16
  60.7 0.3 and_select_fusion
  60.9 1.5 %fusion = f32[128,1024]{1,0:T(8,128)S(1)} fusion(bf16[128,2048]{1,0:T(8,128)(2,1)S(1)} %and_select_fusion, bf16[1,1024,2048]{2,1,0:T(8,128)(2,1)S(1)} %copy-done.1), kind=kOutput, calls=%fused_computation.1 | convolution fusion | flops 536870912 | bytes 5242880 | tf_op jit(solution)/shard_map/dot_general | solution.py:93
  62.5 0.1 collective-permute-start.7
  62.5 20.6 %collective-permute-done.3 = bf16[128,2048]{1,0:T(8,128)(2,1)S(1)} collective-permute-done((bf16[128,2048]{1,0:T(8,128)(2,1)S(1)}, bf16[128,2048]{1,0:T(8,128)(2,1)S(1)}, u32[]{:S(2)}, u32[]{:S(2)}) %collective-permute-start.3) | collective-permute-done | bytes 524320 | tf_op jit(solution)/shard_map/ppermute | solution.py:16
  83.1 0.3 and_select_fusion.2
  83.4 2.3 %fusion.4 = f32[128,1024]{1,0:T(8,128)} fusion(bf16[128,2048]{1,0:T(8,128)(2,1)S(1)} %and_select_fusion.2, bf16[1,1024,2048]{2,1,0:T(8,128)(2,1)S(1)} %copy-done.1), kind=kOutput, calls=%fused_computation.5 | convolution fusion | flops 536870912 | bytes 5242880 | tf_op jit(solution)/shard_map/dot_general | solution.py:93
  85.7 0.0 collective-permute-start.6
  85.7 0.0 collective-permute-done.4
  85.7 0.3 and_select_fusion.1
  86.0 0.0 collective-permute-done.7
  86.0 2.2 %fusion.49 = bf16[128,1024]{1,0:T(8,128)(2,1)} fusion(f32[128,1024]{1,0:T(8,128)S(1)} %collective-permute-done.7, bf16[128,2048]{1,0:T(8,128)(2,1)S(1)} %and_select_fusion.1, bf16[1,1024,2048]{2,1,0:T(8,128)(2,1)S(1)} %copy-done.1), kind=kOutput, calls=%fused_computation.36 | convolution fusion | flops 537133056 | bytes 5505024 | tf_op jit(solution)/shard_map/dot_general | solution.py:93
  88.2 4.0 %all-to-all-start.4 = ((bf16[8,16,1024]{2,1,0:T(8,128)(2,1)}), bf16[8,16,1024]{2,1,0:T(8,128)(2,1)}, u32[]{:S(2)}, u32[]{:S(2)}) async-start(bf16[8,16,1024]{2,1,0:T(8,128)(2,1)} %bitcast.73), calls=%async_computation.4 | async-start | bytes 524288 | tf_op jit(solution)/shard_map/all_to_all | solution.py:22
  92.3 1.7 %collective-permute-done.2 = bf16[128,2048]{1,0:T(8,128)(2,1)} collective-permute-done((bf16[128,2048]{1,0:T(8,128)(2,1)S(1)}, bf16[128,2048]{1,0:T(8,128)(2,1)}, u32[]{:S(2)}, u32[]{:S(2)}) %collective-permute-start.2) | collective-permute-done | bytes 524320 | tf_op jit(solution)/shard_map/ppermute | solution.py:16
  93.9 1.3 %and_select_fusion.3 = bf16[128,2048]{1,0:T(8,128)(2,1)S(1)} fusion(bf16[128,2048]{1,0:T(8,128)(2,1)} %collective-permute-done.2, bf16[128,2048]{1,0:T(8,128)(2,1)S(1)} %fusion.40, pred[]{:T(512)S(6)} %eq.32), kind=kLoop, calls=%fused_computation.46 | loop fusion | flops 1310720 | bytes 1572865 | tf_op jit(solution)/shard_map/jit(_where)/select_n | solution.py:90
  95.2 0.0 collective-permute-done.6
  95.2 0.8 copy-done.2
  96.0 3.8 %fusion.52 = bf16[128,1024]{1,0:T(8,128)(2,1)S(1)} fusion(f32[128,1024]{1,0:T(8,128)} %collective-permute-done.6, bf16[128,2048]{1,0:T(8,128)(2,1)S(1)} %and_select_fusion.3, bf16[1,1024,2048]{2,1,0:T(8,128)(2,1)} %param.11), kind=kOutput, calls=%fused_computation.37 | convolution fusion | flops 537133056 | bytes 5505024 | tf_op jit(solution)/shard_map/dot_general | solution.py:93
  99.9 2.3 %all-to-all-done.4 = bf16[8,16,1024]{2,1,0:T(8,128)(2,1)} async-done(((bf16[8,16,1024]{2,1,0:T(8,128)(2,1)}), bf16[8,16,1024]{2,1,0:T(8,128)(2,1)}, u32[]{:S(2)}, u32[]{:S(2)}) %all-to-all-start.4) | async-done | bytes 262176 | tf_op jit(solution)/shard_map/all_to_all | solution.py:22
  102.1 12.5 %all_to_all.25 = bf16[8,16,1024]{2,1,0:T(8,128)(2,1)S(1)} all-to-all(bf16[8,16,1024]{2,1,0:T(8,128)(2,1)S(1)} %bitcast.74), channel_id=1, replica_groups={{0,2,4,6,8,10,12,14},{1,3,5,7,9,11,13,15},{16,18,20,22,24,26,28,30},{17..., dimensions={0} | all-to-all | bytes 524288 | tf_op jit(solution)/shard_map/all_to_all | solution.py:22
  114.6 1.2 convolution_convert_fusion.1
  115.9 3.4 %collective-permute-start.8 = (bf16[128,512]{1,0:T(8,128)(2,1)S(1)}, bf16[128,512]{1,0:T(8,128)(2,1)S(1)}, u32[]{:S(2)}, u32[]{:S(2)}) collective-permute-start(bf16[128,512]{1,0:T(8,128)(2,1)S(1)} %slice.43), channel_id=1, source_target_pairs={{0,16},{1,17},{2,18},{3,19},{4,20},{5,21},{6,22},{7,23},{8,24},{9,... | collective-permute-start | bytes 393224 | tf_op jit(solution)/shard_map/ppermute | solution.py:116
  119.3 6.8 %convolution_bitcast_fusion = f32[1,1024,2048]{2,1,0:T(8,128)} fusion(bf16[128,2048]{1,0:T(8,128)(2,1)S(1)} %and_select_fusion, bf16[128,2048]{1,0:T(8,128)(2,1)S(1)} %and_select_fusion.1, bf16[128,2048]{1,0:T(8,128)(2,1)S(1)} %and_select_fusion.2, bf16[128,2048]{1,0:T(8,128)(2,1)} %copy-done.2, bf16[256,1024]{1,0:T(8,128)(2,1)S(1)} %fusion.59, ...), kind=kOutput, calls=%fused_computation | convolution fusion | flops 2157969408 | bytes 11534336 | tf_op jit(solution)/shard_map/dot_general | solution.py:104
  126.1 0.0 collective-permute-done.8
  126.1 0.7 slice_select_fusion
  (11 shorter events, 0.1 us)
Async XLA Ops:
  0.6 10.8 %copy-start = (bf16[1,128,1024]{2,1,0:T(8,128)(2,1)S(1)}, bf16[1,128,1024]{2,1,0:T(8,128)(2,1)}, u32[]{:S(2)}) copy-start(bf16[1,128,1024]{2,1,0:T(8,128)(2,1)} %param.6) | copy-start | bytes 786436
  4.0 13.9 %all-to-all-start.1 = ((s32[16,1,232]{2,1,0:T(1,128)}), s32[16,1,232]{2,1,0:T(1,128)S(1)}, u32[]{:S(2)}, u32[]{:S(2)}) async-start(s32[16,1,232]{2,1,0:T(1,128)} %broadcast_in_dim_reshape.3), calls=%async_computation.1 | async-start | bytes 32768 | tf_op jit(solution)/shard_map/all_to_all | solution.py:68
  17.9 12.5 %all-to-all-start.2 = ((bf16[8,16,1024]{2,1,0:T(8,128)(2,1)}), bf16[8,16,1024]{2,1,0:T(8,128)(2,1)S(1)}, u32[]{:S(2)}, u32[]{:S(2)}) async-start(bf16[8,16,1024]{2,1,0:T(8,128)(2,1)} %bitcast.6), calls=%async_computation.2 | async-start | bytes 524288 | tf_op jit(solution)/shard_map/all_to_all | solution.py:22
  30.4 12.2 %all-to-all-start = ((bf16[8,16,1024]{2,1,0:T(8,128)(2,1)}), bf16[8,16,1024]{2,1,0:T(8,128)(2,1)S(1)}, u32[]{:S(2)}, u32[]{:S(2)}) async-start(bf16[8,16,1024]{2,1,0:T(8,128)(2,1)} %bitcast.1), calls=%async_computation | async-start | bytes 524288 | tf_op jit(solution)/shard_map/all_to_all | solution.py:22
  34.6 7.9 %collective-permute-start.1 = (bf16[128,1024]{1,0:T(8,128)(2,1)S(1)}, bf16[128,1024]{1,0:T(8,128)(2,1)S(1)}, u32[]{:S(2)}, u32[]{:S(2)}) collective-permute-start(bf16[128,1024]{1,0:T(8,128)(2,1)S(1)} %bitcast.69), channel_id=1, source_target_pairs={{0,1},{1,0},{2,3},{3,2},{4,5},{5,4},{6,7},{7,6},{8,9},{9,8},{10,11... | collective-permute-start | bytes 786440 | tf_op jit(solution)/shard_map/ppermute | solution.py:12
  42.6 4.9 %copy-start.1 = (bf16[1,1024,2048]{2,1,0:T(8,128)(2,1)S(1)}, bf16[1,1024,2048]{2,1,0:T(8,128)(2,1)}, u32[]{:S(2)}) copy-start(bf16[1,1024,2048]{2,1,0:T(8,128)(2,1)} %param.11) | copy-start | bytes 12582916
  42.6 6.2 %collective-permute-start = (bf16[128,1024]{1,0:T(8,128)(2,1)S(1)}, bf16[128,1024]{1,0:T(8,128)(2,1)S(1)}, u32[]{:S(2)}, u32[]{:S(2)}) collective-permute-start(bf16[128,1024]{1,0:T(8,128)(2,1)S(1)} %bitcast.71), channel_id=1, source_target_pairs={{0,1},{1,0},{2,3},{3,2},{4,5},{5,4},{6,7},{7,6},{8,9},{9,8},{10,11... | collective-permute-start | bytes 786440 | tf_op jit(solution)/shard_map/ppermute | solution.py:12
  45.9 14.8 %collective-permute-start.5 = (bf16[128,2048]{1,0:T(8,128)(2,1)S(1)}, bf16[128,2048]{1,0:T(8,128)(2,1)S(1)}, u32[]{:S(2)}, u32[]{:S(2)}) collective-permute-start(bf16[128,2048]{1,0:T(8,128)(2,1)S(1)} %fusion.25), channel_id=1, source_target_pairs={{0,16},{16,0},{1,17},{17,1},{2,18},{18,2},{3,19},{19,3},{4,20},{20... | collective-permute-start | bytes 1572872 | tf_op jit(solution)/shard_map/ppermute | solution.py:16
  48.2 37.5 %collective-permute-start.4 = (bf16[128,2048]{1,0:T(8,128)(2,1)S(1)}, bf16[128,2048]{1,0:T(8,128)(2,1)S(1)}, u32[]{:S(2)}, u32[]{:S(2)}) collective-permute-start(bf16[128,2048]{1,0:T(8,128)(2,1)S(1)} %fusion.30), channel_id=1, source_target_pairs={{0,16},{16,0},{1,17},{17,1},{2,18},{18,2},{3,19},{19,3},{4,20},{20... | collective-permute-start | bytes 1572872 | tf_op jit(solution)/shard_map/ppermute | solution.py:16
  49.8 33.4 %collective-permute-start.3 = (bf16[128,2048]{1,0:T(8,128)(2,1)S(1)}, bf16[128,2048]{1,0:T(8,128)(2,1)S(1)}, u32[]{:S(2)}, u32[]{:S(2)}) collective-permute-start(bf16[128,2048]{1,0:T(8,128)(2,1)S(1)} %fusion.35), channel_id=1, source_target_pairs={{0,16},{16,0},{1,17},{17,1},{2,18},{18,2},{3,19},{19,3},{4,20},{20... | collective-permute-start | bytes 1572872 | tf_op jit(solution)/shard_map/ppermute | solution.py:16
  52.1 41.8 %collective-permute-start.2 = (bf16[128,2048]{1,0:T(8,128)(2,1)S(1)}, bf16[128,2048]{1,0:T(8,128)(2,1)}, u32[]{:S(2)}, u32[]{:S(2)}) collective-permute-start(bf16[128,2048]{1,0:T(8,128)(2,1)S(1)} %fusion.40), channel_id=1, source_target_pairs={{0,16},{16,0},{1,17},{17,1},{2,18},{18,2},{3,19},{19,3},{4,20},{20... | collective-permute-start | bytes 1572872 | tf_op jit(solution)/shard_map/ppermute | solution.py:16
  62.5 23.5 %collective-permute-start.7 = (f32[128,1024]{1,0:T(8,128)S(1)}, f32[128,1024]{1,0:T(8,128)S(1)}, u32[]{:S(2)}, u32[]{:S(2)}) collective-permute-start(f32[128,1024]{1,0:T(8,128)S(1)} %fusion), channel_id=1, source_target_pairs={{0,1},{1,0},{2,3},{3,2},{4,5},{5,4},{6,7},{7,6},{8,9},{9,8},{10,11... | collective-permute-start | bytes 1572872 | tf_op jit(solution)/shard_map/ppermute | solution.py:12
  85.7 9.5 %collective-permute-start.6 = (f32[128,1024]{1,0:T(8,128)}, f32[128,1024]{1,0:T(8,128)}, u32[]{:S(2)}, u32[]{:S(2)}) collective-permute-start(f32[128,1024]{1,0:T(8,128)} %fusion.4), channel_id=1, source_target_pairs={{0,1},{1,0},{2,3},{3,2},{4,5},{5,4},{6,7},{7,6},{8,9},{9,8},{10,11... | collective-permute-start | bytes 1572872 | tf_op jit(solution)/shard_map/ppermute | solution.py:12
  88.2 13.9 %all-to-all-start.4 = ((bf16[8,16,1024]{2,1,0:T(8,128)(2,1)}), bf16[8,16,1024]{2,1,0:T(8,128)(2,1)}, u32[]{:S(2)}, u32[]{:S(2)}) async-start(bf16[8,16,1024]{2,1,0:T(8,128)(2,1)} %bitcast.73), calls=%async_computation.4 | async-start | bytes 524288 | tf_op jit(solution)/shard_map/all_to_all | solution.py:22
  95.2 0.8 copy-start.2
  115.9 10.2 %collective-permute-start.8 = (bf16[128,512]{1,0:T(8,128)(2,1)S(1)}, bf16[128,512]{1,0:T(8,128)(2,1)S(1)}, u32[]{:S(2)}, u32[]{:S(2)}) collective-permute-start(bf16[128,512]{1,0:T(8,128)(2,1)S(1)} %slice.43), channel_id=1, source_target_pairs={{0,16},{1,17},{2,18},{3,19},{4,20},{5,21},{6,22},{7,23},{8,24},{9,... | collective-permute-start | bytes 393224 | tf_op jit(solution)/shard_map/ppermute | solution.py:116

commit v2 on v1

v2 whole, which is shorter than its diff:
```python
import jax
import jax.numpy as jnp
from jax import lax
from jax.sharding import PartitionSpec as P

F32 = jnp.float32
BF16 = jnp.bfloat16


def sibling(value):
    count = lax.axis_size("dp")
    return lax.ppermute(value, "dp", [(i, i ^ 1) for i in range(count)])


def relation(value, rel):
    count = lax.axis_size("dp")
    return lax.ppermute(value, "dp", [(i, i ^ (2 * rel)) for i in range(count)])


def across(value):
    return lax.ppermute(value, "section", [(0, 1), (1, 0)])


def same_core_exchange(value):
    count = lax.axis_size("dp")
    groups = [list(range(core, count, 2)) for core in range(2)]
    return lax.all_to_all(
        value, "dp", split_axis=0, concat_axis=0, axis_index_groups=groups, tiled=True
    )


def chip_piece(stack, chip):
    return lax.dynamic_index_in_dim(stack, chip, axis=0, keepdims=False)


def on_device(section_rows, lang_ids, lang_table, lang_counts, temp_num, weights):
    is_up = lax.axis_index("section") == 0
    replicas = lax.axis_size("dp")
    place_index = lax.axis_index("dp")
    chip = place_index // 2
    core = place_index % 2
    chips = replicas // 2
    unit = chips // 8
    rows_dev = lang_ids.shape[0]
    capacity = 2 * rows_dev // chips
    row_width = section_rows.shape[2]
    half_width = row_width // 2
    languages = lang_table.shape[0]
    own_weight = weights[0]
    local_rows = section_rows[0]

    lang_hot = lang_ids[:, None] == jnp.arange(languages, dtype=jnp.int32)[None, :]
    row_block = jnp.sum(jnp.where(lang_hot, lang_table[None, :], 0), axis=1)
    same = row_block[:, None] == row_block[None, :]
    earlier = jnp.arange(rows_dev)[None, :] < jnp.arange(rows_dev)[:, None]
    slot_index = jnp.sum((same & earlier).astype(jnp.int32), axis=1)
    target = row_block * capacity + slot_index
    row_rel = row_block ^ chip
    near_target = row_rel * capacity + slot_index
    placing = target[None, :] == jnp.arange(chips * capacity, dtype=jnp.int32)[:, None]
    place_hot = placing.astype(BF16)
    packed = jnp.dot(place_hot, local_rows, preferred_element_type=F32).astype(BF16)
    packed = packed.reshape(chips, capacity, row_width)
    near_rows = jnp.concatenate([chip_piece(packed, chip ^ r) for r in range(2 * unit)], axis=0)

    came = same_core_exchange(packed)
    near_other = sibling(near_rows)
    size0 = unit * capacity
    rows_own = jnp.concatenate([near_rows[:size0], near_other[:size0]], axis=0)
    rows_next = jnp.concatenate([near_rows[size0:], near_other[size0:]], axis=0)
    if unit == 1:
        rows_next = relation(rows_next, 1)
    else:
        shaped = rows_next.reshape(2 * unit, capacity, row_width)
        rows_own_list = rows_own.reshape(2 * unit, capacity, row_width)
        moved = [
            relation(jnp.stack([rows_own_list[r], rows_own_list[unit + r]]), r)
            for r in range(1, unit)
        ]
        moved = [jnp.stack([rows_own_list[0], rows_own_list[unit]])] + moved
        rows_own = jnp.stack(moved, axis=1).reshape(-1, row_width)
        moved = [
            relation(jnp.stack([shaped[r], shaped[unit + r]]), unit + r) for r in range(unit)
        ]
        rows_next = jnp.stack(moved, axis=1).reshape(-1, row_width)

    def rels(first, last):
        return list(range(first * unit, last * unit))

    far_groups = [rels(4, 6), rels(6, 8), rels(2, 4)]
    far_own = jnp.concatenate(
        [chip_piece(came, chip ^ r) for group in far_groups for r in group], axis=0
    )
    far_other = sibling(far_own)
    groups = [rels(0, 1), rels(1, 2)] + far_groups
    group_rows = [rows_own, rows_next]
    size = 2 * unit * capacity
    for i in range(len(far_groups)):
        group_rows.append(
            jnp.concatenate(
                [far_own[i * size : (i + 1) * size], far_other[i * size : (i + 1) * size]], axis=0
            )
        )

    slot_lang = jnp.sum(jnp.where(placing, lang_ids[None, :], 0), axis=1)
    slot_lang = slot_lang.reshape(chips, capacity)
    notes = jnp.concatenate(
        [jnp.broadcast_to(lang_counts, (chips, languages)), slot_lang], axis=1
    )
    notes = jnp.repeat(notes, 2, axis=0)[:, None, :]

    handed, received = [], []
    for i, rows in enumerate(group_rows):
        projected = jnp.dot(rows, own_weight, preferred_element_type=F32)
        hand = jnp.where(is_up, jnp.maximum(projected, 0.0), projected).astype(BF16)
        handed.append(hand)
        received.append(across(hand))
        if i == 2:
            notes, _ = lax.optimization_barrier((notes, hand))

    notes = lax.all_to_all(notes, "dp", split_axis=0, concat_axis=0, tiled=True)[:, 0, :]
    totals = jnp.sum(notes[:, :languages].astype(F32), axis=0)
    lang_scale = 2.0 * replicas * temp_num.astype(F32) / totals
    came_lang = notes[:, languages:].reshape(chips, 2, capacity)
    came_lang = jnp.where(core == 0, came_lang, came_lang[:, ::-1])
    came_hot = came_lang[..., None] == jnp.arange(languages, dtype=jnp.int32)
    came_scale = jnp.sum(jnp.where(came_hot, lang_scale, 0.0), axis=-1)
    rel_scale = [chip_piece(came_scale, chip ^ r) for r in range(chips)]

    direct = rels(0, 1) + rels(2, 4)
    scaled_rows, partners, sums = [], [], {}
    for i, (group, rows, hand, recv) in enumerate(zip(groups, group_rows, handed, received)):
        if i < 2:
            recv, _ = lax.optimization_barrier((recv, handed[-1]))
        if i == len(groups) - 1:
            stack = jnp.stack([sums[r] if r not in direct else sums[unit] for r in range(chips)])
            stack = jnp.stack([chip_piece(stack, chip ^ j) for j in range(chips)])
            recv, stack = lax.optimization_barrier((recv, stack))
        partner = jnp.where(is_up & (hand <= 0), jnp.zeros_like(recv), recv)
        partners.append(partner)
        count = rows.shape[0] // 2
        terms = [
            lax.dot_general(
                part, own_weight, (((1,), (1,)), ((), ())), preferred_element_type=F32
            )
            for part in (partner[:count], partner[count:])
        ]
        scale = jnp.stack([rel_scale[r] for r in group], axis=1).reshape(-1, 1)
        scaled_rows.append((rows * scale).astype(BF16))
        summed = ((terms[0] + sibling(terms[1])) * scale[:count]).astype(BF16)
        for j, r in enumerate(group):
            sums[r] = summed[j * capacity : (j + 1) * capacity]

    back = same_core_exchange(stack)
    final = [back.reshape(-1, row_width)]
    far_hot = jnp.where((row_rel >= 2 * unit) & (row_rel < 4 * unit), -1, target)
    far_hot = jnp.where(row_rel < unit, -1, far_hot)
    hots = [
        (far_hot[None, :] == jnp.arange(chips * capacity, dtype=jnp.int32)[:, None]).astype(BF16)
    ]
    for r in direct:
        final.append(relation(sums[r], r) if r else sums[r])
        hots.append(
            (
                near_target[None, :]
                == (r * capacity + jnp.arange(capacity, dtype=jnp.int32))[:, None]
            ).astype(BF16)
        )
    weight_grad = lax.dot_general(
        jnp.concatenate(scaled_rows, axis=0),
        jnp.concatenate(partners, axis=0),
        (((0,), (0,)), ((), ())),
        preferred_element_type=F32,
    )
    full_rows = lax.dot_general(
        jnp.concatenate(hots, axis=0),
        jnp.concatenate(final, axis=0),
        (((0,), (0,)), ((), ())),
        preferred_element_type=F32,
    ).astype(BF16)
    right_cols = lax.ppermute(full_rows[:, half_width:], "section", [(0, 1)])
    input_grad = jnp.where(is_up, full_rows[:, :half_width], right_cols)
    return (weight_grad[None], input_grad)


def solution(mesh):
    return jax.shard_map(
        on_device,
        mesh=mesh,
        in_specs=(
            P("section", "dp", None),
            P("dp"),
            P(),
            P("dp", None),
            P(),
            P("section", None, "dp"),
        ),
        out_specs=(P("section", None, "dp"), P("dp", "section")),
        check_vma=False,
    )
```

time: 128 us -> 133 us (1.039)
  waiting for transfers between devices: 54.3 us -> 22.6 us
  local copies, waits for them, and re-layouts: 3.43 us -> 17.5 us
  other arithmetic: 6.01 us -> 20 us
  matrix products: 23.5 us -> 37.4 us
  blocking collectives: 12.5 us -> 0 us
  starting transfers between devices: 26.2 us -> 33.3 us
    ppermute x4 -> x5, waiting for transfers between devices: 30.3 us -> 9.38 us  [across(): return lax.ppermute(value, 'section', [(0, 1), (1, 0)])]
    dot_general x11 -> x18, matrix products: 23.5 us -> 37.4 us  [the longest x10 20.5 us: on_device(): lax.dot_general(part, own_weight, (((1,), (1,)), ((), ())), preferred_ele...]
    all_to_all x1 -> x0, blocking collectives: 12.5 us -> none  [same_core_exchange(): lax.all_to_all(value, 'dp', split_axis=0, concat_axis=0, axis_index_group...]
    unnamed x0 -> x8, other arithmetic: none -> 11.8 us
    all_to_all x3 -> x2, waiting for transfers between devices: 18.6 us -> 8.91 us  [same_core_exchange(): lax.all_to_all(value, 'dp', split_axis=0, concat_axis=0, axis_index_group...]
    mul x2 -> x10, local copies, waits for them, and re-layouts: 0.16 us -> 6.57 us  [the longest x5 3.3 us: on_device(): scaled_rows.append((rows * scale).astype(BF16))]
    unnamed x7 -> x79, local copies, waits for them, and re-layouts: 0.79 us -> 6.53 us
    ppermute x0 -> x3, starting transfers between devices: none -> 5.62 us  [relation(): return lax.ppermute(value, 'dp', [(i, i ^ 2 * rel) for i in range(count)])]
  transfers between devices with their start and end apart: 13 -> 19, of which waited for: 7 -> 5; matrix products, arithmetic and copies ran while one was open for 21% -> 54% of each run, Pallas kernels for 0% -> 0%
where the time goes in v2:
time: 133 us; the launch traced here: 132 us
  matrix products  37.4 us (28%)
  starting transfers between devices  33.3 us (25%)
  waiting for transfers between devices  22.6 us (17%)
  other arithmetic  20 us (15%)
  local copies, waits for them, and re-layouts  17.5 us (13%)
    dot_general x10, matrix products, on_device(): lax.dot_general(part, own_weight, (((1,), (1,)), ((), ())), preferred_ele...  20.5 us
    all_to_all x2, starting transfers between devices, same_core_exchange(): lax.all_to_all(value, 'dp', split_axis=0, concat_axis=0, axis_index_group...  13.1 us
    unnamed x8, other arithmetic  11.8 us
    ppermute x5, waiting for transfers between devices, across(): return lax.ppermute(value, 'section', [(0, 1), (1, 0)])  9.38 us
    all_to_all x2, waiting for transfers between devices, same_core_exchange(): lax.all_to_all(value, 'dp', split_axis=0, concat_axis=0, axis_index_group...  8.91 us
    dot_general x5, matrix products, on_device(): projected = jnp.dot(rows, own_weight, preferred_element_type=F32)  8.52 us
    dot_general x1, matrix products, on_device(): lax.dot_general(jnp.concatenate(scaled_rows, axis=0), jnp.concatenate(par...  7.01 us
    unnamed x79, local copies, waits for them, and re-layouts  6.53 us
  transfers between devices with their start and end apart: 19, of which 5 were waited for; matrix products, arithmetic and copies ran while one was open for 54% of the time, Pallas kernels for 0%

profile of v2, /device:TPU:0, one launch (start us, length us, event | category | flops | bytes accessed | tf_op | source)
XLA Modules:
  0.0 132.0 jit_solution(16537259894582516003)
XLA Ops:
  0.7 0.8 select_reduce_fusion.2
  1.7 1.1 convolution_convert_fusion
  2.8 7.3 %all-to-all-start = ((bf16[8,32,1024]{2,1,0:T(8,128)(2,1)}), bf16[8,32,1024]{2,1,0:T(8,128)(2,1)S(1)}, u32[]{:S(2)}, u32[]{:S(2)}) async-start(bf16[8,32,1024]{2,1,0:T(8,128)(2,1)} %bitcast.1), calls=%async_computation | async-start | bytes 1048576 | tf_op jit(solution)/shard_map/all_to_all | solution.py:27
  10.1 0.9 dynamic-slice_bitcast_fusion.6
  11.1 0.8 select_reduce_fusion.1
  11.8 0.7 pad.25.clone
  12.7 0.6 broadcast_in_dim_reshape.3
  13.3 0.6 iota_compare_fusion.1
  13.9 0.7 iota_compare_fusion.6
  14.6 2.1 %collective-permute-start.2 = (bf16[64,1024]{1,0:T(8,128)(2,1)S(1)}, bf16[64,1024]{1,0:T(8,128)(2,1)S(1)}, u32[]{:S(2)}, u32[]{:S(2)}) collective-permute-start(bf16[64,1024]{1,0:T(8,128)(2,1)S(1)} %pad_maximum_fusion.5), channel_id=1, source_target_pairs={{0,2},{1,3},{2,0},{3,1},{4,6},{5,7},{6,4},{7,5},{8,10},{9,11},{10,... | collective-permute-start | bytes 393224 | tf_op jit(solution)/shard_map/ppermute | solution.py:17
  16.7 7.8 %all-to-all-done = bf16[8,32,1024]{2,1,0:T(8,128)(2,1)S(1)} async-done(((bf16[8,32,1024]{2,1,0:T(8,128)(2,1)}), bf16[8,32,1024]{2,1,0:T(8,128)(2,1)S(1)}, u32[]{:S(2)}, u32[]{:S(2)}) %all-to-all-start) | async-done | bytes 524320 | tf_op jit(solution)/shard_map/all_to_all | solution.py:27
  24.6 0.6 constant_dynamic-update-slice_fusion.3
  25.3 0.6 constant_dynamic-update-slice_fusion.2
  26.0 3.0 %fusion.100 = bf16[64,2048]{1,0:T(8,128)(2,1)S(1)} fusion(bf16[1,1024,2048]{2,1,0:T(8,128)(2,1)} %param.11, pred[]{:T(512)S(6)} %eq.118, bf16[32,1024]{1,0:T(8,128)(2,1)S(1)} %get-tuple-element.35, bf16[32,1024]{1,0:T(8,128)(2,1)S(1)} %get-tuple-element.42), kind=kOutput, calls=%fused_computation.61 | convolution fusion | flops 269090816 | bytes 4587521 | tf_op jit(solution)/shard_map/dot_general | solution.py:114
  29.1 1.6 %collective-permute-start.3 = (bf16[64,2048]{1,0:T(8,128)(2,1)S(1)}, bf16[64,2048]{1,0:T(8,128)(2,1)S(1)}, u32[]{:S(2)}, u32[]{:S(2)}) collective-permute-start(bf16[64,2048]{1,0:T(8,128)(2,1)S(1)} %fusion.100), channel_id=1, source_target_pairs={{0,16},{16,0},{1,17},{17,1},{2,18},{18,2},{3,19},{19,3},{4,20},{20... | collective-permute-start | bytes 786440 | tf_op jit(solution)/shard_map/ppermute | solution.py:21
  30.6 0.9 fusion.95
  32.2 0.7 fusion.37
  32.9 1.6 %collective-permute-start.7 = (bf16[128,2048]{1,0:T(8,128)(2,1)S(1)}, bf16[128,2048]{1,0:T(8,128)(2,1)S(1)}, u32[]{:S(2)}, u32[]{:S(2)}) collective-permute-start(bf16[128,2048]{1,0:T(8,128)(2,1)S(1)} %fusion.37), channel_id=1, source_target_pairs={{0,16},{16,0},{1,17},{17,1},{2,18},{18,2},{3,19},{19,3},{4,20},{20... | collective-permute-start | bytes 1572872 | tf_op jit(solution)/shard_map/ppermute | solution.py:21
  34.5 9.4 %collective-permute-done.4 = bf16[64,2048]{1,0:T(8,128)(2,1)S(1)} collective-permute-done((bf16[64,2048]{1,0:T(8,128)(2,1)S(1)}, bf16[64,2048]{1,0:T(8,128)(2,1)S(1)}, u32[]{:S(2)}, u32[]{:S(2)}) %collective-permute-start.4) | collective-permute-done | bytes 262176 | tf_op jit(solution)/shard_map/ppermute | solution.py:21
  43.9 0.7 copy-done.17
  44.6 0.7 fusion.42
  45.3 1.6 %collective-permute-start.5 = (bf16[128,2048]{1,0:T(8,128)(2,1)S(1)}, bf16[128,2048]{1,0:T(8,128)(2,1)}, u32[]{:S(2)}, u32[]{:S(2)}) collective-permute-start(bf16[128,2048]{1,0:T(8,128)(2,1)S(1)} %fusion.42), channel_id=1, source_target_pairs={{0,16},{16,0},{1,17},{17,1},{2,18},{18,2},{3,19},{19,3},{4,20},{20... | collective-permute-start | bytes 1572872 | tf_op jit(solution)/shard_map/ppermute | solution.py:21
  46.9 3.8 %all-to-all-start.1 = ((s32[16,1,232]{2,1,0:T(1,128)}), s32[16,1,232]{2,1,0:T(1,128)S(1)}, u32[]{:S(2)}, u32[]{:S(2)}) async-start(s32[16,1,232]{2,1,0:T(1,128)} %broadcast_in_dim_reshape.3), calls=%async_computation.1 | async-start | bytes 32768 | tf_op jit(solution)/shard_map/all_to_all | solution.py:121
  50.7 3.1 %fusion.32 = bf16[128,2048]{1,0:T(8,128)(2,1)S(1)} fusion(bf16[1,1024,2048]{2,1,0:T(8,128)(2,1)} %param.11, pred[]{:T(512)S(6)} %eq.118, bf16[64,1024]{1,0:T(8,128)(2,1)S(1)} %get-tuple-element.37, bf16[32,1024]{1,0:T(8,128)(2,1)} %get-tuple-element.27, bf16[32,1024]{1,0:T(8,128)(2,1)} %get-tuple-element.29), kind=kOutput, calls=%fused_computation.32 | convolution fusion | flops 538443776 | bytes 4980737 | tf_op jit(solution)/shard_map/dot_general | solution.py:114
  54.5 0.8 constant_dynamic-update-slice_fusion.26
  55.3 1.8 %constant_dynamic-update-slice_fusion.25 = (bf16[512,2048]{1,0:T(8,128)(2,1)}, bf16[64,2048]{1,0:T(8,128)(2,1)S(1)}) fusion(bf16[512,2048]{1,0:T(8,128)(2,1)} %get-tuple-element.20, bf16[64,2048]{1,0:T(8,128)(2,1)} %copy-done.17, bf16[64,2048]{1,0:T(8,128)(2,1)S(1)} %fusion.95, pred[]{:T(512)S(6)} %eq.118), kind=kLoop, calls=%fused_computation.138 | loop fusion | flops 655360 | bytes 1048577
  57.1 2.0 %fusion.16 = f32[32,1024]{1,0:T(8,128)} fusion(bf16[1,1024,2048]{2,1,0:T(8,128)(2,1)S(1)} %copy-done.2, bf16[64,2048]{1,0:T(8,128)(2,1)S(1)} %get-tuple-element.19), kind=kOutput, calls=%fused_computation.17 | convolution fusion | flops 134217728 | bytes 4456448 | tf_op jit(solution)/shard_map/dot_general | solution.py:143
  59.1 2.0 %fusion.4 = f32[32,1024]{1,0:T(8,128)} fusion(bf16[1,1024,2048]{2,1,0:T(8,128)(2,1)S(1)} %copy-done.2, bf16[64,2048]{1,0:T(8,128)(2,1)S(1)} %get-tuple-element.21), kind=kOutput, calls=%fused_computation.5 | convolution fusion | flops 134217728 | bytes 4456448 | tf_op jit(solution)/shard_map/dot_general | solution.py:143
  62.3 0.7 multiply_divide_fusion
  65.6 1.3 mul.129
  66.9 0.7 mul.126
  68.2 1.2 mul.147
  69.4 1.3 mul.144
  70.7 0.7 copy.14
  72.1 1.6 %fusion.127 = bf16[512,1024]{1,0:T(8,128)(2,1)} fusion(f32[64]{0:T(128)} %mul.126, bf16[32,1024]{1,0:T(8,128)(2,1)S(1)} %get-tuple-element.42, bf16[32,1024]{1,0:T(8,128)(2,1)S(1)} %get-tuple-element.35), kind=kLoop, calls=%fused_computation.100 | loop fusion | flops 393215 | bytes 262400
  73.7 1.5 %fusion.128 = bf16[512,1024]{1,0:T(8,128)(2,1)} fusion(bf16[512,1024]{1,0:T(8,128)(2,1)} %fusion.127, bf16[64,1024]{1,0:T(8,128)(2,1)S(1)} %collective-permute-done.2, f32[64]{0:T(128)} %mul.129), kind=kLoop, calls=%fused_computation.101 | loop fusion | flops 196608 | bytes 262656
  75.2 1.7 %fusion.110 = bf16[512,1024]{1,0:T(8,128)(2,1)} fusion(bf16[512,1024]{1,0:T(8,128)(2,1)} %fusion.128, f32[128]{0:T(128)} %mul.132, bf16[64,1024]{1,0:T(8,128)(2,1)S(1)} %copy-done.8, bf16[32,1024]{1,0:T(8,128)(2,1)} %copy-done.14, bf16[32,1024]{1,0:T(8,128)(2,1)} %copy-done.13), kind=kLoop, calls=%fused_computation.76 | loop fusion | flops 1048576 | bytes 524800
  76.9 1.7 %fusion.111 = bf16[512,1024]{1,0:T(8,128)(2,1)} fusion(bf16[512,1024]{1,0:T(8,128)(2,1)} %fusion.110, f32[128]{0:T(128)S(1)} %mul.135, bf16[64,1024]{1,0:T(8,128)(2,1)S(1)} %copy-done.6, bf16[32,1024]{1,0:T(8,128)(2,1)} %get-tuple-element.27, bf16[32,1024]{1,0:T(8,128)(2,1)} %get-tuple-element.29), kind=kLoop, calls=%fused_computation.77 | loop fusion | flops 1048576 | bytes 524800
  78.6 0.7 slice_bitcast_fusion.5
  79.3 3.5 %constant_dynamic-update-slice_fusion.13 = (bf16[8,32,1024]{2,1,0:T(8,128)(2,1)S(1)}, bf16[1,32,1024]{2,1,0:T(8,128)(2,1)S(1)}) fusion(f32[32]{0:T(128)S(1)} %slice_bitcast_fusion.5, f32[32,1024]{1,0:T(8,128)} %collective-permute-done.8, bf16[1,1024,2048]{2,1,0:T(8,128)(2,1)} %param.11, bf16[64,2048]{1,0:T(8,128)(2,1)S(1)} %get-tuple-element.19), kind=kOutput, calls=%fused_computation.126 | convolution fusion | flops 134316032 | bytes 4588032 | tf_op jit(solution)/shard_map/dot_general | solution.py:143
  82.9 1.3 %constant_dynamic-update-slice_fusion.24 = (bf16[512,2048]{1,0:T(8,128)(2,1)S(1)}, bf16[128,2048]{1,0:T(8,128)(2,1)S(1)}) fusion(bf16[512,2048]{1,0:T(8,128)(2,1)S(1)} %copy-done.19, bf16[128,2048]{1,0:T(8,128)(2,1)} %collective-permute-done.5, bf16[128,2048]{1,0:T(8,128)(2,1)S(1)} %fusion.42, pred[]{:T(512)S(6)} %eq.118), kind=kLoop, calls=%fused_computation.137 | loop fusion | flops 1310720 | bytes 2097153
  84.2 1.4 %fusion.12 = f32[64,1024]{1,0:T(8,128)S(1)} fusion(bf16[1,1024,2048]{2,1,0:T(8,128)(2,1)S(1)} %copy-done.3, bf16[128,2048]{1,0:T(8,128)(2,1)S(1)} %get-tuple-element.17), kind=kOutput, calls=%fused_computation.13 | convolution fusion | flops 268435456 | bytes 4718592 | tf_op jit(solution)/shard_map/dot_general | solution.py:143
  85.9 1.3 constant_dynamic-update-slice_fusion.23
  87.2 1.4 %fusion.8 = f32[64,1024]{1,0:T(8,128)S(1)} fusion(bf16[1,1024,2048]{2,1,0:T(8,128)(2,1)S(1)} %copy-done.3, bf16[128,2048]{1,0:T(8,128)(2,1)S(1)} %get-tuple-element.15), kind=kOutput, calls=%fused_computation.9 | convolution fusion | flops 268435456 | bytes 4718592 | tf_op jit(solution)/shard_map/dot_general | solution.py:143
  89.0 1.4 %fusion.69 = bf16[64,1024]{1,0:T(8,128)(2,1)S(1)} fusion(f32[64,1024]{1,0:T(8,128)S(1)} %collective-permute-done.9, bf16[1,1024,2048]{2,1,0:T(8,128)(2,1)S(1)} %copy-done.3, bf16[128,2048]{1,0:T(8,128)(2,1)S(1)} %get-tuple-element.17, f32[64]{0:T(128)S(1)} %copy-done.29), kind=kOutput, calls=%fused_computation.47 | convolution fusion | flops 268632064 | bytes 4850176 | tf_op jit(solution)/shard_map/dot_general | solution.py:143
  90.4 1.4 %fusion.66 = bf16[64,1024]{1,0:T(8,128)(2,1)S(1)} fusion(f32[64,1024]{1,0:T(8,128)S(1)} %collective-permute-done.10, bf16[1,1024,2048]{2,1,0:T(8,128)(2,1)S(1)} %copy-done.3, bf16[128,2048]{1,0:T(8,128)(2,1)S(1)} %get-tuple-element.15, f32[64]{0:T(128)S(1)} %copy-done.28), kind=kOutput, calls=%fused_computation.46 | convolution fusion | flops 268632064 | bytes 4850176 | tf_op jit(solution)/shard_map/dot_general | solution.py:143
  91.9 0.6 constant_dynamic-update-slice_fusion.21
  93.1 0.6 constant_dynamic-update-slice_fusion.19
  94.4 0.6 constant_dynamic-update-slice_fusion.17
  95.6 0.6 constant_dynamic-update-slice_fusion.15
  96.3 0.6 constant_dynamic-update-slice_fusion.14
  97.2 1.4 %fusion = f32[64,1024]{1,0:T(8,128)S(1)} fusion(bf16[1,1024,2048]{2,1,0:T(8,128)(2,1)S(1)} %copy-done.3, bf16[128,2048]{1,0:T(8,128)(2,1)S(1)} %get-tuple-element.13), kind=kOutput, calls=%fused_computation.1 | convolution fusion | flops 268435456 | bytes 4718592 | tf_op jit(solution)/shard_map/dot_general | solution.py:143
  98.8 0.8 fusion.112
  99.6 5.8 %all-to-all-start.2 = ((bf16[8,32,1024]{2,1,0:T(8,128)(2,1)}), bf16[8,32,1024]{2,1,0:T(8,128)(2,1)S(1)}, u32[]{:S(2)}, u32[]{:S(2)}) async-start(bf16[8,32,1024]{2,1,0:T(8,128)(2,1)} %constant_dynamic-update-slice_fusion.14), calls=%async_computation.2 | async-start | bytes 1048576 | tf_op jit(solution)/shard_map/all_to_all | solution.py:27
  105.6 3.7 %fusion.63 = bf16[64,1024]{1,0:T(8,128)(2,1)S(1)} fusion(f32[64,1024]{1,0:T(8,128)S(1)} %collective-permute-done.12, bf16[1,1024,2048]{2,1,0:T(8,128)(2,1)} %param.11, bf16[128,2048]{1,0:T(8,128)(2,1)S(1)} %get-tuple-element.13, f32[64]{0:T(128)S(1)} %mul.154), kind=kOutput, calls=%fused_computation.45 | convolution fusion | flops 268632064 | bytes 4850176 | tf_op jit(solution)/shard_map/dot_general | solution.py:143
  109.4 2.1 %collective-permute-start.13 = (bf16[32,1024]{1,0:T(8,128)(2,1)S(1)}, bf16[32,1024]{1,0:T(8,128)(2,1)S(1)}, u32[]{:S(2)}, u32[]{:S(2)}) collective-permute-start(bf16[32,1024]{1,0:T(8,128)(2,1)S(1)} %get-tuple-element.39), channel_id=1, source_target_pairs={{0,4},{1,5},{2,6},{3,7},{4,0},{5,1},{6,2},{7,3},{8,12},{9,13},{10,... | collective-permute-start | bytes 196616 | tf_op jit(solution)/shard_map/ppermute | solution.py:17
  111.4 1.5 %collective-permute-start.14 = (bf16[32,1024]{1,0:T(8,128)(2,1)S(1)}, bf16[32,1024]{1,0:T(8,128)(2,1)S(1)}, u32[]{:S(2)}, u32[]{:S(2)}) collective-permute-start(bf16[32,1024]{1,0:T(8,128)(2,1)S(1)} %get-tuple-element.40), channel_id=1, source_target_pairs={{0,6},{1,7},{2,4},{3,5},{4,2},{5,3},{6,0},{7,1},{8,14},{9,15},{10,... | collective-permute-start | bytes 196616 | tf_op jit(solution)/shard_map/ppermute | solution.py:17
  112.9 2.2 %fusion.84 = bf16[32,1024]{1,0:T(8,128)(2,1)S(1)} fusion(f32[32,1024]{1,0:T(8,128)} %collective-permute-done.11, bf16[1,1024,2048]{2,1,0:T(8,128)(2,1)S(1)} %copy-done.4, bf16[64,2048]{1,0:T(8,128)(2,1)S(1)} %get-tuple-element.21, f32[32]{0:T(128)S(1)} %slice_bitcast_fusion.4), kind=kOutput, calls=%fused_computation.52 | convolution fusion | flops 134316032 | bytes 4522496 | tf_op jit(solution)/shard_map/dot_general | solution.py:143
  115.2 1.6 %collective-permute-done.13 = bf16[32,1024]{1,0:T(8,128)(2,1)S(1)} collective-permute-done((bf16[32,1024]{1,0:T(8,128)(2,1)S(1)}, bf16[32,1024]{1,0:T(8,128)(2,1)S(1)}, u32[]{:S(2)}, u32[]{:S(2)}) %collective-permute-start.13) | collective-permute-done | bytes 65568 | tf_op jit(solution)/shard_map/ppermute | solution.py:17
  116.8 2.7 %collective-permute-done.14 = bf16[32,1024]{1,0:T(8,128)(2,1)S(1)} collective-permute-done((bf16[32,1024]{1,0:T(8,128)(2,1)S(1)}, bf16[32,1024]{1,0:T(8,128)(2,1)S(1)}, u32[]{:S(2)}, u32[]{:S(2)}) %collective-permute-start.14) | collective-permute-done | bytes 65568 | tf_op jit(solution)/shard_map/ppermute | solution.py:17
  119.5 1.1 all-to-all-done.2
  120.9 3.4 %collective-permute-start.15 = (bf16[128,512]{1,0:T(8,128)(2,1)S(1)}, bf16[128,512]{1,0:T(8,128)(2,1)S(1)}, u32[]{:S(2)}, u32[]{:S(2)}) collective-permute-start(bf16[128,512]{1,0:T(8,128)(2,1)S(1)} %slice.161), channel_id=1, source_target_pairs={{0,16},{1,17},{2,18},{3,19},{4,20},{5,21},{6,22},{7,23},{8,24},{9,... | collective-permute-start | bytes 393224 | tf_op jit(solution)/shard_map/ppermute | solution.py:181
  124.4 7.0 %convolution_bitcast_fusion = f32[1,1024,2048]{2,1,0:T(8,128)} fusion(bf16[512,1024]{1,0:T(8,128)(2,1)} %fusion.112, bf16[512,2048]{1,0:T(8,128)(2,1)S(1)} %copy-done.21), kind=kOutput, calls=%fused_computation | convolution fusion | flops 2147483648 | bytes 11534336 | tf_op jit(solution)/shard_map/dot_general | solution.py:169
  131.4 0.7 slice_select_fusion
  (129 shorter events, 10.6 us)
Async XLA Ops:
  0.6 1.1 copy-start
  2.8 21.8 %all-to-all-start = ((bf16[8,32,1024]{2,1,0:T(8,128)(2,1)}), bf16[8,32,1024]{2,1,0:T(8,128)(2,1)S(1)}, u32[]{:S(2)}, u32[]{:S(2)}) async-start(bf16[8,32,1024]{2,1,0:T(8,128)(2,1)} %bitcast.1), calls=%async_computation | async-start | bytes 1048576 | tf_op jit(solution)/shard_map/all_to_all | solution.py:27
  11.0 3.6 %collective-permute-start = (bf16[64,1024]{1,0:T(8,128)(2,1)S(1)}, bf16[64,1024]{1,0:T(8,128)(2,1)S(1)}, u32[]{:S(2)}, u32[]{:S(2)}) collective-permute-start(bf16[64,1024]{1,0:T(8,128)(2,1)S(1)} %pad_maximum_fusion.3), channel_id=1, source_target_pairs={{0,1},{1,0},{2,3},{3,2},{4,5},{5,4},{6,7},{7,6},{8,9},{9,8},{10,11... | collective-permute-start | bytes 393224 | tf_op jit(solution)/shard_map/ppermute | solution.py:12
  14.6 16.0 %collective-permute-start.2 = (bf16[64,1024]{1,0:T(8,128)(2,1)S(1)}, bf16[64,1024]{1,0:T(8,128)(2,1)S(1)}, u32[]{:S(2)}, u32[]{:S(2)}) collective-permute-start(bf16[64,1024]{1,0:T(8,128)(2,1)S(1)} %pad_maximum_fusion.5), channel_id=1, source_target_pairs={{0,2},{1,3},{2,0},{3,1},{4,6},{5,7},{6,4},{7,5},{8,10},{9,11},{10,... | collective-permute-start | bytes 393224 | tf_op jit(solution)/shard_map/ppermute | solution.py:17
  24.6 6.1 %copy-start.1 = (bf16[1,1024,2048]{2,1,0:T(8,128)(2,1)S(1)}, bf16[1,1024,2048]{2,1,0:T(8,128)(2,1)}, u32[]{:S(2)}) copy-start(bf16[1,1024,2048]{2,1,0:T(8,128)(2,1)} %param.11) | copy-start | bytes 12582916
  24.6 20.0 %copy-start.13 = (bf16[32,1024]{1,0:T(8,128)(2,1)}, bf16[32,1024]{1,0:T(8,128)(2,1)S(1)}, u32[]{:S(2)}) copy-start(bf16[32,1024]{1,0:T(8,128)(2,1)S(1)} %get-tuple-element.33) | copy-start | bytes 196612
  24.6 19.9 %copy-start.14 = (bf16[32,1024]{1,0:T(8,128)(2,1)}, bf16[32,1024]{1,0:T(8,128)(2,1)S(1)}, u32[]{:S(2)}) copy-start(bf16[32,1024]{1,0:T(8,128)(2,1)S(1)} %get-tuple-element.31) | copy-start | bytes 196612
  25.9 6.2 %copy-start.9 = (bf16[32,1024]{1,0:T(8,128)(2,1)}, bf16[32,1024]{1,0:T(8,128)(2,1)S(1)}, u32[]{:S(2)}) copy-start(bf16[32,1024]{1,0:T(8,128)(2,1)S(1)} %get-tuple-element.25) | copy-start | bytes 196612
  25.9 6.2 %copy-start.11 = (bf16[32,1024]{1,0:T(8,128)(2,1)}, bf16[32,1024]{1,0:T(8,128)(2,1)S(1)}, u32[]{:S(2)}) copy-start(bf16[32,1024]{1,0:T(8,128)(2,1)S(1)} %get-tuple-element.23) | copy-start | bytes 196612
  25.9 6.1 %collective-permute-start.1 = (bf16[192,1024]{1,0:T(8,128)(2,1)S(1)}, bf16[192,1024]{1,0:T(8,128)(2,1)S(1)}, u32[]{:S(2)}, u32[]{:S(2)}) collective-permute-start(bf16[192,1024]{1,0:T(8,128)(2,1)S(1)} %get-tuple-element.22), channel_id=1, source_target_pairs={{0,1},{1,0},{2,3},{3,2},{4,5},{5,4},{6,7},{7,6},{8,9},{9,8},{10,11... | collective-permute-start | bytes 1179656 | tf_op jit(solution)/shard_map/ppermute | solution.py:12
  29.1 14.8 %collective-permute-start.3 = (bf16[64,2048]{1,0:T(8,128)(2,1)S(1)}, bf16[64,2048]{1,0:T(8,128)(2,1)S(1)}, u32[]{:S(2)}, u32[]{:S(2)}) collective-permute-start(bf16[64,2048]{1,0:T(8,128)(2,1)S(1)} %fusion.100), channel_id=1, source_target_pairs={{0,16},{16,0},{1,17},{17,1},{2,18},{18,2},{3,19},{19,3},{4,20},{20... | collective-permute-start | bytes 786440 | tf_op jit(solution)/shard_map/ppermute | solution.py:21
  31.5 12.4 %collective-permute-start.4 = (bf16[64,2048]{1,0:T(8,128)(2,1)S(1)}, bf16[64,2048]{1,0:T(8,128)(2,1)S(1)}, u32[]{:S(2)}, u32[]{:S(2)}) collective-permute-start(bf16[64,2048]{1,0:T(8,128)(2,1)S(1)} %fusion.95), channel_id=1, source_target_pairs={{0,16},{16,0},{1,17},{17,1},{2,18},{18,2},{3,19},{19,3},{4,20},{20... | collective-permute-start | bytes 786440 | tf_op jit(solution)/shard_map/ppermute | solution.py:21
  32.1 13.2 %copy-start.7 = (bf16[64,1024]{1,0:T(8,128)(2,1)}, bf16[64,1024]{1,0:T(8,128)(2,1)S(1)}, u32[]{:S(2)}) copy-start(bf16[64,1024]{1,0:T(8,128)(2,1)S(1)} %get-tuple-element.38) | copy-start | bytes 393220
  32.1 18.6 %copy-start.5 = (bf16[64,1024]{1,0:T(8,128)(2,1)}, bf16[64,1024]{1,0:T(8,128)(2,1)S(1)}, u32[]{:S(2)}) copy-start(bf16[64,1024]{1,0:T(8,128)(2,1)S(1)} %get-tuple-element.37) | copy-start | bytes 393220
  32.9 64.0 %collective-permute-start.7 = (bf16[128,2048]{1,0:T(8,128)(2,1)S(1)}, bf16[128,2048]{1,0:T(8,128)(2,1)S(1)}, u32[]{:S(2)}, u32[]{:S(2)}) collective-permute-start(bf16[128,2048]{1,0:T(8,128)(2,1)S(1)} %fusion.37), channel_id=1, source_target_pairs={{0,16},{16,0},{1,17},{17,1},{2,18},{18,2},{3,19},{19,3},{4,20},{20... | collective-permute-start | bytes 1572872 | tf_op jit(solution)/shard_map/ppermute | solution.py:21
  43.8 0.7 copy-start.17
  43.8 6.8 %copy-start.15 = (bf16[64,2048]{1,0:T(8,128)(2,1)}, bf16[64,2048]{1,0:T(8,128)(2,1)S(1)}, u32[]{:S(2)}) copy-start(bf16[64,2048]{1,0:T(8,128)(2,1)S(1)} %collective-permute-done.3) | copy-start | bytes 786436
  45.3 37.6 %collective-permute-start.5 = (bf16[128,2048]{1,0:T(8,128)(2,1)S(1)}, bf16[128,2048]{1,0:T(8,128)(2,1)}, u32[]{:S(2)}, u32[]{:S(2)}) collective-permute-start(bf16[128,2048]{1,0:T(8,128)(2,1)S(1)} %fusion.42), channel_id=1, source_target_pairs={{0,16},{16,0},{1,17},{17,1},{2,18},{18,2},{3,19},{19,3},{4,20},{20... | collective-permute-start | bytes 1572872 | tf_op jit(solution)/shard_map/ppermute | solution.py:21
  46.9 14.7 %all-to-all-start.1 = ((s32[16,1,232]{2,1,0:T(1,128)}), s32[16,1,232]{2,1,0:T(1,128)S(1)}, u32[]{:S(2)}, u32[]{:S(2)}) async-start(s32[16,1,232]{2,1,0:T(1,128)} %broadcast_in_dim_reshape.3), calls=%async_computation.1 | async-start | bytes 32768 | tf_op jit(solution)/shard_map/all_to_all | solution.py:121
  50.7 6.4 %copy-start.2 = (bf16[1,1024,2048]{2,1,0:T(8,128)(2,1)S(1)}, bf16[1,1024,2048]{2,1,0:T(8,128)(2,1)}, u32[]{:S(2)}) copy-start(bf16[1,1024,2048]{2,1,0:T(8,128)(2,1)} %param.11) | copy-start | bytes 12582916
  50.7 3.8 %copy-start.16 = (bf16[64,2048]{1,0:T(8,128)(2,1)S(1)}, bf16[64,2048]{1,0:T(8,128)(2,1)}, u32[]{:S(2)}) copy-start(bf16[64,2048]{1,0:T(8,128)(2,1)} %copy-done.15) | copy-start | bytes 786436
  53.9 32.0 %collective-permute-start.6 = (bf16[128,2048]{1,0:T(8,128)(2,1)S(1)}, bf16[128,2048]{1,0:T(8,128)(2,1)}, u32[]{:S(2)}, u32[]{:S(2)}) collective-permute-start(bf16[128,2048]{1,0:T(8,128)(2,1)S(1)} %fusion.32), channel_id=1, source_target_pairs={{0,16},{16,0},{1,17},{17,1},{2,18},{18,2},{3,19},{19,3},{4,20},{20... | collective-permute-start | bytes 1572872 | tf_op jit(solution)/shard_map/ppermute | solution.py:21
  57.1 18.1 %copy-start.8 = (bf16[64,1024]{1,0:T(8,128)(2,1)S(1)}, bf16[64,1024]{1,0:T(8,128)(2,1)}, u32[]{:S(2)}) copy-start(bf16[64,1024]{1,0:T(8,128)(2,1)} %copy-done.7) | copy-start | bytes 393220
  57.1 19.8 %copy-start.6 = (bf16[64,1024]{1,0:T(8,128)(2,1)S(1)}, bf16[64,1024]{1,0:T(8,128)(2,1)}, u32[]{:S(2)}) copy-start(bf16[64,1024]{1,0:T(8,128)(2,1)} %copy-done.5) | copy-start | bytes 393220
  61.1 51.8 %collective-permute-start.11 = (f32[32,1024]{1,0:T(8,128)}, f32[32,1024]{1,0:T(8,128)}, u32[]{:S(2)}, u32[]{:S(2)}) collective-permute-start(f32[32,1024]{1,0:T(8,128)} %fusion.4), channel_id=1, source_target_pairs={{0,1},{1,0},{2,3},{3,2},{4,5},{5,4},{6,7},{7,6},{8,9},{9,8},{10,11... | collective-permute-start | bytes 393224 | tf_op jit(solution)/shard_map/ppermute | solution.py:12
  61.2 18.0 %collective-permute-start.8 = (f32[32,1024]{1,0:T(8,128)}, f32[32,1024]{1,0:T(8,128)}, u32[]{:S(2)}, u32[]{:S(2)}) collective-permute-start(f32[32,1024]{1,0:T(8,128)} %fusion.16), channel_id=1, source_target_pairs={{0,1},{1,0},{2,3},{3,2},{4,5},{5,4},{6,7},{7,6},{8,9},{9,8},{10,11... | collective-permute-start | bytes 393224 | tf_op jit(solution)/shard_map/ppermute | solution.py:12
  63.9 3.7 %copy-start.26 = (f32[1,2,32]{2,1,0:T(2,128)}, f32[1,2,32]{2,1,0:T(2,128)S(1)}, u32[]{:S(2)}) copy-start(f32[1,2,32]{2,1,0:T(2,128)S(1)} %get-tuple-element.50) | copy-start | bytes 772
  72.1 10.8 %copy-start.19 = (bf16[512,2048]{1,0:T(8,128)(2,1)S(1)}, bf16[512,2048]{1,0:T(8,128)(2,1)}, u32[]{:S(2)}) copy-start(bf16[512,2048]{1,0:T(8,128)(2,1)} %get-tuple-element.18) | copy-start | bytes 6291460
  73.7 10.6 %copy-start.3 = (bf16[1,1024,2048]{2,1,0:T(8,128)(2,1)S(1)}, bf16[1,1024,2048]{2,1,0:T(8,128)(2,1)}, u32[]{:S(2)}) copy-start(bf16[1,1024,2048]{2,1,0:T(8,128)(2,1)} %param.11) | copy-start | bytes 12582916
  85.6 3.4 %copy-start.29 = (f32[64]{0:T(128)S(1)}, f32[64]{0:T(128)}, u32[]{:S(2)}) copy-start(f32[64]{0:T(128)} %mul.144) | copy-start | bytes 772
  85.6 3.3 %collective-permute-start.9 = (f32[64,1024]{1,0:T(8,128)S(1)}, f32[64,1024]{1,0:T(8,128)S(1)}, u32[]{:S(2)}, u32[]{:S(2)}) collective-permute-start(f32[64,1024]{1,0:T(8,128)S(1)} %fusion.12), channel_id=1, source_target_pairs={{0,1},{1,0},{2,3},{3,2},{4,5},{5,4},{6,7},{7,6},{8,9},{9,8},{10,11... | collective-permute-start | bytes 786440 | tf_op jit(solution)/shard_map/ppermute | solution.py:12
  87.2 3.3 %copy-start.28 = (f32[64]{0:T(128)S(1)}, f32[64]{0:T(128)}, u32[]{:S(2)}) copy-start(f32[64]{0:T(128)} %mul.147) | copy-start | bytes 772
  88.6 1.9 %collective-permute-start.10 = (f32[64,1024]{1,0:T(8,128)S(1)}, f32[64,1024]{1,0:T(8,128)S(1)}, u32[]{:S(2)}, u32[]{:S(2)}) collective-permute-start(f32[64,1024]{1,0:T(8,128)S(1)} %fusion.8), channel_id=1, source_target_pairs={{0,1},{1,0},{2,3},{3,2},{4,5},{5,4},{6,7},{7,6},{8,9},{9,8},{10,11... | collective-permute-start | bytes 786440 | tf_op jit(solution)/shard_map/ppermute | solution.py:12
  91.8 7.0 %copy-start.10 = (bf16[32,1024]{1,0:T(8,128)(2,1)S(1)}, bf16[32,1024]{1,0:T(8,128)(2,1)}, u32[]{:S(2)}) copy-start(bf16[32,1024]{1,0:T(8,128)(2,1)} %copy-done.9) | copy-start | bytes 196612
  91.8 7.0 %copy-start.12 = (bf16[32,1024]{1,0:T(8,128)(2,1)S(1)}, bf16[32,1024]{1,0:T(8,128)(2,1)}, u32[]{:S(2)}) copy-start(bf16[32,1024]{1,0:T(8,128)(2,1)} %copy-done.11) | copy-start | bytes 196612
  91.8 7.0 %copy-start.25 = (f32[128]{0:T(128)S(1)}, f32[128]{0:T(128)}, u32[]{:S(2)}) copy-start(f32[128]{0:T(128)} %mul.138) | copy-start | bytes 1540
  96.9 8.6 %copy-start.27 = (f32[1,2,32]{2,1,0:T(2,128)S(1)}, f32[1,2,32]{2,1,0:T(2,128)}, u32[]{:S(2)}) copy-start(f32[1,2,32]{2,1,0:T(2,128)} %copy-done.26) | copy-start | bytes 772
  97.2 1.6 %copy-start.20 = (bf16[512,2048]{1,0:T(8,128)(2,1)}, bf16[512,2048]{1,0:T(8,128)(2,1)S(1)}, u32[]{:S(2)}) copy-start(bf16[512,2048]{1,0:T(8,128)(2,1)S(1)} %get-tuple-element.12) | copy-start | bytes 6291460
  98.6 7.0 %collective-permute-start.12 = (f32[64,1024]{1,0:T(8,128)S(1)}, f32[64,1024]{1,0:T(8,128)S(1)}, u32[]{:S(2)}, u32[]{:S(2)}) collective-permute-start(f32[64,1024]{1,0:T(8,128)S(1)} %fusion), channel_id=1, source_target_pairs={{0,1},{1,0},{2,3},{3,2},{4,5},{5,4},{6,7},{7,6},{8,9},{9,8},{10,11... | collective-permute-start | bytes 786440 | tf_op jit(solution)/shard_map/ppermute | solution.py:12
  99.6 20.9 %all-to-all-start.2 = ((bf16[8,32,1024]{2,1,0:T(8,128)(2,1)}), bf16[8,32,1024]{2,1,0:T(8,128)(2,1)S(1)}, u32[]{:S(2)}, u32[]{:S(2)}) async-start(bf16[8,32,1024]{2,1,0:T(8,128)(2,1)} %constant_dynamic-update-slice_fusion.14), calls=%async_computation.2 | async-start | bytes 1048576 | tf_op jit(solution)/shard_map/all_to_all | solution.py:27
  105.6 7.3 %copy-start.4 = (bf16[1,1024,2048]{2,1,0:T(8,128)(2,1)S(1)}, bf16[1,1024,2048]{2,1,0:T(8,128)(2,1)}, u32[]{:S(2)}) copy-start(bf16[1,1024,2048]{2,1,0:T(8,128)(2,1)} %param.11) | copy-start | bytes 12582916
  105.6 15.0 %copy-start.18 = (pred[256,128]{1,0:T(32,128)(4,1)S(1)}, pred[256,128]{1,0:T(32,128)(4,1)}, u32[]{:S(2)}) copy-start(pred[256,128]{1,0:T(32,128)(4,1)} %iota_compare_fusion.1) | copy-start | bytes 98308
  105.6 15.0 %copy-start.22 = (pred[32,128]{1,0:T(32,128)(4,1)S(1)}, pred[32,128]{1,0:T(32,128)(4,1)}, u32[]{:S(2)}) copy-start(pred[32,128]{1,0:T(32,128)(4,1)} %get-tuple-element.54) | copy-start | bytes 12292
  105.6 15.0 %copy-start.23 = (pred[32,128]{1,0:T(32,128)(4,1)S(1)}, pred[32,128]{1,0:T(32,128)(4,1)}, u32[]{:S(2)}) copy-start(pred[32,128]{1,0:T(32,128)(4,1)} %get-tuple-element.55) | copy-start | bytes 12292
  105.6 15.0 %copy-start.24 = (pred[32,128]{1,0:T(32,128)(4,1)S(1)}, pred[32,128]{1,0:T(32,128)(4,1)}, u32[]{:S(2)}) copy-start(pred[32,128]{1,0:T(32,128)(4,1)} %get-tuple-element.56) | copy-start | bytes 12292
  109.4 15.0 %copy-start.21 = (bf16[512,2048]{1,0:T(8,128)(2,1)S(1)}, bf16[512,2048]{1,0:T(8,128)(2,1)}, u32[]{:S(2)}) copy-start(bf16[512,2048]{1,0:T(8,128)(2,1)} %copy-done.20) | copy-start | bytes 6291460
  109.4 7.4 %collective-permute-start.13 = (bf16[32,1024]{1,0:T(8,128)(2,1)S(1)}, bf16[32,1024]{1,0:T(8,128)(2,1)S(1)}, u32[]{:S(2)}, u32[]{:S(2)}) collective-permute-start(bf16[32,1024]{1,0:T(8,128)(2,1)S(1)} %get-tuple-element.39), channel_id=1, source_target_pairs={{0,4},{1,5},{2,6},{3,7},{4,0},{5,1},{6,2},{7,3},{8,12},{9,13},{10,... | collective-permute-start | bytes 196616 | tf_op jit(solution)/shard_map/ppermute | solution.py:17
  111.4 8.0 %collective-permute-start.14 = (bf16[32,1024]{1,0:T(8,128)(2,1)S(1)}, bf16[32,1024]{1,0:T(8,128)(2,1)S(1)}, u32[]{:S(2)}, u32[]{:S(2)}) collective-permute-start(bf16[32,1024]{1,0:T(8,128)(2,1)S(1)} %get-tuple-element.40), channel_id=1, source_target_pairs={{0,6},{1,7},{2,4},{3,5},{4,2},{5,3},{6,0},{7,1},{8,14},{9,15},{10,... | collective-permute-start | bytes 196616 | tf_op jit(solution)/shard_map/ppermute | solution.py:17
  120.9 10.4 %collective-permute-start.15 = (bf16[128,512]{1,0:T(8,128)(2,1)S(1)}, bf16[128,512]{1,0:T(8,128)(2,1)S(1)}, u32[]{:S(2)}, u32[]{:S(2)}) collective-permute-start(bf16[128,512]{1,0:T(8,128)(2,1)S(1)} %slice.161), channel_id=1, source_target_pairs={{0,16},{1,17},{2,18},{3,19},{4,20},{5,21},{6,22},{7,23},{8,24},{9,... | collective-permute-start | bytes 393224 | tf_op jit(solution)/shard_map/ppermute | solution.py:181

commit v3 on v0

v3 whole, which is shorter than its diff:
```python
import functools

import jax
import jax.numpy as jnp
from jax import lax
from jax.experimental import pallas as pl
from jax.experimental.pallas import tpu as pltpu
from jax.sharding import PartitionSpec as P

F32 = jnp.float32
BF16 = jnp.bfloat16
I32 = jnp.int32
LANG_LANE = 256
VMEM = pl.BlockSpec(memory_space=pltpu.VMEM)


def sds(shape, dtype):
    return jax.ShapeDtypeStruct(shape, dtype)


def call(kernel, outs, *args, scratch=(), limit=8, spec=VMEM):
    return pl.pallas_call(
        kernel,
        out_shape=outs,
        in_specs=[spec] * len(args),
        out_specs=jax.tree.map(lambda _: VMEM, outs),
        scratch_shapes=list(scratch),
        compiler_params=pltpu.CompilerParams(vmem_limit_bytes=limit << 20),
        cost_estimate=pl.CostEstimate(flops=1000, bytes_accessed=1000, transcendentals=0),
    )(*args)


def sibling(value):
    count = lax.axis_size("dp")
    return lax.ppermute(value, "dp", [(i, i ^ 1) for i in range(count)])


def relation(value, rel):
    if rel == 0:
        return value
    count = lax.axis_size("dp")
    return lax.ppermute(value, "dp", [(i, i ^ (2 * rel)) for i in range(count)])


def across(values):
    return tuple(lax.ppermute(value, "section", [(0, 1), (1, 0)]) for value in values)


def same_core_exchange(value):
    count = lax.axis_size("dp")
    groups = [list(range(core, count, 2)) for core in range(2)]
    return lax.all_to_all(
        value, "dp", split_axis=0, concat_axis=0, axis_index_groups=groups, tiled=True
    )


def after(value, *others):
    return lax.optimization_barrier((value, *others))[0]


def pieces_of(count, cap):
    return [(i, core * cap) for core in range(2) for i in range(count)]


def iota(shape, dim):
    return lax.broadcasted_iota(I32, shape, dim)


def place_kernel(near_rels, *refs):
    inputs, (packed, near, info, notes), copies = refs[:4], refs[4:8], refs[8:]
    moves = [
        pltpu.make_async_copy(src, dst, copies[4].at[i])
        for i, (src, dst) in enumerate(zip(inputs, copies))
    ]
    for move in moves:
        move.start()
    for move in moves:
        move.wait()
    ids, table, counts, rows = copies[:4]
    chips, cap, _ = packed.shape
    chip = lax.axis_index("dp") // 2
    rows_dev = ids.shape[1]
    languages = table.shape[1]
    lang = ids[...]
    lang_hot = (iota((languages, rows_dev), 0) == lang).astype(F32)
    block = jnp.dot(table[...].astype(F32), lang_hot, preferred_element_type=F32).astype(I32)
    block_hot = iota((chips, rows_dev), 0) == block
    earlier = (iota((rows_dev, rows_dev), 0) < iota((rows_dev, rows_dev), 1)).astype(BF16)
    running = jnp.dot(
        block_hot.astype(F32).astype(BF16), earlier, preferred_element_type=F32
    )
    slot = jnp.sum(jnp.where(block_hot, running, 0.0), axis=0, keepdims=True).astype(I32)
    target = block * cap + slot
    hot = (iota((chips * cap, rows_dev), 0) == target).astype(F32).astype(BF16)
    values = rows[...]
    packed[...] = (
        jnp.dot(hot, values, preferred_element_type=F32).astype(BF16).reshape(packed.shape)
    )
    near_target = jnp.full_like(target, -1)
    for place, rel in enumerate(near_rels):
        near_target = jnp.where((block ^ chip) == rel, place * cap + slot, near_target)
    hot = (iota((len(near_rels) * cap, rows_dev), 0) == near_target).astype(F32).astype(BF16)
    near[...] = jnp.dot(hot, values, preferred_element_type=F32).astype(BF16)
    info[0:1, :] = block ^ chip
    info[1:2, :] = slot
    info[2:, :] = jnp.zeros((info.shape[0] - 2, rows_dev), I32)
    block_hot = (iota((2 * chips, rows_dev), 0) // 2 == block).astype(F32)
    slot_hot = (iota((cap, rows_dev), 0) == slot).astype(F32).astype(BF16)
    slot_lang = lax.dot_general(
        (block_hot * lang.astype(F32)).astype(BF16),
        slot_hot,
        (((1,), (1,)), ((), ())),
        preferred_element_type=F32,
    )
    notes[...] = jnp.zeros_like(notes)
    notes[:, :languages] = jnp.broadcast_to(counts[...], (2 * chips, languages))
    notes[:, LANG_LANE : LANG_LANE + cap] = slot_lang.astype(I32)


def packets_kernel(own, other, *outs):
    half = outs[0].shape[0] // 2
    for i, out in enumerate(outs):
        out[:half] = own[i * half : (i + 1) * half]
        out[half:] = other[i * half : (i + 1) * half]


def gather_kernel(rels, stack, out):
    chip = lax.axis_index("dp") // 2
    cap = stack.shape[1]
    for i, rel in enumerate(rels):
        out[i * cap : (i + 1) * cap, :] = stack[chip ^ rel]


def tail_kernel(layout, cap, notes, temp, *refs):
    inputs, scale_out, turned, langs, lhs = refs[:-4], refs[-4], refs[-3], refs[-2], refs[-1]
    device = lax.axis_index("dp")
    languages = temp.shape[1]
    totals = jnp.sum(notes[...].astype(F32), axis=0)[:, :languages]
    lang_scale = 2.0 * notes.shape[0] * temp[...].astype(F32) / totals
    for i, (rel, core, _, _) in enumerate(layout):
        source = device ^ (2 * rel + core)
        langs[i : i + 1, :] = notes[source, :, LANG_LANE : LANG_LANE + 128]
    lang_columns = langs[...].T
    for i, (_, _, which, first) in enumerate(layout):
        column = lang_columns[:cap, i : i + 1]
        scale = jnp.sum(
            jnp.where(column == iota((cap, languages), 1), lang_scale, 0.0),
            axis=1,
            keepdims=True,
        )
        scale_out[i * cap : (i + 1) * cap, :] = scale
        rows = inputs[which][first : first + cap, :].astype(F32) * scale
        lhs[i * cap : (i + 1) * cap, :] = rows.astype(BF16)
    turned[...] = lhs[...].T


def product_kernel(count, pieces, *refs):
    inputs, weight, hands, rows = refs[:count], refs[count], refs[count + 1 : -1], refs[-1]
    cap = rows.shape[0] // len(pieces)
    is_up = lax.axis_index("section") == 0
    for i, (which, first) in enumerate(pieces):
        rows[i * cap : (i + 1) * cap, :] = inputs[which][first : first + cap, :]
    tile = 512
    for j in range(0, weight.shape[1], tile):
        value = jnp.dot(rows[...], weight[:, j : j + tile], preferred_element_type=F32)
        value = jnp.where(is_up, jnp.maximum(value, 0.0), value).astype(BF16)
        first = 0
        for hand in hands:
            hand[:, j : j + tile] = value[first : first + hand.shape[0]]
            first += hand.shape[0]


def join_kernel(cap, first, mine, theirs, scale, *outs):
    for j, out in enumerate(outs):
        rows = slice(j * cap, (j + 1) * cap)
        factor = scale[first + j * cap : first + (j + 1) * cap, :]
        out[...] = ((mine[rows, :] + theirs[rows, :]) * factor).astype(BF16)


def back_kernel(*refs):
    count = (len(refs) - 4) // 2
    recvs, hands, (weight, partner, mine, theirs) = refs[:count], refs[count:-4], refs[-4:]
    is_up = lax.axis_index("section") == 0
    half = mine.shape[0]
    masked = is_up & (jnp.concatenate([h[...] for h in hands], axis=0) <= 0)
    recv = jnp.concatenate([r[...] for r in recvs], axis=0)
    value = jnp.where(masked, jnp.zeros_like(recv), recv)
    partner[...] = value
    product = lax.dot_general(
        value, weight[...], (((1,), (1,)), ((), ())), preferred_element_type=F32
    )
    mine[...] = product[:half]
    theirs[...] = product[half:]


def weight_kernel(turned, *refs):
    partners, out = refs[:-1], refs[-1]
    rhs = jnp.concatenate([p[...] for p in partners], axis=0)
    out[...] = jnp.dot(turned[...], rhs, preferred_element_type=F32)


def final_kernel(direct, cap, info, *refs):
    pieces, left, right = refs[:-2], refs[-2], refs[-1]
    rel, slot = info[0:1, :], info[1:2, :]
    rows_dev = rel.shape[1]
    target = jnp.zeros_like(rel)
    for i, r in enumerate(direct):
        target = jnp.where(rel == r, i * cap + slot, target)
    values = jnp.concatenate([p[...] for p in pieces], axis=0)
    hot = (iota((values.shape[0], rows_dev), 0) == target).astype(F32).astype(BF16)
    rows = lax.dot_general(
        hot, values, (((0,), (0,)), ((), ())), preferred_element_type=F32
    ).astype(BF16)
    half = left.shape[1]
    left[...] = rows[:, :half]
    right[...] = rows[:, half:]


def on_device(section_rows, lang_ids, lang_table, lang_counts, temp_num, weights):
    is_up = lax.axis_index("section") == 0
    replicas = lax.axis_size("dp")
    chips = replicas // 2
    unit = chips // 8
    rows_dev = lang_ids.shape[0]
    cap = 2 * rows_dev // chips
    width = section_rows.shape[2]
    own_weight = weights[0]
    ff_dev = own_weight.shape[1]

    def rels(first, last):
        return list(range(first * unit, last * unit))

    groups = [rels(0, 1), rels(2, 4), rels(4, 6), rels(6, 8), rels(1, 2)]
    near_rels = groups[0] + groups[1]
    far_rels = groups[2] + groups[3] + groups[4]
    table = lang_table.reshape(1, -1)

    packed, near, info, notes = call(
        functools.partial(place_kernel, near_rels),
        (
            sds((chips, cap, width), BF16),
            sds((len(near_rels) * cap, width), BF16),
            sds((8, rows_dev), I32),
            sds((2 * chips, LANG_LANE + 128), I32),
        ),
        lang_ids.reshape(1, -1),
        table,
        lang_counts,
        section_rows[0],
        scratch=[
            pltpu.VMEM((1, rows_dev), I32),
            pltpu.VMEM(table.shape, I32),
            pltpu.VMEM(lang_counts.shape, I32),
            pltpu.VMEM((rows_dev, width), BF16),
            pltpu.SemaphoreType.DMA((4,)),
        ],
        spec=pl.BlockSpec(memory_space=pl.ANY),
    )
    came = same_core_exchange(packed)
    near_other = sibling(near)
    packets = call(
        packets_kernel,
        tuple(sds((2 * cap, width), BF16) for _ in near_rels),
        near,
        near_other,
    )
    moved = {r: relation(p, r) for r, p in zip(near_rels, packets)}

    hands, received, partners, terms = [], [], [], []

    def product(inputs, pieces, parts=1):
        count = len(pieces) * cap
        hand = call(
            functools.partial(product_kernel, len(inputs), pieces),
            (sds((count // parts, ff_dev), BF16),) * parts,
            *inputs,
            own_weight,
            scratch=[pltpu.VMEM((count, width), BF16)],
        )
        hands.append(hand)
        received.append(across(hand))

    def back_product(g, *earlier):
        count = len(groups[g]) * cap
        partner, mine, theirs = call(
            back_kernel,
            (sds((2 * count, ff_dev), BF16), sds((count, width), F32), sds((count, width), F32)),
            *lax.optimization_barrier((*received[g], *earlier))[: len(received[g])],
            *hands[g],
            own_weight,
        )
        partners.append(partner)
        terms.append((mine, sibling(theirs)))

    product([moved[r] for r in groups[0]], pieces_of(len(groups[0]), cap))
    inputs = [moved[r] for r in groups[1]]
    inputs[0] = after(inputs[0], *hands[0])
    product(inputs, pieces_of(len(groups[1]), cap), parts=2)
    came = after(came, *received[0], received[1][0])
    far_own = call(
        functools.partial(gather_kernel, far_rels),
        sds((len(far_rels) * cap, width), BF16),
        came,
    )
    far_other = sibling(far_own)
    far_pieces, start = [], 0
    for g in range(2, 5):
        size = len(groups[g])
        far_pieces.append([(c, (start + i) * cap) for c in range(2) for i in range(size)])
        start += size
    product([far_own, far_other], far_pieces[0])
    product([after(far_own, *received[1], *hands[2]), far_other], far_pieces[1])

    notes = after(notes, *hands[3])
    notes = lax.all_to_all(
        notes.reshape(2 * chips, 1, -1), "dp", split_axis=0, concat_axis=0, tiled=True
    )
    back_product(0, *hands[3])
    back_product(1, partners[0])

    inputs = [moved[r] for r in near_rels] + [far_own, far_other]
    layout, group_first = [], []
    for g, group in enumerate(groups):
        group_first.append(len(layout) * cap)
        for core in range(2):
            for r in group:
                if g < 2:
                    layout.append((r, core, near_rels.index(r), core * cap))
                else:
                    layout.append((r, core, len(near_rels) + core, far_rels.index(r) * cap))
    total_rows = len(layout) * cap
    scale, turned = call(
        functools.partial(tail_kernel, layout, cap),
        (sds((total_rows, 1), F32), sds((width, total_rows), BF16)),
        notes,
        temp_num.reshape(1, -1),
        *inputs,
        scratch=[
            pltpu.VMEM((max(len(layout), 8), 128), I32),
            pltpu.VMEM((total_rows, width), BF16),
        ],
    )
    returned = {}

    def give_back(g):
        joined = call(
            functools.partial(join_kernel, cap, group_first[g]),
            tuple(sds((cap, width), BF16) for _ in groups[g]),
            *terms[g],
            scale,
        )
        for rows, r in zip(joined, groups[g]):
            returned[r] = relation(rows, r)

    def given(g):
        return [returned[r] for r in groups[g]]

    give_back(0)
    give_back(1)
    product([after(far_own, *received[2], scale), far_other], far_pieces[2])
    back_product(2, *hands[4])
    give_back(2)
    back_product(3, partners[2], *given(1))
    give_back(3)
    back_product(4, partners[3], *given(2))
    give_back(4)
    direct = [r for group in groups for r in group]
    left, right = call(
        functools.partial(final_kernel, direct, cap),
        (sds((rows_dev, width // 2), BF16),) * 2,
        info,
        *[returned[r] for r in direct],
    )
    right_cols = lax.ppermute(right, "section", [(0, 1)])
    input_grad = jnp.where(is_up, left, right_cols)
    tile = 256
    weight_grad = pl.pallas_call(
        weight_kernel,
        out_shape=sds((width, ff_dev), F32),
        grid=(ff_dev // tile,),
        in_specs=[pl.BlockSpec((width, total_rows), lambda j: (0, 0))]
        + [pl.BlockSpec((p.shape[0], tile), lambda j: (0, j)) for p in partners],
        out_specs=pl.BlockSpec((width, tile), lambda j: (0, j)),
        compiler_params=pltpu.CompilerParams(vmem_limit_bytes=12 << 20),
        cost_estimate=pl.CostEstimate(
            flops=2 * width * total_rows * ff_dev,
            bytes_accessed=4 * width * ff_dev,
            transcendentals=0,
        ),
    )(turned, *partners)
    return (weight_grad[None], input_grad)


def solution(mesh):
    return jax.shard_map(
        on_device,
        mesh=mesh,
        in_specs=(
            P("section", "dp", None),
            P("dp"),
            P(),
            P("dp", None),
            P(),
            P("section", None, "dp"),
        ),
        out_specs=(P("section", None, "dp"), P("dp", "section")),
        check_vma=False,
    )
```

time: 196 us -> 116 us (0.59)
  blocking collectives: 88.6 us -> 10.4 us
  waiting for transfers between devices: 69.7 us -> 30.1 us
  starting transfers between devices: 6.44 us -> 34.6 us
  Pallas kernels: 0 us -> 24.9 us
  matrix products: 20.1 us -> 0 us
  local copies, waits for them, and re-layouts: 1.12 us -> 14.2 us
  other arithmetic: 8.72 us -> 0.67 us
    all_to_all x1, blocking collectives: 53.7 us -> 10.4 us  [on_device(): lax.all_to_all(notes.reshape(2 * chips, 1, -1), 'dp', split_axis=0, conca...]
    psum x1 -> x0, blocking collectives: 34.9 us -> none  [on_device(): totals = lax.psum(lang_counts[0].astype(jnp.float32), 'dp')]
    pallas_call x0 -> x21, Pallas kernels: none -> 24.9 us  [the longest x20 18.6 us: call(): pl.pallas_call(kernel, out_shape=outs, in_specs=[spec] * len(args), out_s...]
    ppermute x2 -> x23, starting transfers between devices: 2.79 us -> 27.3 us  [the longest x9 14.7 us: relation(): return lax.ppermute(value, 'dp', [(i, i ^ 2 * rel) for i in range(count)])]
    all_to_all x1, waiting for transfers between devices: 22.9 us -> 0.01 us  [same_core_exchange(): lax.all_to_all(value, 'dp', split_axis=0, concat_axis=0, axis_index_group...]
    dot_general x5 -> x0, matrix products: 20.1 us -> none  [the longest x1 7.29 us: on_device(): jnp.einsum('skd,df->skf', arrived, own_weight, preferred_element_type=jnp...]
    ppermute x2 -> x23, waiting for transfers between devices: 46.8 us -> 30.1 us  [the longest x9 19.7 us: relation(): return lax.ppermute(value, 'dp', [(i, i ^ 2 * rel) for i in range(count)])]
    unnamed x2 -> x34, local copies, waits for them, and re-layouts: 0.01 us -> 14.1 us
  transfers between devices with their start and end apart: 3 -> 24, of which waited for: 2 -> 12; matrix products, arithmetic and copies ran while one was open for 3% -> 0% of each run, Pallas kernels for 0% -> 19%
where the time goes in v3:
time: 116 us
  starting transfers between devices  34.6 us (30%)
  waiting for transfers between devices  30.1 us (26%)
  Pallas kernels  24.9 us (21%)
  local copies, waits for them, and re-layouts  14.2 us (12%)
  blocking collectives  10.4 us (9%)
    ppermute x9, waiting for transfers between devices, relation(): return lax.ppermute(value, 'dp', [(i, i ^ 2 * rel) for i in range(count)])  19.7 us
    pallas_call x20, Pallas kernels, call(): pl.pallas_call(kernel, out_shape=outs, in_specs=[spec] * len(args), out_s...  18.6 us
    ppermute x9, starting transfers between devices, relation(): return lax.ppermute(value, 'dp', [(i, i ^ 2 * rel) for i in range(count)])  14.7 us
    unnamed x34, local copies, waits for them, and re-layouts  14.1 us
    all_to_all x1, blocking collectives, on_device(): lax.all_to_all(notes.reshape(2 * chips, 1, -1), 'dp', split_axis=0, conca...  10.4 us
    ppermute x6, waiting for transfers between devices, across(): lax.ppermute(value, 'section', [(0, 1), (1, 0)])  8.86 us
    ppermute x6, starting transfers between devices, across(): lax.ppermute(value, 'section', [(0, 1), (1, 0)])  8.35 us
    all_to_all x1, starting transfers between devices, same_core_exchange(): lax.all_to_all(value, 'dp', split_axis=0, concat_axis=0, axis_index_group...  7.3 us
  transfers between devices with their start and end apart: 24, of which 12 were waited for; matrix products, arithmetic and copies ran while one was open for 0% of the time, Pallas kernels for 19%

profile of v3, /device:TPU:0, one launch (start us, length us, event | category | flops | bytes accessed | tf_op | source)
XLA Modules:
  0.0 115.6 jit_solution(16034471571016653163)
XLA Ops:
  0.6 0.9 copy-done.4
  1.6 0.7 copy-done.13
  2.3 0.7 copy-done.14
  2.9 0.7 copy-done.16
  3.6 1.4 %shard_map.77 = (bf16[8,32,1024]{2,1,0:T(8,128)(2,1)}, bf16[96,1024]{1,0:T(8,128)(2,1)S(1)}, s32[8,128]{1,0:T(8,128)S(1)}, s32[16,384]{1,0:T(8,128)S(1)}) custom-call(s32[1,128]{1,0:T(1,128)S(1)} %bitcast.19, s32[1,200]{1,0:T(1,128)S(1)} %bitcast.17, s32[1,200]{1,0:T(1,128)S(1)} %copy-done.14, bf16[128,1024]{1,0:T(8,128)(2,1)S(1)} %bitcast.16), custom_call_target="tpu_custom_call" | custom-call | flops 1000 | bytes 1000 | tf_op jit(solution)/shard_map/pallas_call | solution.py:22
  5.0 7.3 %all-to-all-start = ((bf16[8,32,1024]{2,1,0:T(8,128)(2,1)}), bf16[8,32,1024]{2,1,0:T(8,128)(2,1)S(1)}, u32[]{:S(2)}, u32[]{:S(2)}) async-start(bf16[8,32,1024]{2,1,0:T(8,128)(2,1)} %get-tuple-element.48), calls=%async_computation | async-start | bytes 1048576 | tf_op jit(solution)/shard_map/all_to_all | solution.py:52
  12.3 1.4 %collective-permute-done.other = bf16[96,1024]{1,0:T(8,128)(2,1)S(1)} collective-permute-done((bf16[96,1024]{1,0:T(8,128)(2,1)S(1)}, bf16[96,1024]{1,0:T(8,128)(2,1)S(1)}, u32[]{:S(2)}, u32[]{:S(2)}) %collective-permute-start) | collective-permute-done | bytes 196640 | tf_op jit(solution)/shard_map/ppermute | solution.py:35
  13.8 2.1 %collective-permute-start.2 = (bf16[64,1024]{1,0:T(8,128)(2,1)S(1)}, bf16[64,1024]{1,0:T(8,128)(2,1)S(1)}, u32[]{:S(2)}, u32[]{:S(2)}) collective-permute-start(bf16[64,1024]{1,0:T(8,128)(2,1)S(1)} %get-tuple-element.51), channel_id=1, source_target_pairs={{0,4},{1,5},{2,6},{3,7},{4,0},{5,1},{6,2},{7,3},{8,12},{9,13},{10,... | collective-permute-start | bytes 393224 | tf_op jit(solution)/shard_map/ppermute | solution.py:42
  15.8 1.5 %collective-permute-start.3 = (bf16[64,1024]{1,0:T(8,128)(2,1)S(1)}, bf16[64,1024]{1,0:T(8,128)(2,1)S(1)}, u32[]{:S(2)}, u32[]{:S(2)}) collective-permute-start(bf16[64,1024]{1,0:T(8,128)(2,1)S(1)} %get-tuple-element.53), channel_id=1, source_target_pairs={{0,6},{1,7},{2,4},{3,5},{4,2},{5,3},{6,0},{7,1},{8,14},{9,15},{10,... | collective-permute-start | bytes 393224 | tf_op jit(solution)/shard_map/ppermute | solution.py:42
  17.3 2.2 %copy-done = bf16[1,1024,2048]{2,1,0:T(8,128)(2,1)S(1)} copy-done((bf16[1,1024,2048]{2,1,0:T(8,128)(2,1)S(1)}, bf16[1,1024,2048]{2,1,0:T(8,128)(2,1)}, u32[]{:S(2)}) %copy-start) | copy-done | bytes 4194328
  19.5 0.8 shard_map.79.refs_1_
  20.3 1.6 %collective-permute-start.1 = (bf16[64,2048]{1,0:T(8,128)(2,1)S(1)}, bf16[64,2048]{1,0:T(8,128)(2,1)S(1)}, u32[]{:S(2)}, u32[]{:S(2)}) collective-permute-start(bf16[64,2048]{1,0:T(8,128)(2,1)S(1)} %shard_map.79.refs_1_), channel_id=1, source_target_pairs={{0,16},{16,0},{1,17},{17,1},{2,18},{18,2},{3,19},{19,3},{4,20},{20... | collective-permute-start | bytes 786440 | tf_op jit(solution)/shard_map/ppermute | solution.py:46
  21.9 4.0 %collective-permute-done.2.refs_0_.refs_1_ = bf16[64,1024]{1,0:T(8,128)(2,1)S(1)} collective-permute-done((bf16[64,1024]{1,0:T(8,128)(2,1)S(1)}, bf16[64,1024]{1,0:T(8,128)(2,1)S(1)}, u32[]{:S(2)}, u32[]{:S(2)}) %collective-permute-start.2) | collective-permute-done | bytes 131104 | tf_op jit(solution)/shard_map/ppermute | solution.py:42
  25.9 3.7 %collective-permute-done.3.refs_1_.refs_2_ = bf16[64,1024]{1,0:T(8,128)(2,1)S(1)} collective-permute-done((bf16[64,1024]{1,0:T(8,128)(2,1)S(1)}, bf16[64,1024]{1,0:T(8,128)(2,1)S(1)}, u32[]{:S(2)}, u32[]{:S(2)}) %collective-permute-start.3) | collective-permute-done | bytes 131104 | tf_op jit(solution)/shard_map/ppermute | solution.py:42
  29.6 2.2 %copy-done.1 = bf16[1,1024,2048]{2,1,0:T(8,128)(2,1)S(1)} copy-done((bf16[1,1024,2048]{2,1,0:T(8,128)(2,1)S(1)}, bf16[1,1024,2048]{2,1,0:T(8,128)(2,1)}, u32[]{:S(2)}) %copy-start.1) | copy-done | bytes 4194328
  31.8 0.7 shard_map.80
  32.6 1.5 %collective-permute-start.4 = (bf16[64,2048]{1,0:T(8,128)(2,1)S(1)}, bf16[64,2048]{1,0:T(8,128)(2,1)S(1)}, u32[]{:S(2)}, u32[]{:S(2)}) collective-permute-start(bf16[64,2048]{1,0:T(8,128)(2,1)S(1)} %get-tuple-element.54.refs_2_), channel_id=1, source_target_pairs={{0,16},{16,0},{1,17},{17,1},{2,18},{18,2},{3,19},{19,3},{4,20},{20... | collective-permute-start | bytes 786440 | tf_op jit(solution)/shard_map/ppermute | solution.py:46
  34.1 5.8 %collective-permute-done.4.refs_0_ = bf16[64,2048]{1,0:T(8,128)(2,1)S(1)} collective-permute-done((bf16[64,2048]{1,0:T(8,128)(2,1)S(1)}, bf16[64,2048]{1,0:T(8,128)(2,1)S(1)}, u32[]{:S(2)}, u32[]{:S(2)}) %collective-permute-start.4) | collective-permute-done | bytes 262176 | tf_op jit(solution)/shard_map/ppermute | solution.py:46
  39.9 0.1 collective-permute-start.6
  40.0 1.6 %collective-permute-start.5 = (bf16[64,2048]{1,0:T(8,128)(2,1)S(1)}, bf16[64,2048]{1,0:T(8,128)(2,1)S(1)}, u32[]{:S(2)}, u32[]{:S(2)}) collective-permute-start(bf16[64,2048]{1,0:T(8,128)(2,1)S(1)} %get-tuple-element.56.refs_3_), channel_id=1, source_target_pairs={{0,16},{16,0},{1,17},{17,1},{2,18},{18,2},{3,19},{19,3},{4,20},{20... | collective-permute-start | bytes 786440 | tf_op jit(solution)/shard_map/ppermute | solution.py:46
  41.6 2.2 %copy-done.2 = bf16[1,1024,2048]{2,1,0:T(8,128)(2,1)S(1)} copy-done((bf16[1,1024,2048]{2,1,0:T(8,128)(2,1)S(1)}, bf16[1,1024,2048]{2,1,0:T(8,128)(2,1)}, u32[]{:S(2)}) %copy-start.2) | copy-done | bytes 4194328
  43.8 0.7 shard_map.82.refs_1_
  44.6 1.5 %collective-permute-start.7 = (bf16[128,2048]{1,0:T(8,128)(2,1)S(1)}, bf16[128,2048]{1,0:T(8,128)(2,1)S(1)}, u32[]{:S(2)}, u32[]{:S(2)}) collective-permute-start(bf16[128,2048]{1,0:T(8,128)(2,1)S(1)} %shard_map.82.refs_1_), channel_id=1, source_target_pairs={{0,16},{16,0},{1,17},{17,1},{2,18},{18,2},{3,19},{19,3},{4,20},{20... | collective-permute-start | bytes 1572872 | tf_op jit(solution)/shard_map/ppermute | solution.py:46
  46.1 3.1 %collective-permute-done.5.refs_1_ = bf16[64,2048]{1,0:T(8,128)(2,1)S(1)} collective-permute-done((bf16[64,2048]{1,0:T(8,128)(2,1)S(1)}, bf16[64,2048]{1,0:T(8,128)(2,1)S(1)}, u32[]{:S(2)}, u32[]{:S(2)}) %collective-permute-start.5) | collective-permute-done | bytes 262176 | tf_op jit(solution)/shard_map/ppermute | solution.py:46
  49.2 0.7 shard_map.83.refs_1_
  49.9 1.6 %collective-permute-start.8 = (bf16[128,2048]{1,0:T(8,128)(2,1)S(1)}, bf16[128,2048]{1,0:T(8,128)(2,1)S(1)}, u32[]{:S(2)}, u32[]{:S(2)}) collective-permute-start(bf16[128,2048]{1,0:T(8,128)(2,1)S(1)} %shard_map.83.refs_1_), channel_id=1, source_target_pairs={{0,16},{16,0},{1,17},{17,1},{2,18},{18,2},{3,19},{19,3},{4,20},{20... | collective-permute-start | bytes 1572872 | tf_op jit(solution)/shard_map/ppermute | solution.py:46
  51.5 2.0 %shard_map.85 = (bf16[64,2048]{1,0:T(8,128)(2,1)S(1)}, f32[32,1024]{1,0:T(8,128)S(1)}, f32[32,1024]{1,0:T(8,128)}) custom-call(bf16[64,2048]{1,0:T(8,128)(2,1)S(1)} %collective-permute-done.1.refs_0_, bf16[64,2048]{1,0:T(8,128)(2,1)S(1)} %shard_map.79.refs_1_, bf16[1024,2048]{1,0:T(8,128)(2,1)S(1)} %bitcast.10), custom_call_target="tpu_custom_call" | custom-call | flops 1000 | bytes 1000 | tf_op jit(solution)/shard_map/pallas_call | solution.py:22
  53.5 1.5 %shard_map.86 = (bf16[128,2048]{1,0:T(8,128)(2,1)S(1)}, f32[64,1024]{1,0:T(8,128)S(1)}, f32[64,1024]{1,0:T(8,128)S(1)}) custom-call(bf16[64,2048]{1,0:T(8,128)(2,1)S(1)} %collective-permute-done.4.refs_0_, bf16[64,2048]{1,0:T(8,128)(2,1)S(1)} %collective-permute-done.5.refs_1_, bf16[64,2048]{1,0:T(8,128)(2,1)S(1)} %get-tuple-element.54.refs_2_, ...), custom_call_target="tpu_custom_call" | custom-call | flops 1000 | bytes 1000 | tf_op jit(solution)/shard_map/pallas_call | solution.py:22
  55.1 10.4 %all_to_all.10.notes = s32[16,1,384]{2,1,0:T(1,128)S(1)} all-to-all(s32[16,1,384]{2,1,0:T(1,128)S(1)} %reshape.18), channel_id=1, replica_groups=mesh['section'=2,'dp'=16] {'dp'}, dimensions={0} | all-to-all | bytes 49152 | tf_op jit(solution)/shard_map/all_to_all | solution.py:315
  65.5 1.6 %shard_map.84 = (f32[512,1]{1,0:T(8,128)S(1)}, bf16[1024,512]{1,0:T(8,128)(2,1)S(1)}) custom-call(s32[16,1,384]{2,1,0:T(1,128)S(1)} %all_to_all.10.notes, s32[1,200]{1,0:T(1,128)S(1)} %bitcast.18, bf16[64,1024]{1,0:T(8,128)(2,1)S(1)} %get-tuple-element.50.refs_0_, bf16[64,1024]{1,0:T(8,128)(2,1)S(1)} %collective-permute-done.2.refs_0_.refs_1_, ...), custom_call_target="tpu_custom_call" | custom-call | flops 1000 | bytes 1000 | tf_op jit(solution)/shard_map/pallas_call | solution.py:22
  67.1 0.8 shard_map.87.refs_1_
  67.9 1.5 %shard_map.88 = (bf16[128,2048]{1,0:T(8,128)(2,1)S(1)}, f32[64,1024]{1,0:T(8,128)S(1)}, f32[64,1024]{1,0:T(8,128)S(1)}) custom-call(bf16[128,2048]{1,0:T(8,128)(2,1)S(1)} %collective-permute-done.7.refs_0_, bf16[128,2048]{1,0:T(8,128)(2,1)S(1)} %shard_map.82.refs_1_, bf16[1024,2048]{1,0:T(8,128)(2,1)S(1)} %bitcast.13), custom_call_target="tpu_custom_call" | custom-call | flops 1000 | bytes 1000 | tf_op jit(solution)/shard_map/pallas_call | solution.py:22
  69.5 0.6 collective-permute-start.12
  70.1 0.1 shard_map.89
  70.2 0.5 collective-permute-start.10
  70.7 1.5 %collective-permute-start.11 = (bf16[32,1024]{1,0:T(8,128)(2,1)S(1)}, bf16[32,1024]{1,0:T(8,128)(2,1)S(1)}, u32[]{:S(2)}, u32[]{:S(2)}) collective-permute-start(bf16[32,1024]{1,0:T(8,128)(2,1)S(1)} %get-tuple-element.72), channel_id=1, source_target_pairs={{0,6},{1,7},{2,4},{3,5},{4,2},{5,3},{6,0},{7,1},{8,14},{9,15},{10,... | collective-permute-start | bytes 196616 | tf_op jit(solution)/shard_map/ppermute | solution.py:42
  72.2 2.9 %collective-permute-done.10.refs_1_ = bf16[32,1024]{1,0:T(8,128)(2,1)S(1)} collective-permute-done((bf16[32,1024]{1,0:T(8,128)(2,1)S(1)}, bf16[32,1024]{1,0:T(8,128)(2,1)S(1)}, u32[]{:S(2)}, u32[]{:S(2)}) %collective-permute-start.10) | collective-permute-done | bytes 65568 | tf_op jit(solution)/shard_map/ppermute | solution.py:42
  75.1 0.7 collective-permute-done.11.refs_2_
  75.9 1.5 %shard_map.90 = (bf16[128,2048]{1,0:T(8,128)(2,1)S(1)}, f32[64,1024]{1,0:T(8,128)S(1)}, f32[64,1024]{1,0:T(8,128)S(1)}) custom-call(bf16[128,2048]{1,0:T(8,128)(2,1)S(1)} %collective-permute-done.8.refs_0_, bf16[128,2048]{1,0:T(8,128)(2,1)S(1)} %shard_map.83.refs_1_, bf16[1024,2048]{1,0:T(8,128)(2,1)S(1)} %bitcast.14), custom_call_target="tpu_custom_call" | custom-call | flops 1000 | bytes 1000 | tf_op jit(solution)/shard_map/pallas_call | solution.py:22
  77.5 0.1 shard_map.91
  77.6 0.7 collective-permute-start.14
  78.3 3.1 %collective-permute-start.15 = (bf16[32,1024]{1,0:T(8,128)(2,1)S(1)}, bf16[32,1024]{1,0:T(8,128)(2,1)S(1)}, u32[]{:S(2)}, u32[]{:S(2)}) collective-permute-start(bf16[32,1024]{1,0:T(8,128)(2,1)S(1)} %get-tuple-element.78), channel_id=1, source_target_pairs={{0,10},{1,11},{2,8},{3,9},{4,14},{5,15},{6,12},{7,13},{8,2},{9,3},... | collective-permute-start | bytes 196616 | tf_op jit(solution)/shard_map/ppermute | solution.py:42
  81.4 4.8 %collective-permute-done.14.refs_3_ = bf16[32,1024]{1,0:T(8,128)(2,1)S(1)} collective-permute-done((bf16[32,1024]{1,0:T(8,128)(2,1)S(1)}, bf16[32,1024]{1,0:T(8,128)(2,1)S(1)}, u32[]{:S(2)}, u32[]{:S(2)}) %collective-permute-start.14) | collective-permute-done | bytes 65568 | tf_op jit(solution)/shard_map/ppermute | solution.py:42
  86.2 0.6 copy-done.9
  86.8 1.3 %collective-permute-done.15.refs_4_ = bf16[32,1024]{1,0:T(8,128)(2,1)S(1)} collective-permute-done((bf16[32,1024]{1,0:T(8,128)(2,1)S(1)}, bf16[32,1024]{1,0:T(8,128)(2,1)S(1)}, u32[]{:S(2)}, u32[]{:S(2)}) %collective-permute-start.15) | collective-permute-done | bytes 65568 | tf_op jit(solution)/shard_map/ppermute | solution.py:42
  88.1 0.6 copy-done.11
  88.7 1.4 %shard_map.92 = (bf16[64,2048]{1,0:T(8,128)(2,1)S(1)}, f32[32,1024]{1,0:T(8,128)S(1)}, f32[32,1024]{1,0:T(8,128)S(1)}) custom-call(bf16[64,2048]{1,0:T(8,128)(2,1)S(1)} %collective-permute-done.12.refs_0_, bf16[64,2048]{1,0:T(8,128)(2,1)S(1)} %shard_map.87.refs_1_, bf16[1024,2048]{1,0:T(8,128)(2,1)S(1)} %bitcast.15), custom_call_target="tpu_custom_call" | custom-call | flops 1000 | bytes 1000 | tf_op jit(solution)/shard_map/pallas_call | solution.py:22
  90.2 0.5 collective-permute-start.16
  90.7 0.7 shard_map.95
  91.4 0.8 collective-permute-start.18
  92.2 3.1 %collective-permute-start.19 = (bf16[32,1024]{1,0:T(8,128)(2,1)}, bf16[32,1024]{1,0:T(8,128)(2,1)}, u32[]{:S(2)}, u32[]{:S(2)}) collective-permute-start(bf16[32,1024]{1,0:T(8,128)(2,1)} %get-tuple-element.87), channel_id=1, source_target_pairs={{0,14},{1,15},{2,12},{3,13},{4,10},{5,11},{6,8},{7,9},{8,6},{9,7},... | collective-permute-start | bytes 196616 | tf_op jit(solution)/shard_map/ppermute | solution.py:42
  95.3 0.7 shard_map.96
  96.0 1.4 %collective-permute-start.21 = (bf16[32,1024]{1,0:T(8,128)(2,1)}, bf16[32,1024]{1,0:T(8,128)(2,1)}, u32[]{:S(2)}, u32[]{:S(2)}) collective-permute-start(bf16[32,1024]{1,0:T(8,128)(2,1)} %shard_map.96), channel_id=1, source_target_pairs={{0,2},{1,3},{2,0},{3,1},{4,6},{5,7},{6,4},{7,5},{8,10},{9,11},{10,... | collective-permute-start | bytes 196616 | tf_op jit(solution)/shard_map/ppermute | solution.py:42
  97.4 1.0 shard_map.94.refs_0_
  98.4 1.1 collective-permute-done.19.refs_6_
  99.5 1.1 collective-permute-done.21.refs_7_
  100.7 0.8 copy-done.6
  101.5 0.8 copy-done.8
  102.3 0.8 copy-done.10
  103.2 0.8 copy-done.12
  104.0 1.2 %shard_map.97 = (bf16[128,512]{1,0:T(8,128)(2,1)S(1)}, bf16[128,512]{1,0:T(8,128)(2,1)S(1)}) custom-call(s32[8,128]{1,0:T(8,128)S(1)} %get-tuple-element.81.info, bf16[32,1024]{1,0:T(8,128)(2,1)S(1)} %shard_map.94.refs_0_, bf16[32,1024]{1,0:T(8,128)(2,1)S(1)} %copy-done.6, bf16[32,1024]{1,0:T(8,128)(2,1)S(1)} %copy-done.8, bf16[32,1024]{1,0:T(8,128)(2,1)S(1)} %copy-done.10, ...), custom_call_target="tpu_custom_call" | custom-call | flops 1000 | bytes 1000 | tf_op jit(solution)/shard_map/pallas_call | solution.py:22
  105.2 3.4 %collective-permute-start.22 = (bf16[128,512]{1,0:T(8,128)(2,1)S(1)}, bf16[128,512]{1,0:T(8,128)(2,1)S(1)}, u32[]{:S(2)}, u32[]{:S(2)}) collective-permute-start(bf16[128,512]{1,0:T(8,128)(2,1)S(1)} %get-tuple-element.91), channel_id=1, source_target_pairs={{0,16},{1,17},{2,18},{3,19},{4,20},{5,21},{6,22},{7,23},{8,24},{9,... | collective-permute-start | bytes 393224 | tf_op jit(solution)/shard_map/ppermute | solution.py:374
  108.6 6.3 %shard_map.93 = f32[1024,2048]{1,0:T(8,128)} custom-call(bf16[1024,512]{1,0:T(8,128)(2,1)S(1)} %get-tuple-element.59.turned, bf16[64,2048]{1,0:T(8,128)(2,1)S(1)} %get-tuple-element.61.refs_0_, bf16[128,2048]{1,0:T(8,128)(2,1)S(1)} %get-tuple-element.64.refs_1_, bf16[128,2048]{1,0:T(8,128)(2,1)S(1)} %get-tuple-element.68.refs_2_, ...), custom_call_target="tpu_custom_call" | custom-call | flops 2147483648 | bytes 8388608 | tf_op jit(solution)/shard_map/pallas_call | solution.py:377
  114.9 0.7 broadcast_select_fusion
  (42 shorter events, 0.5 us)
Async XLA Ops:
  0.6 1.0 copy-start.4
  1.6 0.7 copy-start.13
  2.3 0.7 copy-start.14
  2.9 0.7 copy-start.16
  5.0 34.9 %all-to-all-start = ((bf16[8,32,1024]{2,1,0:T(8,128)(2,1)}), bf16[8,32,1024]{2,1,0:T(8,128)(2,1)S(1)}, u32[]{:S(2)}, u32[]{:S(2)}) async-start(bf16[8,32,1024]{2,1,0:T(8,128)(2,1)} %get-tuple-element.48), calls=%async_computation | async-start | bytes 1048576 | tf_op jit(solution)/shard_map/all_to_all | solution.py:52
  12.3 1.4 %collective-permute-start = (bf16[96,1024]{1,0:T(8,128)(2,1)S(1)}, bf16[96,1024]{1,0:T(8,128)(2,1)S(1)}, u32[]{:S(2)}, u32[]{:S(2)}) collective-permute-start(bf16[96,1024]{1,0:T(8,128)(2,1)S(1)} %get-tuple-element.49.own), channel_id=1, source_target_pairs={{0,1},{1,0},{2,3},{3,2},{4,5},{5,4},{6,7},{7,6},{8,9},{9,8},{10,11... | collective-permute-start | bytes 589832 | tf_op jit(solution)/shard_map/ppermute | solution.py:35
  13.8 12.1 %collective-permute-start.2 = (bf16[64,1024]{1,0:T(8,128)(2,1)S(1)}, bf16[64,1024]{1,0:T(8,128)(2,1)S(1)}, u32[]{:S(2)}, u32[]{:S(2)}) collective-permute-start(bf16[64,1024]{1,0:T(8,128)(2,1)S(1)} %get-tuple-element.51), channel_id=1, source_target_pairs={{0,4},{1,5},{2,6},{3,7},{4,0},{5,1},{6,2},{7,3},{8,12},{9,13},{10,... | collective-permute-start | bytes 393224 | tf_op jit(solution)/shard_map/ppermute | solution.py:42
  15.8 13.8 %collective-permute-start.3 = (bf16[64,1024]{1,0:T(8,128)(2,1)S(1)}, bf16[64,1024]{1,0:T(8,128)(2,1)S(1)}, u32[]{:S(2)}, u32[]{:S(2)}) collective-permute-start(bf16[64,1024]{1,0:T(8,128)(2,1)S(1)} %get-tuple-element.53), channel_id=1, source_target_pairs={{0,6},{1,7},{2,4},{3,5},{4,2},{5,3},{6,0},{7,1},{8,14},{9,15},{10,... | collective-permute-start | bytes 393224 | tf_op jit(solution)/shard_map/ppermute | solution.py:42
  17.3 2.2 %copy-start = (bf16[1,1024,2048]{2,1,0:T(8,128)(2,1)S(1)}, bf16[1,1024,2048]{2,1,0:T(8,128)(2,1)}, u32[]{:S(2)}) copy-start(bf16[1,1024,2048]{2,1,0:T(8,128)(2,1)} %param.11) | copy-start | bytes 12582916
  20.3 13.8 %collective-permute-start.1 = (bf16[64,2048]{1,0:T(8,128)(2,1)S(1)}, bf16[64,2048]{1,0:T(8,128)(2,1)S(1)}, u32[]{:S(2)}, u32[]{:S(2)}) collective-permute-start(bf16[64,2048]{1,0:T(8,128)(2,1)S(1)} %shard_map.79.refs_1_), channel_id=1, source_target_pairs={{0,16},{16,0},{1,17},{17,1},{2,18},{18,2},{3,19},{19,3},{4,20},{20... | collective-permute-start | bytes 786440 | tf_op jit(solution)/shard_map/ppermute | solution.py:46
  29.6 2.2 %copy-start.1 = (bf16[1,1024,2048]{2,1,0:T(8,128)(2,1)S(1)}, bf16[1,1024,2048]{2,1,0:T(8,128)(2,1)}, u32[]{:S(2)}) copy-start(bf16[1,1024,2048]{2,1,0:T(8,128)(2,1)} %param.11) | copy-start | bytes 12582916
  32.6 7.3 %collective-permute-start.4 = (bf16[64,2048]{1,0:T(8,128)(2,1)S(1)}, bf16[64,2048]{1,0:T(8,128)(2,1)S(1)}, u32[]{:S(2)}, u32[]{:S(2)}) collective-permute-start(bf16[64,2048]{1,0:T(8,128)(2,1)S(1)} %get-tuple-element.54.refs_2_), channel_id=1, source_target_pairs={{0,16},{16,0},{1,17},{17,1},{2,18},{18,2},{3,19},{19,3},{4,20},{20... | collective-permute-start | bytes 786440 | tf_op jit(solution)/shard_map/ppermute | solution.py:46
  39.9 1.7 %collective-permute-start.6 = (bf16[160,1024]{1,0:T(8,128)(2,1)S(1)}, bf16[160,1024]{1,0:T(8,128)(2,1)S(1)}, u32[]{:S(2)}, u32[]{:S(2)}) collective-permute-start(bf16[160,1024]{1,0:T(8,128)(2,1)S(1)} %shard_map.81.refs_0_.refs_3_), channel_id=1, source_target_pairs={{0,1},{1,0},{2,3},{3,2},{4,5},{5,4},{6,7},{7,6},{8,9},{9,8},{10,11... | collective-permute-start | bytes 983048 | tf_op jit(solution)/shard_map/ppermute | solution.py:35
  40.0 9.2 %collective-permute-start.5 = (bf16[64,2048]{1,0:T(8,128)(2,1)S(1)}, bf16[64,2048]{1,0:T(8,128)(2,1)S(1)}, u32[]{:S(2)}, u32[]{:S(2)}) collective-permute-start(bf16[64,2048]{1,0:T(8,128)(2,1)S(1)} %get-tuple-element.56.refs_3_), channel_id=1, source_target_pairs={{0,16},{16,0},{1,17},{17,1},{2,18},{18,2},{3,19},{19,3},{4,20},{20... | collective-permute-start | bytes 786440 | tf_op jit(solution)/shard_map/ppermute | solution.py:46
  41.6 2.2 %copy-start.2 = (bf16[1,1024,2048]{2,1,0:T(8,128)(2,1)S(1)}, bf16[1,1024,2048]{2,1,0:T(8,128)(2,1)}, u32[]{:S(2)}) copy-start(bf16[1,1024,2048]{2,1,0:T(8,128)(2,1)} %param.11) | copy-start | bytes 12582916
  43.8 7.7 %copy-start.3 = (bf16[1,1024,2048]{2,1,0:T(8,128)(2,1)S(1)}, bf16[1,1024,2048]{2,1,0:T(8,128)(2,1)}, u32[]{:S(2)}) copy-start(bf16[1,1024,2048]{2,1,0:T(8,128)(2,1)} %param.11) | copy-start | bytes 12582916
  44.6 20.9 %copy-start.15 = (s32[200]{0:T(256)S(1)}, s32[200]{0:T(256)}, u32[]{:S(2)}) copy-start(s32[200]{0:T(256)} %param.10) | copy-start | bytes 2404
  44.6 22.5 %collective-permute-start.7 = (bf16[128,2048]{1,0:T(8,128)(2,1)S(1)}, bf16[128,2048]{1,0:T(8,128)(2,1)S(1)}, u32[]{:S(2)}, u32[]{:S(2)}) collective-permute-start(bf16[128,2048]{1,0:T(8,128)(2,1)S(1)} %shard_map.82.refs_1_), channel_id=1, source_target_pairs={{0,16},{16,0},{1,17},{17,1},{2,18},{18,2},{3,19},{19,3},{4,20},{20... | collective-permute-start | bytes 1572872 | tf_op jit(solution)/shard_map/ppermute | solution.py:46
  49.9 26.0 %collective-permute-start.8 = (bf16[128,2048]{1,0:T(8,128)(2,1)S(1)}, bf16[128,2048]{1,0:T(8,128)(2,1)S(1)}, u32[]{:S(2)}, u32[]{:S(2)}) collective-permute-start(bf16[128,2048]{1,0:T(8,128)(2,1)S(1)} %shard_map.83.refs_1_), channel_id=1, source_target_pairs={{0,16},{16,0},{1,17},{17,1},{2,18},{18,2},{3,19},{19,3},{4,20},{20... | collective-permute-start | bytes 1572872 | tf_op jit(solution)/shard_map/ppermute | solution.py:46
  55.0 15.1 %collective-permute-start.9 = (f32[64,1024]{1,0:T(8,128)S(1)}, f32[64,1024]{1,0:T(8,128)S(1)}, u32[]{:S(2)}, u32[]{:S(2)}) collective-permute-start(f32[64,1024]{1,0:T(8,128)S(1)} %get-tuple-element.70), channel_id=1, source_target_pairs={{0,1},{1,0},{2,3},{3,2},{4,5},{5,4},{6,7},{7,6},{8,9},{9,8},{10,11... | collective-permute-start | bytes 786440 | tf_op jit(solution)/shard_map/ppermute | solution.py:35
  69.4 8.0 %collective-permute-start.13 = (f32[64,1024]{1,0:T(8,128)S(1)}, f32[64,1024]{1,0:T(8,128)S(1)}, u32[]{:S(2)}, u32[]{:S(2)}) collective-permute-start(f32[64,1024]{1,0:T(8,128)S(1)} %get-tuple-element.76), channel_id=1, source_target_pairs={{0,1},{1,0},{2,3},{3,2},{4,5},{5,4},{6,7},{7,6},{8,9},{9,8},{10,11... | collective-permute-start | bytes 786440 | tf_op jit(solution)/shard_map/ppermute | solution.py:35
  69.5 11.9 %collective-permute-start.12 = (bf16[64,2048]{1,0:T(8,128)(2,1)S(1)}, bf16[64,2048]{1,0:T(8,128)(2,1)S(1)}, u32[]{:S(2)}, u32[]{:S(2)}) collective-permute-start(bf16[64,2048]{1,0:T(8,128)(2,1)S(1)} %shard_map.87.refs_1_), channel_id=1, source_target_pairs={{0,16},{16,0},{1,17},{17,1},{2,18},{18,2},{3,19},{19,3},{4,20},{20... | collective-permute-start | bytes 786440 | tf_op jit(solution)/shard_map/ppermute | solution.py:46
  70.2 4.9 %collective-permute-start.10 = (bf16[32,1024]{1,0:T(8,128)(2,1)S(1)}, bf16[32,1024]{1,0:T(8,128)(2,1)S(1)}, u32[]{:S(2)}, u32[]{:S(2)}) collective-permute-start(bf16[32,1024]{1,0:T(8,128)(2,1)S(1)} %get-tuple-element.71), channel_id=1, source_target_pairs={{0,4},{1,5},{2,6},{3,7},{4,0},{5,1},{6,2},{7,3},{8,12},{9,13},{10,... | collective-permute-start | bytes 196616 | tf_op jit(solution)/shard_map/ppermute | solution.py:42
  70.7 5.2 %collective-permute-start.11 = (bf16[32,1024]{1,0:T(8,128)(2,1)S(1)}, bf16[32,1024]{1,0:T(8,128)(2,1)S(1)}, u32[]{:S(2)}, u32[]{:S(2)}) collective-permute-start(bf16[32,1024]{1,0:T(8,128)(2,1)S(1)} %get-tuple-element.72), channel_id=1, source_target_pairs={{0,6},{1,7},{2,4},{3,5},{4,2},{5,3},{6,0},{7,1},{8,14},{9,15},{10,... | collective-permute-start | bytes 196616 | tf_op jit(solution)/shard_map/ppermute | solution.py:42
  75.1 13.0 %copy-start.5 = (bf16[32,1024]{1,0:T(8,128)(2,1)}, bf16[32,1024]{1,0:T(8,128)(2,1)S(1)}, u32[]{:S(2)}) copy-start(bf16[32,1024]{1,0:T(8,128)(2,1)S(1)} %collective-permute-done.10.refs_1_) | copy-start | bytes 196612
  75.9 12.2 %copy-start.7 = (bf16[32,1024]{1,0:T(8,128)(2,1)}, bf16[32,1024]{1,0:T(8,128)(2,1)S(1)}, u32[]{:S(2)}) copy-start(bf16[32,1024]{1,0:T(8,128)(2,1)S(1)} %collective-permute-done.11.refs_2_) | copy-start | bytes 196612
  77.4 13.3 %collective-permute-start.17 = (f32[64,1024]{1,0:T(8,128)S(1)}, f32[64,1024]{1,0:T(8,128)S(1)}, u32[]{:S(2)}, u32[]{:S(2)}) collective-permute-start(f32[64,1024]{1,0:T(8,128)S(1)} %get-tuple-element.85), channel_id=1, source_target_pairs={{0,1},{1,0},{2,3},{3,2},{4,5},{5,4},{6,7},{7,6},{8,9},{9,8},{10,11... | collective-permute-start | bytes 786440 | tf_op jit(solution)/shard_map/ppermute | solution.py:35
  77.6 8.6 %collective-permute-start.14 = (bf16[32,1024]{1,0:T(8,128)(2,1)S(1)}, bf16[32,1024]{1,0:T(8,128)(2,1)S(1)}, u32[]{:S(2)}, u32[]{:S(2)}) collective-permute-start(bf16[32,1024]{1,0:T(8,128)(2,1)S(1)} %get-tuple-element.77), channel_id=1, source_target_pairs={{0,8},{1,9},{2,10},{3,11},{4,12},{5,13},{6,14},{7,15},{8,0},{9,1},... | collective-permute-start | bytes 196616 | tf_op jit(solution)/shard_map/ppermute | solution.py:42
  78.3 9.8 %collective-permute-start.15 = (bf16[32,1024]{1,0:T(8,128)(2,1)S(1)}, bf16[32,1024]{1,0:T(8,128)(2,1)S(1)}, u32[]{:S(2)}, u32[]{:S(2)}) collective-permute-start(bf16[32,1024]{1,0:T(8,128)(2,1)S(1)} %get-tuple-element.78), channel_id=1, source_target_pairs={{0,10},{1,11},{2,8},{3,9},{4,14},{5,15},{6,12},{7,13},{8,2},{9,3},... | collective-permute-start | bytes 196616 | tf_op jit(solution)/shard_map/ppermute | solution.py:42
  86.2 0.6 copy-start.9
  88.1 0.6 copy-start.11
  90.1 5.2 %collective-permute-start.20 = (f32[32,1024]{1,0:T(8,128)S(1)}, f32[32,1024]{1,0:T(8,128)S(1)}, u32[]{:S(2)}, u32[]{:S(2)}) collective-permute-start(f32[32,1024]{1,0:T(8,128)S(1)} %get-tuple-element.89), channel_id=1, source_target_pairs={{0,1},{1,0},{2,3},{3,2},{4,5},{5,4},{6,7},{7,6},{8,9},{9,8},{10,11... | collective-permute-start | bytes 393224 | tf_op jit(solution)/shard_map/ppermute | solution.py:35
  90.2 7.2 %collective-permute-start.16 = (f32[32,1024]{1,0:T(8,128)}, f32[32,1024]{1,0:T(8,128)}, u32[]{:S(2)}, u32[]{:S(2)}) collective-permute-start(f32[32,1024]{1,0:T(8,128)} %get-tuple-element.83), channel_id=1, source_target_pairs={{0,1},{1,0},{2,3},{3,2},{4,5},{5,4},{6,7},{7,6},{8,9},{9,8},{10,11... | collective-permute-start | bytes 393224 | tf_op jit(solution)/shard_map/ppermute | solution.py:35
  91.4 7.0 %collective-permute-start.18 = (bf16[32,1024]{1,0:T(8,128)(2,1)}, bf16[32,1024]{1,0:T(8,128)(2,1)}, u32[]{:S(2)}, u32[]{:S(2)}) collective-permute-start(bf16[32,1024]{1,0:T(8,128)(2,1)} %get-tuple-element.86), channel_id=1, source_target_pairs={{0,12},{1,13},{2,14},{3,15},{4,8},{5,9},{6,10},{7,11},{8,4},{9,5},... | collective-permute-start | bytes 196616 | tf_op jit(solution)/shard_map/ppermute | solution.py:42
  92.2 7.3 %collective-permute-start.19 = (bf16[32,1024]{1,0:T(8,128)(2,1)}, bf16[32,1024]{1,0:T(8,128)(2,1)}, u32[]{:S(2)}, u32[]{:S(2)}) collective-permute-start(bf16[32,1024]{1,0:T(8,128)(2,1)} %get-tuple-element.87), channel_id=1, source_target_pairs={{0,14},{1,15},{2,12},{3,13},{4,10},{5,11},{6,8},{7,9},{8,6},{9,7},... | collective-permute-start | bytes 196616 | tf_op jit(solution)/shard_map/ppermute | solution.py:42
  96.0 4.7 %collective-permute-start.21 = (bf16[32,1024]{1,0:T(8,128)(2,1)}, bf16[32,1024]{1,0:T(8,128)(2,1)}, u32[]{:S(2)}, u32[]{:S(2)}) collective-permute-start(bf16[32,1024]{1,0:T(8,128)(2,1)} %shard_map.96), channel_id=1, source_target_pairs={{0,2},{1,3},{2,0},{3,1},{4,6},{5,7},{6,4},{7,5},{8,10},{9,11},{10,... | collective-permute-start | bytes 196616 | tf_op jit(solution)/shard_map/ppermute | solution.py:42
  100.6 0.8 copy-start.6
  101.5 0.8 copy-start.8
  102.3 0.8 copy-start.10
  103.2 0.8 copy-start.12
  105.2 9.7 %collective-permute-start.22 = (bf16[128,512]{1,0:T(8,128)(2,1)S(1)}, bf16[128,512]{1,0:T(8,128)(2,1)S(1)}, u32[]{:S(2)}, u32[]{:S(2)}) collective-permute-start(bf16[128,512]{1,0:T(8,128)(2,1)S(1)} %get-tuple-element.91), channel_id=1, source_target_pairs={{0,16},{1,17},{2,18},{3,19},{4,20},{5,21},{6,22},{7,23},{8,24},{9,... | collective-permute-start | bytes 393224 | tf_op jit(solution)/shard_map/ppermute | solution.py:374

commit v4 on v3

v4 whole, which is shorter than its diff:
```python
import functools

import jax
import jax.numpy as jnp
from jax import lax
from jax.experimental import pallas as pl
from jax.experimental.pallas import tpu as pltpu
from jax.sharding import PartitionSpec as P

F32 = jnp.float32
BF16 = jnp.bfloat16
I32 = jnp.int32
NOTES = 128
VMEM = pl.BlockSpec(memory_space=pltpu.VMEM)


def sds(shape, dtype):
    return jax.ShapeDtypeStruct(shape, dtype)


def call(kernel, outs, *args, scratch=(), limit=8, spec=VMEM):
    return pl.pallas_call(
        kernel,
        out_shape=outs,
        in_specs=[spec] * len(args),
        out_specs=jax.tree.map(lambda _: VMEM, outs),
        scratch_shapes=list(scratch),
        compiler_params=pltpu.CompilerParams(vmem_limit_bytes=limit << 20),
        cost_estimate=pl.CostEstimate(flops=1000, bytes_accessed=1000, transcendentals=0),
    )(*args)


def sibling(value):
    count = lax.axis_size("dp")
    return lax.ppermute(value, "dp", [(i, i ^ 1) for i in range(count)])


def across(values):
    return tuple(lax.ppermute(value, "section", [(0, 1), (1, 0)]) for value in values)


def same_core_exchange(value):
    count = lax.axis_size("dp")
    groups = [list(range(core, count, 2)) for core in range(2)]
    return lax.all_to_all(
        value, "dp", split_axis=0, concat_axis=0, axis_index_groups=groups, tiled=True
    )


def after(value, *others):
    return lax.optimization_barrier((value, *others))[0]


def iota(shape, dim):
    return lax.broadcasted_iota(I32, shape, dim)


def place_kernel(*refs):
    inputs, (*packed, info), copies = refs[:4], refs[4:-5], refs[-5:]
    moves = [
        pltpu.make_async_copy(src, dst, copies[4].at[i])
        for i, (src, dst) in enumerate(zip(inputs, copies))
    ]
    for move in moves:
        move.start()
    for move in moves:
        move.wait()
    ids, table, counts, rows = copies[:4]
    chips, part, _ = packed[0].shape
    width = rows.shape[1]
    chip = lax.axis_index("dp") // 2
    rows_dev = ids.shape[1]
    languages = table.shape[1]
    lang = ids[...]
    lang_hot = (iota((languages, rows_dev), 0) == lang).astype(F32)
    block = jnp.dot(table[...].astype(F32), lang_hot, preferred_element_type=F32).astype(I32)
    block_hot = iota((chips, rows_dev), 0) == block
    earlier = (iota((rows_dev, rows_dev), 0) < iota((rows_dev, rows_dev), 1)).astype(BF16)
    running = jnp.dot(
        block_hot.astype(F32).astype(BF16), earlier, preferred_element_type=F32
    )
    slot = jnp.sum(jnp.where(block_hot, running, 0.0), axis=0, keepdims=True).astype(I32)
    info[0:1, :] = slot
    info[1:2, :] = block
    info[2:, :] = jnp.zeros((info.shape[0] - 2, rows_dev), I32)
    values = counts[...].astype(F32)
    blank = jnp.zeros((1, 2 * NOTES - 2 - languages), F32)
    tail = jnp.concatenate([values[:, NOTES - 1 :], blank, jnp.zeros((1, 1), F32)], axis=1)
    head = jnp.concatenate([values[:, : NOTES - 1], jnp.zeros((1, 1), F32)], axis=1)

    def slots(target, count, first):
        hot = iota((count, rows_dev), 0) == target
        moved = jnp.dot(
            hot.astype(F32).astype(BF16), rows[...], preferred_element_type=F32
        ).astype(BF16)
        slot_lang = jnp.sum(jnp.where(hot, lang, 0), axis=1, keepdims=True).astype(F32)
        notes = jnp.where(iota((count, NOTES), 1) == NOTES - 1, slot_lang, 0.0)
        if first:
            within = iota((count, NOTES), 0) % part
            notes = notes + jnp.where(within == 0, head, 0.0) + jnp.where(within == 1, tail, 0.0)
        return moved, notes.astype(BF16)

    for p, out in enumerate(packed):
        inside = (slot // part) == p
        target = jnp.where(inside, block * part + slot % part, -1)
        moved, notes = slots(target, chips * part, p == 0)
        out[:, :, :width] = moved.reshape(chips, part, width)
        out[:, :, width:] = notes.reshape(chips, part, NOTES)


def load_piece(inputs, piece):
    which, first, rel, size = piece
    if rel is None:
        return inputs[which][first : first + size, :]
    return inputs[which][(lax.axis_index("dp") // 2) ^ rel]


def tail_kernel(pieces, sources, temp, *refs):
    inputs, scale_out, turned, lhs = refs[:-3], refs[-3], refs[-2], refs[-1]
    width, languages = lhs.shape[1], temp.shape[1]
    totals = [0.0, 0.0]
    for source in sources:
        for row in range(2):
            for c in range(inputs[source].shape[0]):
                totals[row] = totals[row] + inputs[source][c, row : row + 1, width:].astype(F32)
    values = temp[...].astype(F32)
    blank = jnp.zeros((1, 2 * NOTES - 2 - languages), F32)
    pads = jnp.zeros((1, 1), F32)
    numer = [
        jnp.concatenate([values[:, : NOTES - 1], pads], axis=1),
        jnp.concatenate([values[:, NOTES - 1 :], blank, pads], axis=1),
    ]
    factor = 2.0 * lax.axis_size("dp")
    lane = iota((1, NOTES), 1)
    valid = [lane < NOTES - 1, lane < languages - (NOTES - 1)]
    table = [
        jnp.where(ok, factor * n / jnp.where(ok, t, 1.0), 0.0)
        for n, t, ok in zip(numer, totals, valid)
    ]
    first = 0
    for piece in pieces:
        size = piece[3]
        values = load_piece(inputs, piece).astype(F32)
        lang = values[:, width + NOTES - 1 :].astype(I32)
        number = iota((size, NOTES), 1)
        hit = jnp.where(lang == number, table[0], 0.0) + jnp.where(
            lang - (NOTES - 1) == number, table[1], 0.0
        )
        scale = jnp.sum(hit, axis=1, keepdims=True)
        scale_out[first : first + size, :] = scale
        lhs[first : first + size, :] = (values[:, :width] * scale).astype(BF16)
        first += size
    turned[...] = lhs[...].T


def product_kernel(count, pieces, *refs):
    inputs, weight, hands, rows = refs[:count], refs[count], refs[count + 1 : -1], refs[-1]
    width = rows.shape[1]
    is_up = lax.axis_index("section") == 0
    first = 0
    for piece in pieces:
        size = piece[3]
        rows[first : first + size, :] = load_piece(inputs, piece)[:, :width]
        first += size
    tile = 512
    for j in range(0, weight.shape[1], tile):
        value = jnp.dot(rows[...], weight[:, j : j + tile], preferred_element_type=F32)
        value = jnp.where(is_up, jnp.maximum(value, 0.0), value).astype(BF16)
        first = 0
        for hand in hands:
            hand[:, j : j + tile] = value[first : first + hand.shape[0]]
            first += hand.shape[0]


def stack_kernel(first, count, scale, *rest):
    mine, theirs, out = rest[:count], rest[count:-1], rest[-1]
    chip = lax.axis_index("dp") // 2
    chips, part, _ = out.shape
    total = jnp.concatenate([m[...] for m in mine], axis=0)
    total = total + jnp.concatenate([t[...] for t in theirs], axis=1)
    total = (total * scale[first : first + part * chips, :]).astype(BF16)
    for rel in range(chips):
        out[chip ^ rel] = total[rel * part : (rel + 1) * part]


def back_kernel(recv, hand, weight, partner, *outs):
    is_up = lax.axis_index("section") == 0
    masked = is_up & (hand[...] <= 0)
    value = jnp.where(masked, jnp.zeros_like(recv), recv[...])
    partner[...] = value
    product = lax.dot_general(
        value, weight[...], (((1,), (1,)), ((), ())), preferred_element_type=F32
    )
    first = 0
    column = 0
    for out in outs:
        size, columns = out.shape
        out[...] = product[first : first + size, column : column + columns]
        column = (column + columns) % product.shape[1]
        first += size if column == 0 else 0


def weight_kernel(turned, *refs):
    partners, out = refs[:-1], refs[-1]
    rhs = jnp.concatenate([p[...] for p in partners], axis=0)
    out[...] = jnp.dot(turned[...], rhs, preferred_element_type=F32)


def final_kernel(info, *refs):
    backs, left, right = refs[:-2], refs[-2], refs[-1]
    slot, block = info[0:1, :], info[1:2, :]
    rows_dev = slot.shape[1]
    chips, part, _ = backs[0].shape
    target = (slot // part) * (chips * part) + block * part + slot % part
    values = jnp.concatenate([b[...].reshape(chips * part, -1) for b in backs], axis=0)
    hot = (iota((values.shape[0], rows_dev), 0) == target).astype(F32).astype(BF16)
    rows = lax.dot_general(
        hot, values, (((0,), (0,)), ((), ())), preferred_element_type=F32
    ).astype(BF16)
    half = left.shape[1]
    left[...] = rows[:, :half]
    right[...] = rows[:, half:]


def on_device(section_rows, lang_ids, lang_table, lang_counts, temp_num, weights):
    is_up = lax.axis_index("section") == 0
    replicas = lax.axis_size("dp")
    chips = replicas // 2
    rows_dev = lang_ids.shape[0]
    cap = 2 * rows_dev // chips
    width = section_rows.shape[2]
    own_weight = weights[0]
    ff_dev = own_weight.shape[1]

    halves = 2
    part = cap // halves
    wide = width + NOTES

    *packed, info = call(
        place_kernel,
        (
            *(sds((chips, part, wide), BF16) for _ in range(halves)),
            sds((8, rows_dev), I32),
        ),
        lang_ids.reshape(1, -1),
        lang_table.reshape(1, -1),
        lang_counts,
        section_rows[0],
        scratch=[
            pltpu.VMEM((1, rows_dev), I32),
            pltpu.VMEM((1, lang_table.shape[0]), I32),
            pltpu.VMEM(lang_counts.shape, I32),
            pltpu.VMEM((rows_dev, width), BF16),
            pltpu.SemaphoreType.DMA((4,)),
        ],
        spec=pl.BlockSpec(memory_space=pltpu.HBM),
        limit=60,
    )

    hands, received, partners = [], [], []

    def product(inputs, pieces, sizes):
        count = sum(sizes)
        hand = call(
            functools.partial(product_kernel, len(inputs), pieces),
            tuple(sds((size, ff_dev), BF16) for size in sizes),
            *inputs,
            own_weight,
            scratch=[pltpu.VMEM((count, width), BF16)],
        )
        hands.append(hand)
        received.append(across(hand))

    def back_product(g, which, shapes, *earlier):
        rows = hands[g][which].shape[0]
        partner, *outs = call(
            back_kernel,
            (sds((rows, ff_dev), BF16), *(sds(shape, F32) for shape in shapes)),
            after(received[g][which], *earlier),
            hands[g][which],
            own_weight,
        )
        partners.append(partner)
        return outs

    came, chunks = [], []
    for p in range(halves):
        packed[p] = after(packed[p], *(hands[-1] if p else ()))
        own = same_core_exchange(packed[p])
        came += [own, sibling(own)]
        cores = (1, 0) if p else (0, 1)
        chunks.append([(c, 0, r, part) for c in cores for r in range(chips)])
        rows = 2 * part * chips
        product(came[2 * p :], chunks[p], [5 * rows // 8, 3 * rows // 8] if p else [rows])
    layout = [(2 * p + which, *rest) for p in range(halves) for which, *rest in chunks[p]]
    total_rows = halves * rows
    scale, turned = call(
        functools.partial(tail_kernel, layout, [0, 1]),
        (sds((total_rows, 1), F32), sds((width, total_rows), BF16)),
        after(temp_num.reshape(1, -1), *hands[-1]),
        *came,
        scratch=[pltpu.VMEM((total_rows, width), BF16)],
    )
    def stacked(first, mine, theirs):
        return call(
            functools.partial(stack_kernel, first, len(mine)),
            sds((chips, part, width), BF16),
            scale,
            *mine,
            *theirs,
        )

    count = rows // 2
    half = (count, width // 2)
    mine, *theirs = back_product(0, 0, [(count, width), half, half], scale, *hands[1])
    stack = stacked(0, [mine], [sibling(t) for t in theirs])
    back = [same_core_exchange(stack)]
    *theirs, first = back_product(
        1, 0, [half, half, (count // 4, width)], partners[0], back[0]
    )
    theirs = [sibling(t) for t in theirs]
    (second,) = back_product(1, 1, [(3 * count // 4, width)], partners[1])
    back.append(same_core_exchange(stacked(rows + count, [first, second], theirs)))
    tile = 256
    weight_grad = pl.pallas_call(
        weight_kernel,
        out_shape=sds((width, ff_dev), F32),
        grid=(ff_dev // tile,),
        in_specs=[pl.BlockSpec((width, total_rows), lambda j: (0, 0))]
        + [pl.BlockSpec((p.shape[0], tile), lambda j: (0, j)) for p in partners],
        out_specs=pl.BlockSpec((width, tile), lambda j: (0, j)),
        compiler_params=pltpu.CompilerParams(vmem_limit_bytes=60 << 20),
        cost_estimate=pl.CostEstimate(
            flops=2 * width * total_rows * ff_dev,
            bytes_accessed=4 * width * ff_dev,
            transcendentals=0,
        ),
    )(turned, *partners)
    info = after(info, weight_grad)
    left, right = call(
        final_kernel,
        (sds((rows_dev, width // 2), BF16),) * 2,
        info,
        *back,
    )
    (right_cols,) = across([right])
    input_grad = jnp.where(is_up, left, right_cols)
    return (weight_grad[None], input_grad)


def solution(mesh):
    return jax.shard_map(
        on_device,
        mesh=mesh,
        in_specs=(
            P("section", "dp", None),
            P("dp"),
            P(),
            P("dp", None),
            P(),
            P("section", None, "dp"),
        ),
        out_specs=(P("section", None, "dp"), P("dp", "section")),
        check_vma=False,
    )
```

time: 116 us -> 101 us (0.87)
  blocking collectives: 10.4 us -> 31.6 us
  starting transfers between devices: 34.6 us -> 13.9 us
  waiting for transfers between devices: 30.1 us -> 22.5 us
  local copies, waits for them, and re-layouts: 14.2 us -> 7.89 us
  Pallas kernels: 24.9 us -> 22.7 us
    all_to_all x1 -> x2, blocking collectives: 10.4 us -> 31.6 us  [same_core_exchange(): lax.all_to_all(value, 'dp', split_axis=0, concat_axis=0, axis_index_group...]
    ppermute x10 -> x0, waiting for transfers between devices: 19.7 us -> none  [the longest x9 19.7 us: relation(): return lax.ppermute(value, 'dp', [(i, i ^ 2 * rel) for i in range(count)])]
    ppermute x10 -> x0, starting transfers between devices: 18.1 us -> none  [the longest x9 14.7 us: relation(): return lax.ppermute(value, 'dp', [(i, i ^ 2 * rel) for i in range(count)])]
    ppermute x6 -> x4, waiting for transfers between devices: 8.86 us -> 19.3 us  [across(): lax.ppermute(value, 'section', [(0, 1), (1, 0)])]
    unnamed x34 -> x18, local copies, waits for them, and re-layouts: 14.1 us -> 7.89 us
    pallas_call x20 -> x10, Pallas kernels: 18.6 us -> 13.9 us  [call(): pl.pallas_call(kernel, out_shape=outs, in_specs=[spec] * len(args), out_s...]
    pallas_call x1, Pallas kernels: 6.3 us -> 8.8 us  [on_device(): pl.pallas_call(weight_kernel, out_shape=sds((width, ff_dev), F32), grid=(...]
    ppermute x6 -> x4, starting transfers between devices: 8.35 us -> 6.05 us  [across(): lax.ppermute(value, 'section', [(0, 1), (1, 0)])]
  transfers between devices with their start and end apart: 24 -> 12, of which waited for: 12 -> 6; matrix products, arithmetic and copies ran while one was open for 0% -> 0% of each run, Pallas kernels for 19% -> 17%
where the time goes in v4:
time: 101 us; the launch traced here: 100 us
  blocking collectives  31.6 us (31%)
  Pallas kernels  22.7 us (22%)
  waiting for transfers between devices  22.5 us (22%)
  starting transfers between devices  13.9 us (14%)
  local copies, waits for them, and re-layouts  7.89 us (8%)
    all_to_all x2, blocking collectives, same_core_exchange(): lax.all_to_all(value, 'dp', split_axis=0, concat_axis=0, axis_index_group...  31.6 us
    ppermute x4, waiting for transfers between devices, across(): lax.ppermute(value, 'section', [(0, 1), (1, 0)])  19.3 us
    pallas_call x10, Pallas kernels, call(): pl.pallas_call(kernel, out_shape=outs, in_specs=[spec] * len(args), out_s...  13.9 us
    pallas_call x1, Pallas kernels, on_device(): pl.pallas_call(weight_kernel, out_shape=sds((width, ff_dev), F32), grid=(...  8.8 us
    unnamed x18, local copies, waits for them, and re-layouts  7.89 us
    all_to_all x2, starting transfers between devices, same_core_exchange(): lax.all_to_all(value, 'dp', split_axis=0, concat_axis=0, axis_index_group...  6.82 us
    ppermute x4, starting transfers between devices, across(): lax.ppermute(value, 'section', [(0, 1), (1, 0)])  6.05 us
    ppermute x6, waiting for transfers between devices, sibling(): return lax.ppermute(value, 'dp', [(i, i ^ 1) for i in range(count)])  3.17 us
  transfers between devices with their start and end apart: 12, of which 6 were waited for; matrix products, arithmetic and copies ran while one was open for 0% of the time, Pallas kernels for 17%

profile of v4, /device:TPU:0, one launch (start us, length us, event | category | flops | bytes accessed | tf_op | source)
XLA Modules:
  0.0 100.0 jit_solution(2412442408160337235)
XLA Ops:
  0.6 0.0 copy-start.8
  0.6 2.3 %shard_map.77 = (bf16[8,16,1152]{2,1,0:T(8,128)(2,1)}, bf16[8,16,1152]{2,1,0:T(8,128)(2,1)}, s32[8,128]{1,0:T(8,128)}) custom-call(s32[1,128]{1,0:T(1,128)} %bitcast.15, s32[1,200]{1,0:T(1,128)} %bitcast.14, s32[1,200]{1,0:T(1,128)} %refs_2_.1, bf16[128,1024]{1,0:T(8,128)(2,1)} %bitcast.13), custom_call_target="tpu_custom_call" | custom-call | flops 1000 | bytes 1000 | tf_op jit(solution)/shard_map/pallas_call | solution.py:22
  3.0 17.6 %all_to_all.20.refs_0_ = bf16[8,16,1152]{2,1,0:T(8,128)(2,1)S(1)} all-to-all(bf16[8,16,1152]{2,1,0:T(8,128)(2,1)} %get-tuple-element.28), channel_id=1, replica_groups={{0,2,4,6,8,10,12,14},{1,3,5,7,9,11,13,15},{16,18,20,22,24,26,28,30},{17..., dimensions={0} | all-to-all | bytes 589824 | tf_op jit(solution)/shard_map/all_to_all | solution.py:45
  20.6 0.0 collective-permute-start
  20.6 1.6 %collective-permute-done.refs_1_ = bf16[8,16,1152]{2,1,0:T(8,128)(2,1)S(1)} collective-permute-done((bf16[8,16,1152]{2,1,0:T(8,128)(2,1)S(1)}, bf16[8,16,1152]{2,1,0:T(8,128)(2,1)S(1)}, u32[]{:S(2)}, u32[]{:S(2)}) %collective-permute-start) | collective-permute-done | bytes 294944 | tf_op jit(solution)/shard_map/ppermute | solution.py:35
  22.2 0.0 copy-start
  22.2 2.2 %copy-done = bf16[1,1024,2048]{2,1,0:T(8,128)(2,1)S(1)} copy-done((bf16[1,1024,2048]{2,1,0:T(8,128)(2,1)S(1)}, bf16[1,1024,2048]{2,1,0:T(8,128)(2,1)}, u32[]{:S(2)}) %copy-start) | copy-done | bytes 4194328
  24.4 0.0 copy-start.1
  24.4 1.3 %shard_map.78.hand = bf16[256,2048]{1,0:T(8,128)(2,1)S(1)} custom-call(bf16[8,16,1152]{2,1,0:T(8,128)(2,1)S(1)} %all_to_all.20.refs_0_, bf16[8,16,1152]{2,1,0:T(8,128)(2,1)S(1)} %collective-permute-done.refs_1_, bf16[1024,2048]{1,0:T(8,128)(2,1)S(1)} %bitcast.6), custom_call_target="tpu_custom_call" | custom-call | flops 1000 | bytes 1000 | tf_op jit(solution)/shard_map/pallas_call | solution.py:22
  25.7 1.6 %collective-permute-start.2 = (bf16[256,2048]{1,0:T(8,128)(2,1)S(1)}, bf16[256,2048]{1,0:T(8,128)(2,1)S(1)}, u32[]{:S(2)}, u32[]{:S(2)}) collective-permute-start(bf16[256,2048]{1,0:T(8,128)(2,1)S(1)} %shard_map.78.hand), channel_id=1, source_target_pairs={{0,16},{16,0},{1,17},{17,1},{2,18},{18,2},{3,19},{19,3},{4,20},{20... | collective-permute-start | bytes 3145736 | tf_op jit(solution)/shard_map/ppermute | solution.py:39
  27.2 14.0 %all_to_all.21.refs_0_.refs_2_ = bf16[8,16,1152]{2,1,0:T(8,128)(2,1)S(1)} all-to-all(bf16[8,16,1152]{2,1,0:T(8,128)(2,1)} %get-tuple-element.29), channel_id=1, replica_groups={{0,2,4,6,8,10,12,14},{1,3,5,7,9,11,13,15},{16,18,20,22,24,26,28,30},{17..., dimensions={0} | all-to-all | bytes 589824 | tf_op jit(solution)/shard_map/all_to_all | solution.py:45
  41.2 0.0 collective-permute-start.1
  41.2 1.6 %collective-permute-done.1.refs_1_.refs_3_ = bf16[8,16,1152]{2,1,0:T(8,128)(2,1)S(1)} collective-permute-done((bf16[8,16,1152]{2,1,0:T(8,128)(2,1)S(1)}, bf16[8,16,1152]{2,1,0:T(8,128)(2,1)S(1)}, u32[]{:S(2)}, u32[]{:S(2)}) %collective-permute-start.1) | collective-permute-done | bytes 294944 | tf_op jit(solution)/shard_map/ppermute | solution.py:35
  42.8 1.3 %shard_map.79 = (bf16[160,2048]{1,0:T(8,128)(2,1)S(1)}, bf16[96,2048]{1,0:T(8,128)(2,1)S(1)}) custom-call(bf16[8,16,1152]{2,1,0:T(8,128)(2,1)S(1)} %all_to_all.21.refs_0_.refs_2_, bf16[8,16,1152]{2,1,0:T(8,128)(2,1)S(1)} %collective-permute-done.1.refs_1_.refs_3_, bf16[1024,2048]{1,0:T(8,128)(2,1)S(1)} %bitcast.7), custom_call_target="tpu_custom_call" | custom-call | flops 1000 | bytes 1000 | tf_op jit(solution)/shard_map/pallas_call | solution.py:22
  44.1 0.0 copy-done.8
  44.1 2.9 %shard_map.80 = (f32[512,1]{1,0:T(8,128)S(1)}, bf16[1024,512]{1,0:T(8,128)(2,1)S(1)}) custom-call(s32[1,200]{1,0:T(1,128)S(1)} %bitcast.11, bf16[8,16,1152]{2,1,0:T(8,128)(2,1)S(1)} %all_to_all.20.refs_0_, bf16[8,16,1152]{2,1,0:T(8,128)(2,1)S(1)} %collective-permute-done.refs_1_, bf16[8,16,1152]{2,1,0:T(8,128)(2,1)S(1)} %all_to_all.21.refs_0_.refs_2_, ...), custom_call_target="tpu_custom_call" | custom-call | flops 1000 | bytes 1000 | tf_op jit(solution)/shard_map/pallas_call | solution.py:22
  46.9 0.0 copy-start.3
  47.0 1.0 copy-done.3
  47.9 3.0 %collective-permute-done.2.recv = bf16[256,2048]{1,0:T(8,128)(2,1)S(1)} collective-permute-done((bf16[256,2048]{1,0:T(8,128)(2,1)S(1)}, bf16[256,2048]{1,0:T(8,128)(2,1)S(1)}, u32[]{:S(2)}, u32[]{:S(2)}) %collective-permute-start.2) | collective-permute-done | bytes 1048608 | tf_op jit(solution)/shard_map/ppermute | solution.py:39
  50.9 0.0 copy-done.1
  50.9 1.4 %shard_map.81 = (bf16[256,2048]{1,0:T(8,128)(2,1)S(1)}, f32[128,1024]{1,0:T(8,128)S(1)}, f32[128,512]{1,0:T(8,128)S(1)}, f32[128,512]{1,0:T(8,128)S(1)}) custom-call(bf16[256,2048]{1,0:T(8,128)(2,1)S(1)} %collective-permute-done.2.recv, bf16[256,2048]{1,0:T(8,128)(2,1)S(1)} %shard_map.78.hand, bf16[1024,2048]{1,0:T(8,128)(2,1)S(1)} %bitcast.8), custom_call_target="tpu_custom_call" | custom-call | flops 1000 | bytes 1000 | tf_op jit(solution)/shard_map/pallas_call | solution.py:22
  52.3 0.0 copy-start.4
  52.3 0.9 copy-done.4
  53.3 0.0 collective-permute-start.4
  53.3 0.5 collective-permute-start.5
  53.8 1.5 %collective-permute-start.3 = (bf16[160,2048]{1,0:T(8,128)(2,1)S(1)}, bf16[160,2048]{1,0:T(8,128)(2,1)S(1)}, u32[]{:S(2)}, u32[]{:S(2)}) collective-permute-start(bf16[160,2048]{1,0:T(8,128)(2,1)S(1)} %get-tuple-element.30.hand), channel_id=1, source_target_pairs={{0,16},{16,0},{1,17},{17,1},{2,18},{18,2},{3,19},{19,3},{4,20},{20... | collective-permute-start | bytes 1966088 | tf_op jit(solution)/shard_map/ppermute | solution.py:39
  55.3 0.0 collective-permute-done.4.rest_1_
  55.3 0.0 collective-permute-done.5.rest_2_
  55.3 0.8 shard_map.82
  56.1 3.4 %all-to-all-start.2 = ((bf16[8,16,1024]{2,1,0:T(8,128)(2,1)}), bf16[8,16,1024]{2,1,0:T(8,128)(2,1)S(1)}, u32[]{:S(2)}, u32[]{:S(2)}) async-start(bf16[8,16,1024]{2,1,0:T(8,128)(2,1)} %shard_map.82), calls=%async_computation.2 | async-start | bytes 524288 | tf_op jit(solution)/shard_map/all_to_all | solution.py:45
  59.5 1.5 %collective-permute-start.6 = (bf16[96,2048]{1,0:T(8,128)(2,1)S(1)}, bf16[96,2048]{1,0:T(8,128)(2,1)S(1)}, u32[]{:S(2)}, u32[]{:S(2)}) collective-permute-start(bf16[96,2048]{1,0:T(8,128)(2,1)S(1)} %get-tuple-element.31.hand), channel_id=1, source_target_pairs={{0,16},{16,0},{1,17},{17,1},{2,18},{18,2},{3,19},{19,3},{4,20},{20... | collective-permute-start | bytes 1179656 | tf_op jit(solution)/shard_map/ppermute | solution.py:39
  61.0 10.4 %collective-permute-done.3.recv = bf16[160,2048]{1,0:T(8,128)(2,1)S(1)} collective-permute-done((bf16[160,2048]{1,0:T(8,128)(2,1)S(1)}, bf16[160,2048]{1,0:T(8,128)(2,1)S(1)}, u32[]{:S(2)}, u32[]{:S(2)}) %collective-permute-start.3) | collective-permute-done | bytes 655392 | tf_op jit(solution)/shard_map/ppermute | solution.py:39
  71.4 0.0 all-to-all-done.2.refs_0_
  71.4 0.0 copy-start.2
  71.4 2.2 %copy-done.2 = bf16[1,1024,2048]{2,1,0:T(8,128)(2,1)S(1)} copy-done((bf16[1,1024,2048]{2,1,0:T(8,128)(2,1)S(1)}, bf16[1,1024,2048]{2,1,0:T(8,128)(2,1)}, u32[]{:S(2)}) %copy-start.2) | copy-done | bytes 4194328
  73.6 1.5 %shard_map.83 = (bf16[160,2048]{1,0:T(8,128)(2,1)S(1)}, f32[128,512]{1,0:T(8,128)S(1)}, f32[128,512]{1,0:T(8,128)S(1)}, f32[32,1024]{1,0:T(8,128)S(1)}) custom-call(bf16[160,2048]{1,0:T(8,128)(2,1)S(1)} %collective-permute-done.3.recv, bf16[160,2048]{1,0:T(8,128)(2,1)S(1)} %get-tuple-element.30.hand, bf16[1024,2048]{1,0:T(8,128)(2,1)S(1)} %bitcast.9), custom_call_target="tpu_custom_call" | custom-call | flops 1000 | bytes 1000 | tf_op jit(solution)/shard_map/pallas_call | solution.py:22
  75.1 0.0 copy-start.5
  75.1 0.8 copy-done.5
  76.0 0.0 collective-permute-start.7
  76.0 0.5 collective-permute-start.8
  76.5 2.4 %collective-permute-done.6.recv = bf16[96,2048]{1,0:T(8,128)(2,1)S(1)} collective-permute-done((bf16[96,2048]{1,0:T(8,128)(2,1)S(1)}, bf16[96,2048]{1,0:T(8,128)(2,1)S(1)}, u32[]{:S(2)}, u32[]{:S(2)}) %collective-permute-start.6) | collective-permute-done | bytes 393248 | tf_op jit(solution)/shard_map/ppermute | solution.py:39
  78.9 0.0 copy-start.7
  78.9 1.4 %shard_map.84 = (bf16[96,2048]{1,0:T(8,128)(2,1)S(1)}, f32[96,1024]{1,0:T(8,128)S(1)}) custom-call(bf16[96,2048]{1,0:T(8,128)(2,1)S(1)} %collective-permute-done.6.recv, bf16[96,2048]{1,0:T(8,128)(2,1)S(1)} %get-tuple-element.31.hand, bf16[1024,2048]{1,0:T(8,128)(2,1)S(1)} %bitcast.10), custom_call_target="tpu_custom_call" | custom-call | flops 1000 | bytes 1000 | tf_op jit(solution)/shard_map/pallas_call | solution.py:22
  80.3 0.0 copy-start.6
  80.3 0.7 copy-done.6
  81.0 0.0 collective-permute-done.7.rest_2_
  81.0 0.0 collective-permute-done.8.rest_3_
  81.0 0.8 shard_map.86
  81.8 3.4 %all-to-all-start.3 = ((bf16[8,16,1024]{2,1,0:T(8,128)(2,1)}), bf16[8,16,1024]{2,1,0:T(8,128)(2,1)S(1)}, u32[]{:S(2)}, u32[]{:S(2)}) async-start(bf16[8,16,1024]{2,1,0:T(8,128)(2,1)} %shard_map.86), calls=%async_computation.3 | async-start | bytes 524288 | tf_op jit(solution)/shard_map/all_to_all | solution.py:45
  85.2 8.8 %shard_map.85 = f32[1024,2048]{1,0:T(8,128)} custom-call(bf16[1024,512]{1,0:T(8,128)(2,1)} %copy-done.3, bf16[256,2048]{1,0:T(8,128)(2,1)} %copy-done.4, bf16[160,2048]{1,0:T(8,128)(2,1)} %copy-done.5, bf16[96,2048]{1,0:T(8,128)(2,1)} %copy-done.6), custom_call_target="tpu_custom_call" | custom-call | flops 2147483648 | bytes 8388608 | tf_op jit(solution)/shard_map/pallas_call | solution.py:325
  94.0 0.0 all-to-all-done.3.refs_1_
  94.0 0.0 copy-done.7
  94.0 0.3 shard_map.87
  94.3 1.6 %collective-permute-start.9 = (bf16[128,512]{1,0:T(8,128)(2,1)S(1)}, bf16[128,512]{1,0:T(8,128)(2,1)S(1)}, u32[]{:S(2)}, u32[]{:S(2)}) collective-permute-start(bf16[128,512]{1,0:T(8,128)(2,1)S(1)} %get-tuple-element.51), channel_id=1, source_target_pairs={{0,16},{16,0},{1,17},{17,1},{2,18},{18,2},{3,19},{19,3},{4,20},{20... | collective-permute-start | bytes 393224 | tf_op jit(solution)/shard_map/ppermute | solution.py:39
  95.9 3.5 %collective-permute-done.9 = bf16[128,512]{1,0:T(8,128)(2,1)S(1)} collective-permute-done((bf16[128,512]{1,0:T(8,128)(2,1)S(1)}, bf16[128,512]{1,0:T(8,128)(2,1)S(1)}, u32[]{:S(2)}, u32[]{:S(2)}) %collective-permute-start.9) | collective-permute-done | bytes 131104 | tf_op jit(solution)/shard_map/ppermute | solution.py:39
  99.3 0.7 broadcast_select_fusion
Async XLA Ops:
  0.6 43.4 %copy-start.8 = (s32[200]{0:T(256)S(1)}, s32[200]{0:T(256)}, u32[]{:S(2)}) copy-start(s32[200]{0:T(256)} %param.10) | copy-start | bytes 2404
  20.6 1.6 %collective-permute-start = (bf16[8,16,1152]{2,1,0:T(8,128)(2,1)S(1)}, bf16[8,16,1152]{2,1,0:T(8,128)(2,1)S(1)}, u32[]{:S(2)}, u32[]{:S(2)}) collective-permute-start(bf16[8,16,1152]{2,1,0:T(8,128)(2,1)S(1)} %all_to_all.20.refs_0_), channel_id=1, source_target_pairs={{0,1},{1,0},{2,3},{3,2},{4,5},{5,4},{6,7},{7,6},{8,9},{9,8},{10,11... | collective-permute-start | bytes 884744 | tf_op jit(solution)/shard_map/ppermute | solution.py:35
  22.2 2.2 %copy-start = (bf16[1,1024,2048]{2,1,0:T(8,128)(2,1)S(1)}, bf16[1,1024,2048]{2,1,0:T(8,128)(2,1)}, u32[]{:S(2)}) copy-start(bf16[1,1024,2048]{2,1,0:T(8,128)(2,1)} %param.11) | copy-start | bytes 12582916
  24.4 26.6 %copy-start.1 = (bf16[1,1024,2048]{2,1,0:T(8,128)(2,1)S(1)}, bf16[1,1024,2048]{2,1,0:T(8,128)(2,1)}, u32[]{:S(2)}) copy-start(bf16[1,1024,2048]{2,1,0:T(8,128)(2,1)} %param.11) | copy-start | bytes 12582916
  25.7 25.3 %collective-permute-start.2 = (bf16[256,2048]{1,0:T(8,128)(2,1)S(1)}, bf16[256,2048]{1,0:T(8,128)(2,1)S(1)}, u32[]{:S(2)}, u32[]{:S(2)}) collective-permute-start(bf16[256,2048]{1,0:T(8,128)(2,1)S(1)} %shard_map.78.hand), channel_id=1, source_target_pairs={{0,16},{16,0},{1,17},{17,1},{2,18},{18,2},{3,19},{19,3},{4,20},{20... | collective-permute-start | bytes 3145736 | tf_op jit(solution)/shard_map/ppermute | solution.py:39
  41.2 1.6 %collective-permute-start.1 = (bf16[8,16,1152]{2,1,0:T(8,128)(2,1)S(1)}, bf16[8,16,1152]{2,1,0:T(8,128)(2,1)S(1)}, u32[]{:S(2)}, u32[]{:S(2)}) collective-permute-start(bf16[8,16,1152]{2,1,0:T(8,128)(2,1)S(1)} %all_to_all.21.refs_0_.refs_2_), channel_id=1, source_target_pairs={{0,1},{1,0},{2,3},{3,2},{4,5},{5,4},{6,7},{7,6},{8,9},{9,8},{10,11... | collective-permute-start | bytes 884744 | tf_op jit(solution)/shard_map/ppermute | solution.py:35
  46.9 1.0 copy-start.3
  52.3 1.0 copy-start.4
  53.3 2.0 %collective-permute-start.4 = (f32[128,512]{1,0:T(8,128)S(1)}, f32[128,512]{1,0:T(8,128)S(1)}, u32[]{:S(2)}, u32[]{:S(2)}) collective-permute-start(f32[128,512]{1,0:T(8,128)S(1)} %get-tuple-element.38), channel_id=1, source_target_pairs={{0,1},{1,0},{2,3},{3,2},{4,5},{5,4},{6,7},{7,6},{8,9},{9,8},{10,11... | collective-permute-start | bytes 786440 | tf_op jit(solution)/shard_map/ppermute | solution.py:35
  53.3 2.0 %collective-permute-start.5 = (f32[128,512]{1,0:T(8,128)S(1)}, f32[128,512]{1,0:T(8,128)S(1)}, u32[]{:S(2)}, u32[]{:S(2)}) collective-permute-start(f32[128,512]{1,0:T(8,128)S(1)} %get-tuple-element.39), channel_id=1, source_target_pairs={{0,1},{1,0},{2,3},{3,2},{4,5},{5,4},{6,7},{7,6},{8,9},{9,8},{10,11... | collective-permute-start | bytes 786440 | tf_op jit(solution)/shard_map/ppermute | solution.py:35
  53.8 17.6 %collective-permute-start.3 = (bf16[160,2048]{1,0:T(8,128)(2,1)S(1)}, bf16[160,2048]{1,0:T(8,128)(2,1)S(1)}, u32[]{:S(2)}, u32[]{:S(2)}) collective-permute-start(bf16[160,2048]{1,0:T(8,128)(2,1)S(1)} %get-tuple-element.30.hand), channel_id=1, source_target_pairs={{0,16},{16,0},{1,17},{17,1},{2,18},{18,2},{3,19},{19,3},{4,20},{20... | collective-permute-start | bytes 1966088 | tf_op jit(solution)/shard_map/ppermute | solution.py:39
  56.1 15.3 %all-to-all-start.2 = ((bf16[8,16,1024]{2,1,0:T(8,128)(2,1)}), bf16[8,16,1024]{2,1,0:T(8,128)(2,1)S(1)}, u32[]{:S(2)}, u32[]{:S(2)}) async-start(bf16[8,16,1024]{2,1,0:T(8,128)(2,1)} %shard_map.82), calls=%async_computation.2 | async-start | bytes 524288 | tf_op jit(solution)/shard_map/all_to_all | solution.py:45
  59.5 19.3 %collective-permute-start.6 = (bf16[96,2048]{1,0:T(8,128)(2,1)S(1)}, bf16[96,2048]{1,0:T(8,128)(2,1)S(1)}, u32[]{:S(2)}, u32[]{:S(2)}) collective-permute-start(bf16[96,2048]{1,0:T(8,128)(2,1)S(1)} %get-tuple-element.31.hand), channel_id=1, source_target_pairs={{0,16},{16,0},{1,17},{17,1},{2,18},{18,2},{3,19},{19,3},{4,20},{20... | collective-permute-start | bytes 1179656 | tf_op jit(solution)/shard_map/ppermute | solution.py:39
  71.4 2.2 %copy-start.2 = (bf16[1,1024,2048]{2,1,0:T(8,128)(2,1)S(1)}, bf16[1,1024,2048]{2,1,0:T(8,128)(2,1)}, u32[]{:S(2)}) copy-start(bf16[1,1024,2048]{2,1,0:T(8,128)(2,1)} %param.11) | copy-start | bytes 12582916
  75.1 0.8 copy-start.5
  76.0 5.1 %collective-permute-start.7 = (f32[128,512]{1,0:T(8,128)S(1)}, f32[128,512]{1,0:T(8,128)S(1)}, u32[]{:S(2)}, u32[]{:S(2)}) collective-permute-start(f32[128,512]{1,0:T(8,128)S(1)} %get-tuple-element.48), channel_id=1, source_target_pairs={{0,1},{1,0},{2,3},{3,2},{4,5},{5,4},{6,7},{7,6},{8,9},{9,8},{10,11... | collective-permute-start | bytes 786440 | tf_op jit(solution)/shard_map/ppermute | solution.py:35
  76.0 5.1 %collective-permute-start.8 = (f32[128,512]{1,0:T(8,128)S(1)}, f32[128,512]{1,0:T(8,128)S(1)}, u32[]{:S(2)}, u32[]{:S(2)}) collective-permute-start(f32[128,512]{1,0:T(8,128)S(1)} %get-tuple-element.49), channel_id=1, source_target_pairs={{0,1},{1,0},{2,3},{3,2},{4,5},{5,4},{6,7},{7,6},{8,9},{9,8},{10,11... | collective-permute-start | bytes 786440 | tf_op jit(solution)/shard_map/ppermute | solution.py:35
  78.9 15.2 %copy-start.7 = (s32[8,128]{1,0:T(8,128)S(1)}, s32[8,128]{1,0:T(8,128)}, u32[]{:S(2)}) copy-start(s32[8,128]{1,0:T(8,128)} %get-tuple-element.45.info) | copy-start | bytes 12292
  80.3 0.7 copy-start.6
  81.8 12.2 %all-to-all-start.3 = ((bf16[8,16,1024]{2,1,0:T(8,128)(2,1)}), bf16[8,16,1024]{2,1,0:T(8,128)(2,1)S(1)}, u32[]{:S(2)}, u32[]{:S(2)}) async-start(bf16[8,16,1024]{2,1,0:T(8,128)(2,1)} %shard_map.86), calls=%async_computation.3 | async-start | bytes 524288 | tf_op jit(solution)/shard_map/all_to_all | solution.py:45
  94.3 5.0 %collective-permute-start.9 = (bf16[128,512]{1,0:T(8,128)(2,1)S(1)}, bf16[128,512]{1,0:T(8,128)(2,1)S(1)}, u32[]{:S(2)}, u32[]{:S(2)}) collective-permute-start(bf16[128,512]{1,0:T(8,128)(2,1)S(1)} %get-tuple-element.51), channel_id=1, source_target_pairs={{0,16},{16,0},{1,17},{17,1},{2,18},{18,2},{3,19},{19,3},{4,20},{20... | collective-permute-start | bytes 393224 | tf_op jit(solution)/shard_map/ppermute | solution.py:39

commit v5 on v4

--- a/solution.py
+++ b/solution.py
@@ -18,14 +18,18 @@
     return jax.ShapeDtypeStruct(shape, dtype)
 
 
-def call(kernel, outs, *args, scratch=(), limit=8, spec=VMEM):
+def call(kernel, outs, *args, scratch=(), spec=VMEM, out_spaces=None):
     return pl.pallas_call(
         kernel,
         out_shape=outs,
-        in_specs=[spec] * len(args),
-        out_specs=jax.tree.map(lambda _: VMEM, outs),
+        in_specs=spec if isinstance(spec, list) else [spec] * len(args),
+        out_specs=(
+            tuple(pl.BlockSpec(memory_space=space) for space in out_spaces)
+            if out_spaces
+            else jax.tree.map(lambda _: VMEM, outs)
+        ),
         scratch_shapes=list(scratch),
-        compiler_params=pltpu.CompilerParams(vmem_limit_bytes=limit << 20),
+        compiler_params=pltpu.CompilerParams(vmem_limit_bytes=12 << 20),
         cost_estimate=pl.CostEstimate(flops=1000, bytes_accessed=1000, transcendentals=0),
     )(*args)
 
@@ -56,14 +60,14 @@
 
 
 def place_kernel(*refs):
-    inputs, (*packed, info), copies = refs[:4], refs[4:-5], refs[-5:]
+    inputs, (*packed, info, weight), copies = refs[:5], refs[5:-5], refs[-5:]
     moves = [
         pltpu.make_async_copy(src, dst, copies[4].at[i])
-        for i, (src, dst) in enumerate(zip(inputs, copies))
+        for i, (src, dst) in enumerate(zip(inputs, (*copies[:4], weight)))
     ]
     for move in moves:
         move.start()
-    for move in moves:
+    for move in moves[:4]:
         move.wait()
     ids, table, counts, rows = copies[:4]
     chips, part, _ = packed[0].shape
@@ -106,6 +110,7 @@
         moved, notes = slots(target, chips * part, p == 0)
         out[:, :, :width] = moved.reshape(chips, part, width)
         out[:, :, width:] = notes.reshape(chips, part, NOTES)
+    moves[4].wait()
 
 
 def load_piece(inputs, piece):
@@ -172,32 +177,78 @@
             first += hand.shape[0]
 
 
-def stack_kernel(first, count, scale, *rest):
-    mine, theirs, out = rest[:count], rest[count:-1], rest[-1]
+def give(first, scale, total, out):
     chip = lax.axis_index("dp") // 2
     chips, part, _ = out.shape
-    total = jnp.concatenate([m[...] for m in mine], axis=0)
-    total = total + jnp.concatenate([t[...] for t in theirs], axis=1)
     total = (total * scale[first : first + part * chips, :]).astype(BF16)
     for rel in range(chips):
         out[chip ^ rel] = total[rel * part : (rel + 1) * part]
 
 
-def back_kernel(recv, hand, weight, partner, *outs):
+def stack_kernel(first, scale, mine, left, right, out):
+    theirs = jnp.concatenate([left[...], right[...]], axis=1)
+    give(first, scale, mine[...] + theirs.astype(F32), out)
+
+
+def mask_and_leave(recv, hand, value, partner, done):
     is_up = lax.axis_index("section") == 0
     masked = is_up & (hand[...] <= 0)
-    value = jnp.where(masked, jnp.zeros_like(recv), recv[...])
-    partner[...] = value
-    product = lax.dot_general(
-        value, weight[...], (((1,), (1,)), ((), ())), preferred_element_type=F32
-    )
-    first = 0
-    column = 0
-    for out in outs:
-        size, columns = out.shape
-        out[...] = product[first : first + size, column : column + columns]
-        column = (column + columns) % product.shape[1]
-        first += size if column == 0 else 0
+    value[...] = jnp.where(masked, jnp.zeros_like(recv), recv[...])
+    leave = pltpu.make_async_copy(value, partner, done)
+    leave.start()
+    return leave
+
+
+def product_of(value, weight):
+    return lax.dot_general(value, weight, (((1,), (1,)), ((), ())), preferred_element_type=F32)
+
+
+def spread(product, theirs_first, mine, left, right):
+    count, columns = left.shape
+    theirs = 0 if theirs_first else mine.shape[0]
+    left[...] = product[theirs : theirs + count, :columns].astype(BF16)
+    right[...] = product[theirs : theirs + count, columns:].astype(BF16)
+    own = count if theirs_first else 0
+    mine[...] = product[own : own + mine.shape[0]]
+
+
+def back_kernel(recv, hand, weight, partner, mine, left, right, value, done):
+    leave = mask_and_leave(recv, hand, value, partner, done)
+    spread(product_of(value[...], weight[...]), False, mine, left, right)
+    leave.wait()
+
+
+def fetch_kernel(recv, hand, weight, partner, mine, left, right, value, done, kept, came):
+    tile = weight.shape[1] // 4
+    cuts = [slice(i * tile, (i + 1) * tile) for i in range(4)]
+    moves = [
+        pltpu.make_async_copy(weight.at[:, cut], kept.at[:, cut], came.at[i])
+        for i, cut in enumerate(cuts)
+    ]
+    for move in moves:
+        move.start()
+    leave = mask_and_leave(recv, hand, value, partner, done)
+    product = 0.0
+    for move, cut in zip(moves, cuts):
+        move.wait()
+        product = product + product_of(value[:, cut], kept[:, cut])
+    spread(product, True, mine, left, right)
+    leave.wait()
+
+
+def keep_kernel(weight, token, kept, done):
+    move = pltpu.make_async_copy(weight, kept, done)
+    move.start()
+    move.wait()
+
+
+def last_kernel(first, recv, hand, weight, scale, mine, left, right, partner, out, value, done):
+    leave = mask_and_leave(recv, hand, value, partner, done)
+    product = product_of(value[...], weight[...])
+    theirs = jnp.concatenate([left[...], right[...]], axis=1)
+    total = jnp.concatenate([mine[...], product], axis=0) + theirs.astype(F32)
+    give(first, scale, total, out)
+    leave.wait()
 
 
 def weight_kernel(turned, *refs):
@@ -206,17 +257,25 @@
     out[...] = jnp.dot(turned[...], rhs, preferred_element_type=F32)
 
 
-def final_kernel(info, *refs):
-    backs, left, right = refs[:-2], refs[-2], refs[-1]
+def unpack(half, info, back):
     slot, block = info[0:1, :], info[1:2, :]
-    rows_dev = slot.shape[1]
-    chips, part, _ = backs[0].shape
-    target = (slot // part) * (chips * part) + block * part + slot % part
-    values = jnp.concatenate([b[...].reshape(chips * part, -1) for b in backs], axis=0)
-    hot = (iota((values.shape[0], rows_dev), 0) == target).astype(F32).astype(BF16)
-    rows = lax.dot_general(
-        hot, values, (((0,), (0,)), ((), ())), preferred_element_type=F32
-    ).astype(BF16)
+    chips, part, width = back.shape
+    target = jnp.where(slot // part == half, block * part + slot % part, -1)
+    hot = (iota((chips * part, target.shape[1]), 0) == target).astype(F32).astype(BF16)
+    return lax.dot_general(
+        hot,
+        back[...].reshape(chips * part, width),
+        (((0,), (0,)), ((), ())),
+        preferred_element_type=F32,
+    )
+
+
+def unpack_kernel(info, back, out):
+    out[...] = unpack(0, info, back).astype(BF16)
+
+
+def final_kernel(info, back, early, left, right):
+    rows = (unpack(1, info, back) + early[...].astype(F32)).astype(BF16)
     half = left.shape[1]
     left[...] = rows[:, :half]
     right[...] = rows[:, half:]
@@ -236,25 +295,31 @@
     part = cap // halves
     wide = width + NOTES
 
-    *packed, info = call(
+    *packed, info, fast_weight = call(
         place_kernel,
         (
             *(sds((chips, part, wide), BF16) for _ in range(halves)),
             sds((8, rows_dev), I32),
+            pltpu.VMEM(own_weight.shape, BF16),
         ),
-        lang_ids.reshape(1, -1),
-        lang_table.reshape(1, -1),
-        lang_counts,
-        section_rows[0],
+        *(
+            pltpu.with_memory_space_constraint(value, pltpu.HBM)
+            for value in (
+                lang_ids.reshape(1, -1),
+                lang_table.reshape(1, -1),
+                lang_counts,
+                section_rows[0],
+                own_weight,
+            )
+        ),
         scratch=[
             pltpu.VMEM((1, rows_dev), I32),
             pltpu.VMEM((1, lang_table.shape[0]), I32),
             pltpu.VMEM(lang_counts.shape, I32),
             pltpu.VMEM((rows_dev, width), BF16),
-            pltpu.SemaphoreType.DMA((4,)),
+            pltpu.SemaphoreType.DMA((5,)),
         ],
         spec=pl.BlockSpec(memory_space=pltpu.HBM),
-        limit=60,
     )
 
     hands, received, partners = [], [], []
@@ -265,23 +330,11 @@
             functools.partial(product_kernel, len(inputs), pieces),
             tuple(sds((size, ff_dev), BF16) for size in sizes),
             *inputs,
-            own_weight,
+            fast_weight,
             scratch=[pltpu.VMEM((count, width), BF16)],
         )
         hands.append(hand)
         received.append(across(hand))
-
-    def back_product(g, which, shapes, *earlier):
-        rows = hands[g][which].shape[0]
-        partner, *outs = call(
-            back_kernel,
-            (sds((rows, ff_dev), BF16), *(sds(shape, F32) for shape in shapes)),
-            after(received[g][which], *earlier),
-            hands[g][which],
-            own_weight,
-        )
-        partners.append(partner)
-        return outs
 
     came, chunks = [], []
     for p in range(halves):
@@ -301,26 +354,78 @@
         *came,
         scratch=[pltpu.VMEM((total_rows, width), BF16)],
     )
-    def stacked(first, mine, theirs):
-        return call(
-            functools.partial(stack_kernel, first, len(mine)),
-            sds((chips, part, width), BF16),
+    count = rows // 2
+    half = sds((count, width // 2), BF16)
+    late_rows = [hand.shape[0] for hand in hands[1]]
+
+    def room(size):
+        return [pltpu.VMEM((size, ff_dev), BF16), pltpu.SemaphoreType.DMA]
+
+    def backed(kernel, size, outs, args, scratch=(), specs=VMEM):
+        partner, *rest = call(
+            kernel,
+            (pltpu.HBM((size, ff_dev), BF16), *outs),
+            *args,
+            scratch=[*room(size), *scratch],
+            out_spaces=(pltpu.HBM, *(pltpu.VMEM for _ in outs)),
+            spec=specs,
+        )
+        partners.append(partner)
+        return rest
+
+    mine, left, right = backed(
+        back_kernel,
+        rows,
+        [sds((count, width), F32), half, half],
+        [after(received[0][0], scale, *hands[1]), hands[0][0], fast_weight],
+    )
+    stack = call(
+        functools.partial(stack_kernel, 0),
+        sds((chips, part, width), BF16),
+        scale,
+        mine,
+        sibling(left),
+        sibling(right),
+    )
+    early = call(
+        unpack_kernel,
+        sds((rows_dev, width), BF16),
+        info,
+        same_core_exchange(stack),
+    )
+    far_weight = pltpu.with_memory_space_constraint(own_weight, pltpu.HBM)
+    in_hbm = pl.BlockSpec(memory_space=pltpu.HBM)
+    mine, left, right = backed(
+        fetch_kernel,
+        late_rows[0],
+        [sds((late_rows[0] - count, width), F32), half, half],
+        [after(received[1][0], partners[0], stack), hands[1][0], far_weight],
+        scratch=[pltpu.VMEM(own_weight.shape, BF16), pltpu.SemaphoreType.DMA((4,))],
+        specs=[VMEM, VMEM, in_hbm],
+    )
+    (kept,) = call(
+        keep_kernel,
+        (pltpu.VMEM(own_weight.shape, BF16),),
+        far_weight,
+        after(info, early, mine),
+        scratch=[pltpu.SemaphoreType.DMA],
+        spec=[in_hbm, VMEM],
+    )
+    (stack,) = backed(
+        functools.partial(last_kernel, rows + count),
+        late_rows[1],
+        [sds((chips, part, width), BF16)],
+        [
+            after(received[1][1], partners[1], kept),
+            hands[1][1],
+            kept,
             scale,
-            *mine,
-            *theirs,
-        )
-
-    count = rows // 2
-    half = (count, width // 2)
-    mine, *theirs = back_product(0, 0, [(count, width), half, half], scale, *hands[1])
-    stack = stacked(0, [mine], [sibling(t) for t in theirs])
-    back = [same_core_exchange(stack)]
-    *theirs, first = back_product(
-        1, 0, [half, half, (count // 4, width)], partners[0], back[0]
-    )
-    theirs = [sibling(t) for t in theirs]
-    (second,) = back_product(1, 1, [(3 * count // 4, width)], partners[1])
-    back.append(same_core_exchange(stacked(rows + count, [first, second], theirs)))
+            mine,
+            sibling(left),
+            sibling(right),
+        ],
+    )
+    late = same_core_exchange(stack)
     tile = 256
     weight_grad = pl.pallas_call(
         weight_kernel,
@@ -341,7 +446,8 @@
         final_kernel,
         (sds((rows_dev, width // 2), BF16),) * 2,
         info,
-        *back,
+        late,
+        early,
     )
     (right_cols,) = across([right])
     input_grad = jnp.where(is_up, left, right_cols)

time: 101 us -> 92.6 us (0.917)
  local copies, waits for them, and re-layouts: 7.89 us -> 0.01 us
  Pallas kernels: 22.7 us -> 28.3 us
  waiting for transfers between devices: 22.5 us -> 18.5 us
  blocking collectives: 31.6 us -> 30.4 us
    unnamed x18 -> x4, local copies, waits for them, and re-layouts: 7.89 us -> 0.01 us
    pallas_call x10 -> x11, Pallas kernels: 13.9 us -> 19.5 us  [call(): pl.pallas_call(kernel, out_shape=outs, in_specs=spec if isinstance(spec,...]
    ppermute x4, waiting for transfers between devices: 19.3 us -> 14.3 us  [across(): lax.ppermute(value, 'section', [(0, 1), (1, 0)])]
    all_to_all x2, blocking collectives: 31.6 us -> 30.4 us  [same_core_exchange(): lax.all_to_all(value, 'dp', split_axis=0, concat_axis=0, axis_index_group...]
    ppermute x6, waiting for transfers between devices: 3.17 us -> 4.19 us  [sibling(): return lax.ppermute(value, 'dp', [(i, i ^ 1) for i in range(count)])]
  transfers between devices with their start and end apart: 12 -> 12, of which waited for: 6 -> 8; matrix products, arithmetic and copies ran while one was open for 0% -> 0% of each run, Pallas kernels for 17% -> 24%
where the time goes in v5:
time: 92.6 us; the launch traced here: 91.9 us
  blocking collectives  30.4 us (33%)
  Pallas kernels  28.3 us (31%)
  waiting for transfers between devices  18.5 us (20%)
  starting transfers between devices  13.2 us (14%)
    all_to_all x2, blocking collectives, same_core_exchange(): lax.all_to_all(value, 'dp', split_axis=0, concat_axis=0, axis_index_group...  30.4 us
    pallas_call x11, Pallas kernels, call(): pl.pallas_call(kernel, out_shape=outs, in_specs=spec if isinstance(spec,...  19.5 us
    ppermute x4, waiting for transfers between devices, across(): lax.ppermute(value, 'section', [(0, 1), (1, 0)])  14.3 us
    pallas_call x1, Pallas kernels, on_device(): pl.pallas_call(weight_kernel, out_shape=sds((width, ff_dev), F32), grid=(...  8.8 us
    all_to_all x2, starting transfers between devices, same_core_exchange(): lax.all_to_all(value, 'dp', split_axis=0, concat_axis=0, axis_index_group...  6.83 us
    ppermute x4, starting transfers between devices, across(): lax.ppermute(value, 'section', [(0, 1), (1, 0)])  5.26 us
    ppermute x6, waiting for transfers between devices, sibling(): return lax.ppermute(value, 'dp', [(i, i ^ 1) for i in range(count)])  4.19 us
  transfers between devices with their start and end apart: 12, of which 8 were waited for; matrix products, arithmetic and copies ran while one was open for 0% of the time, Pallas kernels for 24%

profile of v5, /device:TPU:0, one launch (start us, length us, event | category | flops | bytes accessed | tf_op | source)
XLA Modules:
  0.0 91.9 jit_solution(700618726702021776)
XLA Ops:
  0.6 2.4 %shard_map.77 = (bf16[8,16,1152]{2,1,0:T(8,128)(2,1)S(1)}, bf16[8,16,1152]{2,1,0:T(8,128)(2,1)S(1)}, s32[8,128]{1,0:T(8,128)S(1)}, bf16[1024,2048]{1,0:T(8,128)(2,1)S(1)}) custom-call(s32[1,128]{1,0:T(1,128)} %bitcast.13, s32[1,200]{1,0:T(1,128)} %bitcast.12, s32[1,200]{1,0:T(1,128)} %refs_2_.1, bf16[128,1024]{1,0:T(8,128)(2,1)} %bitcast.11, ...), custom_call_target="tpu_custom_call" | custom-call | flops 1000 | bytes 1000 | tf_op jit(solution)/shard_map/pallas_call | solution.py:22
  3.0 17.4 %all_to_all.20.refs_0_ = bf16[8,16,1152]{2,1,0:T(8,128)(2,1)S(1)} all-to-all(bf16[8,16,1152]{2,1,0:T(8,128)(2,1)S(1)} %get-tuple-element.30), channel_id=1, replica_groups={{0,2,4,6,8,10,12,14},{1,3,5,7,9,11,13,15},{16,18,20,22,24,26,28,30},{17..., dimensions={0} | all-to-all | bytes 589824 | tf_op jit(solution)/shard_map/all_to_all | solution.py:49
  20.4 0.0 collective-permute-start
  20.4 1.6 %collective-permute-done.refs_1_ = bf16[8,16,1152]{2,1,0:T(8,128)(2,1)S(1)} collective-permute-done((bf16[8,16,1152]{2,1,0:T(8,128)(2,1)S(1)}, bf16[8,16,1152]{2,1,0:T(8,128)(2,1)S(1)}, u32[]{:S(2)}, u32[]{:S(2)}) %collective-permute-start) | collective-permute-done | bytes 294944 | tf_op jit(solution)/shard_map/ppermute | solution.py:39
  22.0 0.0 copy-start.1
  22.0 1.3 %shard_map.78.hand = bf16[256,2048]{1,0:T(8,128)(2,1)S(1)} custom-call(bf16[8,16,1152]{2,1,0:T(8,128)(2,1)S(1)} %all_to_all.20.refs_0_, bf16[8,16,1152]{2,1,0:T(8,128)(2,1)S(1)} %collective-permute-done.refs_1_, bf16[1024,2048]{1,0:T(8,128)(2,1)S(1)} %get-tuple-element.31.refs_2_.weight), custom_call_target="tpu_custom_call" | custom-call | flops 1000 | bytes 1000 | tf_op jit(solution)/shard_map/pallas_call | solution.py:22
  23.3 1.6 %collective-permute-start.2 = (bf16[256,2048]{1,0:T(8,128)(2,1)S(1)}, bf16[256,2048]{1,0:T(8,128)(2,1)S(1)}, u32[]{:S(2)}, u32[]{:S(2)}) collective-permute-start(bf16[256,2048]{1,0:T(8,128)(2,1)S(1)} %shard_map.78.hand), channel_id=1, source_target_pairs={{0,16},{16,0},{1,17},{17,1},{2,18},{18,2},{3,19},{19,3},{4,20},{20... | collective-permute-start | bytes 3145736 | tf_op jit(solution)/shard_map/ppermute | solution.py:43
  24.9 13.0 %all_to_all.21.refs_0_.refs_2_ = bf16[8,16,1152]{2,1,0:T(8,128)(2,1)S(1)} all-to-all(bf16[8,16,1152]{2,1,0:T(8,128)(2,1)S(1)} %get-tuple-element.32), channel_id=1, replica_groups={{0,2,4,6,8,10,12,14},{1,3,5,7,9,11,13,15},{16,18,20,22,24,26,28,30},{17..., dimensions={0} | all-to-all | bytes 589824 | tf_op jit(solution)/shard_map/all_to_all | solution.py:49
  37.9 0.0 collective-permute-start.1
  37.9 1.6 %collective-permute-done.1.refs_1_.refs_3_ = bf16[8,16,1152]{2,1,0:T(8,128)(2,1)S(1)} collective-permute-done((bf16[8,16,1152]{2,1,0:T(8,128)(2,1)S(1)}, bf16[8,16,1152]{2,1,0:T(8,128)(2,1)S(1)}, u32[]{:S(2)}, u32[]{:S(2)}) %collective-permute-start.1) | collective-permute-done | bytes 294944 | tf_op jit(solution)/shard_map/ppermute | solution.py:39
  39.4 1.3 %shard_map.79 = (bf16[160,2048]{1,0:T(8,128)(2,1)S(1)}, bf16[96,2048]{1,0:T(8,128)(2,1)S(1)}) custom-call(bf16[8,16,1152]{2,1,0:T(8,128)(2,1)S(1)} %all_to_all.21.refs_0_.refs_2_, bf16[8,16,1152]{2,1,0:T(8,128)(2,1)S(1)} %collective-permute-done.1.refs_1_.refs_3_, bf16[1024,2048]{1,0:T(8,128)(2,1)S(1)} %get-tuple-element.31.refs_2_.weight), custom_call_target="tpu_custom_call" | custom-call | flops 1000 | bytes 1000 | tf_op jit(solution)/shard_map/pallas_call | solution.py:22
  40.7 0.6 collective-permute-start.3
  41.3 0.0 copy-done.1
  41.3 2.9 %shard_map.80 = (f32[512,1]{1,0:T(8,128)S(1)}, bf16[1024,512]{1,0:T(8,128)(2,1)S(1)}) custom-call(s32[1,200]{1,0:T(1,128)S(1)} %bitcast.6, bf16[8,16,1152]{2,1,0:T(8,128)(2,1)S(1)} %all_to_all.20.refs_0_, bf16[8,16,1152]{2,1,0:T(8,128)(2,1)S(1)} %collective-permute-done.refs_1_, bf16[8,16,1152]{2,1,0:T(8,128)(2,1)S(1)} %all_to_all.21.refs_0_.refs_2_, ...), custom_call_target="tpu_custom_call" | custom-call | flops 1000 | bytes 1000 | tf_op jit(solution)/shard_map/pallas_call | solution.py:22
  44.2 0.0 copy-start
  44.2 5.2 %collective-permute-done.2.recv = bf16[256,2048]{1,0:T(8,128)(2,1)S(1)} collective-permute-done((bf16[256,2048]{1,0:T(8,128)(2,1)S(1)}, bf16[256,2048]{1,0:T(8,128)(2,1)S(1)}, u32[]{:S(2)}, u32[]{:S(2)}) %collective-permute-start.2) | collective-permute-done | bytes 1048608 | tf_op jit(solution)/shard_map/ppermute | solution.py:43
  49.4 2.1 %shard_map.81 = (bf16[256,2048]{1,0:T(8,128)(2,1)}, f32[128,1024]{1,0:T(8,128)S(1)}, bf16[128,512]{1,0:T(8,128)(2,1)S(1)}, bf16[128,512]{1,0:T(8,128)(2,1)S(1)}) custom-call(bf16[256,2048]{1,0:T(8,128)(2,1)S(1)} %collective-permute-done.2.recv, bf16[256,2048]{1,0:T(8,128)(2,1)S(1)} %shard_map.78.hand, bf16[1024,2048]{1,0:T(8,128)(2,1)S(1)} %get-tuple-element.31.refs_2_.weight), custom_call_target="tpu_custom_call" | custom-call | flops 1000 | bytes 1000 | tf_op jit(solution)/shard_map/pallas_call | solution.py:22
  51.4 0.0 copy-done
  51.5 0.1 collective-permute-start.4
  51.5 0.5 collective-permute-start.5
  52.0 0.8 collective-permute-done.4.left
  52.9 0.2 collective-permute-done.5.right
  53.1 0.8 shard_map.82
  53.9 3.4 %all-to-all-start.2 = ((bf16[8,16,1024]{2,1,0:T(8,128)(2,1)}), bf16[8,16,1024]{2,1,0:T(8,128)(2,1)S(1)}, u32[]{:S(2)}, u32[]{:S(2)}) async-start(bf16[8,16,1024]{2,1,0:T(8,128)(2,1)} %shard_map.82), calls=%async_computation.2 | async-start | bytes 524288 | tf_op jit(solution)/shard_map/all_to_all | solution.py:49
  57.3 1.5 %collective-permute-start.6 = (bf16[96,2048]{1,0:T(8,128)(2,1)S(1)}, bf16[96,2048]{1,0:T(8,128)(2,1)S(1)}, u32[]{:S(2)}, u32[]{:S(2)}) collective-permute-start(bf16[96,2048]{1,0:T(8,128)(2,1)S(1)} %get-tuple-element.34.hand), channel_id=1, source_target_pairs={{0,16},{16,0},{1,17},{17,1},{2,18},{18,2},{3,19},{19,3},{4,20},{20... | collective-permute-start | bytes 1179656 | tf_op jit(solution)/shard_map/ppermute | solution.py:43
  58.8 4.6 %collective-permute-done.3.recv = bf16[160,2048]{1,0:T(8,128)(2,1)S(1)} collective-permute-done((bf16[160,2048]{1,0:T(8,128)(2,1)S(1)}, bf16[160,2048]{1,0:T(8,128)(2,1)S(1)}, u32[]{:S(2)}, u32[]{:S(2)}) %collective-permute-start.3) | collective-permute-done | bytes 655392 | tf_op jit(solution)/shard_map/ppermute | solution.py:43
  63.4 3.4 %shard_map.83 = (bf16[160,2048]{1,0:T(8,128)(2,1)}, f32[32,1024]{1,0:T(8,128)S(1)}, bf16[128,512]{1,0:T(8,128)(2,1)S(1)}, bf16[128,512]{1,0:T(8,128)(2,1)S(1)}) custom-call(bf16[160,2048]{1,0:T(8,128)(2,1)S(1)} %collective-permute-done.3.recv, bf16[160,2048]{1,0:T(8,128)(2,1)S(1)} %get-tuple-element.33.hand, bf16[1024,2048]{1,0:T(8,128)(2,1)} %bitcast.8), custom_call_target="tpu_custom_call" | custom-call | flops 1000 | bytes 1000 | tf_op jit(solution)/shard_map/pallas_call | solution.py:22
  66.9 0.1 collective-permute-start.7
  66.9 0.5 collective-permute-start.8
  67.4 0.0 all-to-all-done.2.back
  67.4 0.3 shard_map.84.early
  67.7 2.2 %shard_map.85.weight = bf16[1024,2048]{1,0:T(8,128)(2,1)S(1)} custom-call(bf16[1024,2048]{1,0:T(8,128)(2,1)} %bitcast.9, s32[8,128]{1,0:T(8,128)S(1)} %get-tuple-element.52.info.token), custom_call_target="tpu_custom_call" | custom-call | flops 1000 | bytes 1000 | tf_op jit(solution)/shard_map/pallas_call | solution.py:22
  69.9 1.1 %collective-permute-done.6.recv = bf16[96,2048]{1,0:T(8,128)(2,1)S(1)} collective-permute-done((bf16[96,2048]{1,0:T(8,128)(2,1)S(1)}, bf16[96,2048]{1,0:T(8,128)(2,1)S(1)}, u32[]{:S(2)}, u32[]{:S(2)}) %collective-permute-start.6) | collective-permute-done | bytes 393248 | tf_op jit(solution)/shard_map/ppermute | solution.py:43
  71.0 0.0 collective-permute-done.7.left
  71.0 0.0 collective-permute-done.8.right
  71.0 2.7 %shard_map.86 = (bf16[96,2048]{1,0:T(8,128)(2,1)}, bf16[8,16,1024]{2,1,0:T(8,128)(2,1)}) custom-call(bf16[96,2048]{1,0:T(8,128)(2,1)S(1)} %collective-permute-done.6.recv, bf16[96,2048]{1,0:T(8,128)(2,1)S(1)} %get-tuple-element.34.hand, bf16[1024,2048]{1,0:T(8,128)(2,1)S(1)} %shard_map.85.weight, f32[512,1]{1,0:T(8,128)S(1)} %get-tuple-element.37.scale, ...), custom_call_target="tpu_custom_call" | custom-call | flops 1000 | bytes 1000 | tf_op jit(solution)/shard_map/pallas_call | solution.py:22
  73.7 3.4 %all-to-all-start.3 = ((bf16[8,16,1024]{2,1,0:T(8,128)(2,1)}), bf16[8,16,1024]{2,1,0:T(8,128)(2,1)S(1)}, u32[]{:S(2)}, u32[]{:S(2)}) async-start(bf16[8,16,1024]{2,1,0:T(8,128)(2,1)} %get-tuple-element.53), calls=%async_computation.3 | async-start | bytes 524288 | tf_op jit(solution)/shard_map/all_to_all | solution.py:49
  77.2 8.8 %shard_map.87 = f32[1024,2048]{1,0:T(8,128)} custom-call(bf16[1024,512]{1,0:T(8,128)(2,1)} %copy-done, bf16[256,2048]{1,0:T(8,128)(2,1)} %get-tuple-element.39.refs_0_, bf16[160,2048]{1,0:T(8,128)(2,1)} %get-tuple-element.44.refs_1_, bf16[96,2048]{1,0:T(8,128)(2,1)} %get-tuple-element.51.refs_2_), custom_call_target="tpu_custom_call" | custom-call | flops 2147483648 | bytes 8388608 | tf_op jit(solution)/shard_map/pallas_call | solution.py:430
  86.0 0.0 all-to-all-done.3.back
  86.0 0.3 shard_map.88
  86.2 1.6 %collective-permute-start.9 = (bf16[128,512]{1,0:T(8,128)(2,1)S(1)}, bf16[128,512]{1,0:T(8,128)(2,1)S(1)}, u32[]{:S(2)}, u32[]{:S(2)}) collective-permute-start(bf16[128,512]{1,0:T(8,128)(2,1)S(1)} %get-tuple-element.55), channel_id=1, source_target_pairs={{0,16},{16,0},{1,17},{17,1},{2,18},{18,2},{3,19},{19,3},{4,20},{20... | collective-permute-start | bytes 393224 | tf_op jit(solution)/shard_map/ppermute | solution.py:43
  87.8 3.5 %collective-permute-done.9 = bf16[128,512]{1,0:T(8,128)(2,1)S(1)} collective-permute-done((bf16[128,512]{1,0:T(8,128)(2,1)S(1)}, bf16[128,512]{1,0:T(8,128)(2,1)S(1)}, u32[]{:S(2)}, u32[]{:S(2)}) %collective-permute-start.9) | collective-permute-done | bytes 131104 | tf_op jit(solution)/shard_map/ppermute | solution.py:43
  91.3 0.7 broadcast_select_fusion
Async XLA Ops:
  20.4 1.6 %collective-permute-start = (bf16[8,16,1152]{2,1,0:T(8,128)(2,1)S(1)}, bf16[8,16,1152]{2,1,0:T(8,128)(2,1)S(1)}, u32[]{:S(2)}, u32[]{:S(2)}) collective-permute-start(bf16[8,16,1152]{2,1,0:T(8,128)(2,1)S(1)} %all_to_all.20.refs_0_), channel_id=1, source_target_pairs={{0,1},{1,0},{2,3},{3,2},{4,5},{5,4},{6,7},{7,6},{8,9},{9,8},{10,11... | collective-permute-start | bytes 884744 | tf_op jit(solution)/shard_map/ppermute | solution.py:39
  22.0 19.3 %copy-start.1 = (s32[200]{0:T(256)S(1)}, s32[200]{0:T(256)}, u32[]{:S(2)}) copy-start(s32[200]{0:T(256)} %param.10) | copy-start | bytes 2404
  23.3 26.1 %collective-permute-start.2 = (bf16[256,2048]{1,0:T(8,128)(2,1)S(1)}, bf16[256,2048]{1,0:T(8,128)(2,1)S(1)}, u32[]{:S(2)}, u32[]{:S(2)}) collective-permute-start(bf16[256,2048]{1,0:T(8,128)(2,1)S(1)} %shard_map.78.hand), channel_id=1, source_target_pairs={{0,16},{16,0},{1,17},{17,1},{2,18},{18,2},{3,19},{19,3},{4,20},{20... | collective-permute-start | bytes 3145736 | tf_op jit(solution)/shard_map/ppermute | solution.py:43
  37.9 1.6 %collective-permute-start.1 = (bf16[8,16,1152]{2,1,0:T(8,128)(2,1)S(1)}, bf16[8,16,1152]{2,1,0:T(8,128)(2,1)S(1)}, u32[]{:S(2)}, u32[]{:S(2)}) collective-permute-start(bf16[8,16,1152]{2,1,0:T(8,128)(2,1)S(1)} %all_to_all.21.refs_0_.refs_2_), channel_id=1, source_target_pairs={{0,1},{1,0},{2,3},{3,2},{4,5},{5,4},{6,7},{7,6},{8,9},{9,8},{10,11... | collective-permute-start | bytes 884744 | tf_op jit(solution)/shard_map/ppermute | solution.py:39
  40.7 22.7 %collective-permute-start.3 = (bf16[160,2048]{1,0:T(8,128)(2,1)S(1)}, bf16[160,2048]{1,0:T(8,128)(2,1)S(1)}, u32[]{:S(2)}, u32[]{:S(2)}) collective-permute-start(bf16[160,2048]{1,0:T(8,128)(2,1)S(1)} %get-tuple-element.33.hand), channel_id=1, source_target_pairs={{0,16},{16,0},{1,17},{17,1},{2,18},{18,2},{3,19},{19,3},{4,20},{20... | collective-permute-start | bytes 1966088 | tf_op jit(solution)/shard_map/ppermute | solution.py:43
  44.2 7.2 %copy-start = (bf16[1024,512]{1,0:T(8,128)(2,1)}, bf16[1024,512]{1,0:T(8,128)(2,1)S(1)}, u32[]{:S(2)}) copy-start(bf16[1024,512]{1,0:T(8,128)(2,1)S(1)} %get-tuple-element.36.turned) | copy-start | bytes 3145732
  51.5 1.4 %collective-permute-start.4 = (bf16[128,512]{1,0:T(8,128)(2,1)S(1)}, bf16[128,512]{1,0:T(8,128)(2,1)S(1)}, u32[]{:S(2)}, u32[]{:S(2)}) collective-permute-start(bf16[128,512]{1,0:T(8,128)(2,1)S(1)} %get-tuple-element.41), channel_id=1, source_target_pairs={{0,1},{1,0},{2,3},{3,2},{4,5},{5,4},{6,7},{7,6},{8,9},{9,8},{10,11... | collective-permute-start | bytes 393224 | tf_op jit(solution)/shard_map/ppermute | solution.py:39
  51.5 1.5 %collective-permute-start.5 = (bf16[128,512]{1,0:T(8,128)(2,1)S(1)}, bf16[128,512]{1,0:T(8,128)(2,1)S(1)}, u32[]{:S(2)}, u32[]{:S(2)}) collective-permute-start(bf16[128,512]{1,0:T(8,128)(2,1)S(1)} %get-tuple-element.42), channel_id=1, source_target_pairs={{0,1},{1,0},{2,3},{3,2},{4,5},{5,4},{6,7},{7,6},{8,9},{9,8},{10,11... | collective-permute-start | bytes 393224 | tf_op jit(solution)/shard_map/ppermute | solution.py:39
  53.9 13.6 %all-to-all-start.2 = ((bf16[8,16,1024]{2,1,0:T(8,128)(2,1)}), bf16[8,16,1024]{2,1,0:T(8,128)(2,1)S(1)}, u32[]{:S(2)}, u32[]{:S(2)}) async-start(bf16[8,16,1024]{2,1,0:T(8,128)(2,1)} %shard_map.82), calls=%async_computation.2 | async-start | bytes 524288 | tf_op jit(solution)/shard_map/all_to_all | solution.py:49
  57.3 13.8 %collective-permute-start.6 = (bf16[96,2048]{1,0:T(8,128)(2,1)S(1)}, bf16[96,2048]{1,0:T(8,128)(2,1)S(1)}, u32[]{:S(2)}, u32[]{:S(2)}) collective-permute-start(bf16[96,2048]{1,0:T(8,128)(2,1)S(1)} %get-tuple-element.34.hand), channel_id=1, source_target_pairs={{0,16},{16,0},{1,17},{17,1},{2,18},{18,2},{3,19},{19,3},{4,20},{20... | collective-permute-start | bytes 1179656 | tf_op jit(solution)/shard_map/ppermute | solution.py:43
  66.9 4.2 %collective-permute-start.7 = (bf16[128,512]{1,0:T(8,128)(2,1)S(1)}, bf16[128,512]{1,0:T(8,128)(2,1)S(1)}, u32[]{:S(2)}, u32[]{:S(2)}) collective-permute-start(bf16[128,512]{1,0:T(8,128)(2,1)S(1)} %get-tuple-element.49), channel_id=1, source_target_pairs={{0,1},{1,0},{2,3},{3,2},{4,5},{5,4},{6,7},{7,6},{8,9},{9,8},{10,11... | collective-permute-start | bytes 393224 | tf_op jit(solution)/shard_map/ppermute | solution.py:39
  66.9 4.1 %collective-permute-start.8 = (bf16[128,512]{1,0:T(8,128)(2,1)S(1)}, bf16[128,512]{1,0:T(8,128)(2,1)S(1)}, u32[]{:S(2)}, u32[]{:S(2)}) collective-permute-start(bf16[128,512]{1,0:T(8,128)(2,1)S(1)} %get-tuple-element.50), channel_id=1, source_target_pairs={{0,1},{1,0},{2,3},{3,2},{4,5},{5,4},{6,7},{7,6},{8,9},{9,8},{10,11... | collective-permute-start | bytes 393224 | tf_op jit(solution)/shard_map/ppermute | solution.py:39
  73.7 12.2 %all-to-all-start.3 = ((bf16[8,16,1024]{2,1,0:T(8,128)(2,1)}), bf16[8,16,1024]{2,1,0:T(8,128)(2,1)S(1)}, u32[]{:S(2)}, u32[]{:S(2)}) async-start(bf16[8,16,1024]{2,1,0:T(8,128)(2,1)} %get-tuple-element.53), calls=%async_computation.3 | async-start | bytes 524288 | tf_op jit(solution)/shard_map/all_to_all | solution.py:49
  86.2 5.0 %collective-permute-start.9 = (bf16[128,512]{1,0:T(8,128)(2,1)S(1)}, bf16[128,512]{1,0:T(8,128)(2,1)S(1)}, u32[]{:S(2)}, u32[]{:S(2)}) collective-permute-start(bf16[128,512]{1,0:T(8,128)(2,1)S(1)} %get-tuple-element.55), channel_id=1, source_target_pairs={{0,16},{16,0},{1,17},{17,1},{2,18},{18,2},{3,19},{19,3},{4,20},{20... | collective-permute-start | bytes 393224 | tf_op jit(solution)/shard_map/ppermute | solution.py:43

commit v6 on v5

--- a/solution.py
+++ b/solution.py
@@ -18,7 +18,7 @@
     return jax.ShapeDtypeStruct(shape, dtype)
 
 
-def call(kernel, outs, *args, scratch=(), spec=VMEM, out_spaces=None):
+def call(kernel, outs, *args, scratch=(), spec=VMEM, out_spaces=None, aliases=None):
     return pl.pallas_call(
         kernel,
         out_shape=outs,
@@ -29,6 +29,7 @@
             else jax.tree.map(lambda _: VMEM, outs)
         ),
         scratch_shapes=list(scratch),
+        input_output_aliases=aliases or {},
         compiler_params=pltpu.CompilerParams(vmem_limit_bytes=12 << 20),
         cost_estimate=pl.CostEstimate(flops=1000, bytes_accessed=1000, transcendentals=0),
     )(*args)
@@ -158,8 +159,11 @@
     turned[...] = lhs[...].T
 
 
-def product_kernel(count, pieces, *refs):
-    inputs, weight, hands, rows = refs[:count], refs[count], refs[count + 1 : -1], refs[-1]
+def product_kernel(count, pieces, at, *refs):
+    inputs, weight = refs[:count], refs[count]
+    hands, rows = refs[count + 1 : -1], refs[-1]
+    if at:
+        hands = hands[1:]
     width = rows.shape[1]
     is_up = lax.axis_index("section") == 0
     first = 0
@@ -173,16 +177,20 @@
         value = jnp.where(is_up, jnp.maximum(value, 0.0), value).astype(BF16)
         first = 0
         for hand in hands:
-            hand[:, j : j + tile] = value[first : first + hand.shape[0]]
-            first += hand.shape[0]
-
-
-def give(first, scale, total, out):
+            size = min(hand.shape[0], value.shape[0])
+            hand[at : at + size, j : j + tile] = value[first : first + size]
+            first += size
+
+
+def give(first, scale, total, *outs):
     chip = lax.axis_index("dp") // 2
-    chips, part, _ = out.shape
+    chips, part, columns = outs[0].shape
     total = (total * scale[first : first + part * chips, :]).astype(BF16)
-    for rel in range(chips):
-        out[chip ^ rel] = total[rel * part : (rel + 1) * part]
+    for i, out in enumerate(outs):
+        for rel in range(chips):
+            out[chip ^ rel] = total[
+                rel * part : (rel + 1) * part, i * columns : (i + 1) * columns
+            ]
 
 
 def stack_kernel(first, scale, mine, left, right, out):
@@ -242,17 +250,18 @@
     move.wait()
 
 
-def last_kernel(first, recv, hand, weight, scale, mine, left, right, partner, out, value, done):
+def last_kernel(first, recv, hand, weight, scale, mine, left, right, partner, *rest):
+    outs, value, done = rest[:-2], rest[-2], rest[-1]
     leave = mask_and_leave(recv, hand, value, partner, done)
     product = product_of(value[...], weight[...])
     theirs = jnp.concatenate([left[...], right[...]], axis=1)
     total = jnp.concatenate([mine[...], product], axis=0) + theirs.astype(F32)
-    give(first, scale, total, out)
+    give(first, scale, total, *outs)
     leave.wait()
 
 
-def weight_kernel(turned, *refs):
-    partners, out = refs[:-1], refs[-1]
+def weight_kernel(count, turned, *refs):
+    partners, out = refs[:count], refs[-1]
     rhs = jnp.concatenate([p[...] for p in partners], axis=0)
     out[...] = jnp.dot(turned[...], rhs, preferred_element_type=F32)
 
@@ -270,15 +279,22 @@
     )
 
 
-def unpack_kernel(info, back, out):
-    out[...] = unpack(0, info, back).astype(BF16)
-
-
-def final_kernel(info, back, early, left, right):
-    rows = (unpack(1, info, back) + early[...].astype(F32)).astype(BF16)
+def unpack_kernel(info, back, left, right):
+    rows = unpack(0, info, back).astype(BF16)
     half = left.shape[1]
     left[...] = rows[:, :half]
     right[...] = rows[:, half:]
+
+
+def choose_kernel(left, right, out):
+    is_up = lax.axis_index("section") == 0
+    out[...] = jnp.where(is_up, left[...], right[...])
+
+
+def final_kernel(info, back, left, right, out):
+    is_up = lax.axis_index("section") == 0
+    early = jnp.where(is_up, left[...], right[...]).astype(F32)
+    out[...] = (unpack(1, info, back) + early).astype(BF16)
 
 
 def on_device(section_rows, lang_ids, lang_table, lang_counts, temp_num, weights):
@@ -324,17 +340,16 @@
 
     hands, received, partners = [], [], []
 
-    def product(inputs, pieces, sizes):
-        count = sum(sizes)
-        hand = call(
-            functools.partial(product_kernel, len(inputs), pieces),
+    def product(inputs, pieces, sizes, at=0, sofar=()):
+        return call(
+            functools.partial(product_kernel, len(inputs), pieces, at),
             tuple(sds((size, ff_dev), BF16) for size in sizes),
             *inputs,
             fast_weight,
-            scratch=[pltpu.VMEM((count, width), BF16)],
+            *sofar,
+            scratch=[pltpu.VMEM((sum(piece[3] for piece in pieces), width), BF16)],
+            aliases={len(inputs) + 1: 0} if sofar else {},
         )
-        hands.append(hand)
-        received.append(across(hand))
 
     came, chunks = [], []
     for p in range(halves):
@@ -344,7 +359,14 @@
         cores = (1, 0) if p else (0, 1)
         chunks.append([(c, 0, r, part) for c in cores for r in range(chips)])
         rows = 2 * part * chips
-        product(came[2 * p :], chunks[p], [5 * rows // 8, 3 * rows // 8] if p else [rows])
+        if p:
+            hand = product(came[2:], chunks[p], [5 * rows // 8, 3 * rows // 8])
+        else:
+            mine = product(came[:1], chunks[p][:chips], [rows])
+            theirs = [(0, *rest) for _, *rest in chunks[p][chips:]]
+            hand = product(came[1:], theirs, [rows], rows // 2, mine)
+        hands.append(hand)
+        received.append(across(hand))
     layout = [(2 * p + which, *rest) for p in range(halves) for which, *rest in chunks[p]]
     total_rows = halves * rows
     scale, turned = call(
@@ -387,9 +409,9 @@
         sibling(left),
         sibling(right),
     )
-    early = call(
+    early_left, early_right = call(
         unpack_kernel,
-        sds((rows_dev, width), BF16),
+        (sds((rows_dev, width // 2), BF16),) * 2,
         info,
         same_core_exchange(stack),
     )
@@ -407,14 +429,14 @@
         keep_kernel,
         (pltpu.VMEM(own_weight.shape, BF16),),
         far_weight,
-        after(info, early, mine),
+        after(info, early_left, mine),
         scratch=[pltpu.SemaphoreType.DMA],
         spec=[in_hbm, VMEM],
     )
-    (stack,) = backed(
+    late_left, late_right = backed(
         functools.partial(last_kernel, rows + count),
         late_rows[1],
-        [sds((chips, part, width), BF16)],
+        [sds((chips, part, width // 2), BF16)] * 2,
         [
             after(received[1][1], partners[1], kept),
             hands[1][1],
@@ -425,32 +447,39 @@
             sibling(right),
         ],
     )
-    late = same_core_exchange(stack)
+    (late_recv,) = across([late_right])
     tile = 256
-    weight_grad = pl.pallas_call(
-        weight_kernel,
-        out_shape=sds((width, ff_dev), F32),
-        grid=(ff_dev // tile,),
-        in_specs=[pl.BlockSpec((width, total_rows), lambda j: (0, 0))]
-        + [pl.BlockSpec((p.shape[0], tile), lambda j: (0, j)) for p in partners],
-        out_specs=pl.BlockSpec((width, tile), lambda j: (0, j)),
-        compiler_params=pltpu.CompilerParams(vmem_limit_bytes=60 << 20),
-        cost_estimate=pl.CostEstimate(
-            flops=2 * width * total_rows * ff_dev,
-            bytes_accessed=4 * width * ff_dev,
-            transcendentals=0,
-        ),
-    )(turned, *partners)
+    first_tiles = ff_dev // tile // 4
+
+    def weight_part(start, steps, sofar=()):
+        return pl.pallas_call(
+            functools.partial(weight_kernel, len(partners)),
+            out_shape=sds((width, ff_dev), F32),
+            grid=(steps,),
+            in_specs=[pl.BlockSpec((width, total_rows), lambda j: (0, 0))]
+            + [pl.BlockSpec((p.shape[0], tile), lambda j: (0, start + j)) for p in partners]
+            + [pl.BlockSpec(memory_space=pl.ANY) for _ in sofar],
+            out_specs=pl.BlockSpec((width, tile), lambda j: (0, start + j)),
+            input_output_aliases={1 + len(partners): 0} if sofar else {},
+            compiler_params=pltpu.CompilerParams(vmem_limit_bytes=60 << 20),
+            cost_estimate=pl.CostEstimate(
+                flops=1000, bytes_accessed=1000, transcendentals=0
+            ),
+        )(turned, *partners, *sofar)
+
+    weight_grad = weight_part(0, first_tiles)
+    late_recv = after(late_recv, weight_grad)
+    late = call(choose_kernel, sds((chips, part, width // 2), BF16), late_left, late_recv)
+    late = same_core_exchange(late)
+    (early_recv,) = across([after(early_right, late_recv)])
+    weight_grad = weight_part(first_tiles, ff_dev // tile - first_tiles, [weight_grad])
     info = after(info, weight_grad)
-    left, right = call(
+    input_grad = pl.pallas_call(
         final_kernel,
-        (sds((rows_dev, width // 2), BF16),) * 2,
-        info,
-        late,
-        early,
-    )
-    (right_cols,) = across([right])
-    input_grad = jnp.where(is_up, left, right_cols)
+        out_shape=sds((rows_dev, width // 2), BF16),
+        compiler_params=pltpu.CompilerParams(vmem_limit_bytes=12 << 20),
+        cost_estimate=pl.CostEstimate(flops=1000, bytes_accessed=1000, transcendentals=0),
+    )(info, late, early_left, early_recv)
     return (weight_grad[None], input_grad)
 
 

time: 92.6 us -> 91.6 us (0.989)
  waiting for transfers between devices: 18.5 us -> 14.4 us
  Pallas kernels: 28.3 us -> 30.6 us
  starting transfers between devices: 13.2 us -> 14.8 us
    ppermute x4 -> x5, waiting for transfers between devices: 14.3 us -> 11 us  [across(): lax.ppermute(value, 'section', [(0, 1), (1, 0)])]
    pallas_call x1 -> x3, Pallas kernels: 8.8 us -> 11.2 us  [the longest x2 10.3 us: weight_part(): pl.pallas_call(functools.partial(weight_kernel, len(partners)), out_shape...]
    ppermute x4 -> x5, starting transfers between devices: 5.26 us -> 6.85 us  [across(): lax.ppermute(value, 'section', [(0, 1), (1, 0)])]
    pallas_call x11 -> x12, Pallas kernels: 19.5 us -> 19.4 us  [call(): pl.pallas_call(kernel, out_shape=outs, in_specs=spec if isinstance(spec,...]
  transfers between devices with their start and end apart: 12 -> 13, of which waited for: 8 -> 8; matrix products, arithmetic and copies ran while one was open for 0% -> 0% of each run, Pallas kernels for 24% -> 26%
where the time goes in v6:
time: 91.6 us; the launch traced here: 91 us
  Pallas kernels  30.6 us (33%)
  blocking collectives  30.4 us (33%)
  starting transfers between devices  14.8 us (16%)
  waiting for transfers between devices  14.4 us (16%)
    all_to_all x2, blocking collectives, same_core_exchange(): lax.all_to_all(value, 'dp', split_axis=0, concat_axis=0, axis_index_group...  30.4 us
    pallas_call x12, Pallas kernels, call(): pl.pallas_call(kernel, out_shape=outs, in_specs=spec if isinstance(spec,...  19.4 us
    ppermute x5, waiting for transfers between devices, across(): lax.ppermute(value, 'section', [(0, 1), (1, 0)])  11 us
    pallas_call x2, Pallas kernels, weight_part(): pl.pallas_call(functools.partial(weight_kernel, len(partners)), out_shape...  10.3 us
    ppermute x5, starting transfers between devices, across(): lax.ppermute(value, 'section', [(0, 1), (1, 0)])  6.85 us
    all_to_all x2, starting transfers between devices, same_core_exchange(): lax.all_to_all(value, 'dp', split_axis=0, concat_axis=0, axis_index_group...  6.78 us
    ppermute x6, waiting for transfers between devices, sibling(): return lax.ppermute(value, 'dp', [(i, i ^ 1) for i in range(count)])  3.42 us
  transfers between devices with their start and end apart: 13, of which 8 were waited for; matrix products, arithmetic and copies ran while one was open for 0% of the time, Pallas kernels for 26%

profile of v6, /device:TPU:0, one launch (start us, length us, event | category | flops | bytes accessed | tf_op | source)
XLA Modules:
  0.0 91.0 jit_solution(8837241200872696113)
XLA Ops:
  0.6 2.4 %shard_map.77 = (bf16[8,16,1152]{2,1,0:T(8,128)(2,1)S(1)}, bf16[8,16,1152]{2,1,0:T(8,128)(2,1)S(1)}, s32[8,128]{1,0:T(8,128)S(1)}, bf16[1024,2048]{1,0:T(8,128)(2,1)S(1)}) custom-call(s32[1,128]{1,0:T(1,128)} %bitcast.13, s32[1,200]{1,0:T(1,128)} %bitcast.12, s32[1,200]{1,0:T(1,128)} %refs_2_.1, bf16[128,1024]{1,0:T(8,128)(2,1)} %bitcast.11, ...), custom_call_target="tpu_custom_call" | custom-call | flops 1000 | bytes 1000 | tf_op jit(solution)/shard_map/pallas_call | solution.py:22
  3.0 17.4 %all_to_all.20.refs_0_ = bf16[8,16,1152]{2,1,0:T(8,128)(2,1)S(1)} all-to-all(bf16[8,16,1152]{2,1,0:T(8,128)(2,1)S(1)} %get-tuple-element.33), channel_id=1, replica_groups={{0,2,4,6,8,10,12,14},{1,3,5,7,9,11,13,15},{16,18,20,22,24,26,28,30},{17..., dimensions={0} | all-to-all | bytes 589824 | tf_op jit(solution)/shard_map/all_to_all | solution.py:50
  20.4 0.0 collective-permute-start
  20.4 0.8 shard_map.78.refs_2_
  21.2 0.8 collective-permute-done.refs_0_.refs_1_
  22.0 0.7 shard_map.79.hand
  22.8 0.0 copy-start.1
  22.8 1.6 %collective-permute-start.2 = (bf16[256,2048]{1,0:T(8,128)(2,1)S(1)}, bf16[256,2048]{1,0:T(8,128)(2,1)S(1)}, u32[]{:S(2)}, u32[]{:S(2)}) collective-permute-start(bf16[256,2048]{1,0:T(8,128)(2,1)S(1)} %shard_map.79.hand), channel_id=1, source_target_pairs={{0,16},{16,0},{1,17},{17,1},{2,18},{18,2},{3,19},{19,3},{4,20},{20... | collective-permute-start | bytes 3145736 | tf_op jit(solution)/shard_map/ppermute | solution.py:44
  24.3 13.0 %all_to_all.21.refs_0_.refs_2_ = bf16[8,16,1152]{2,1,0:T(8,128)(2,1)S(1)} all-to-all(bf16[8,16,1152]{2,1,0:T(8,128)(2,1)S(1)} %get-tuple-element.35), channel_id=1, replica_groups={{0,2,4,6,8,10,12,14},{1,3,5,7,9,11,13,15},{16,18,20,22,24,26,28,30},{17..., dimensions={0} | all-to-all | bytes 589824 | tf_op jit(solution)/shard_map/all_to_all | solution.py:50
  37.3 0.0 collective-permute-start.1
  37.4 1.6 %collective-permute-done.1.refs_1_.refs_3_ = bf16[8,16,1152]{2,1,0:T(8,128)(2,1)S(1)} collective-permute-done((bf16[8,16,1152]{2,1,0:T(8,128)(2,1)S(1)}, bf16[8,16,1152]{2,1,0:T(8,128)(2,1)S(1)}, u32[]{:S(2)}, u32[]{:S(2)}) %collective-permute-start.1) | collective-permute-done | bytes 294944 | tf_op jit(solution)/shard_map/ppermute | solution.py:40
  38.9 1.3 %shard_map.80 = (bf16[160,2048]{1,0:T(8,128)(2,1)S(1)}, bf16[96,2048]{1,0:T(8,128)(2,1)S(1)}) custom-call(bf16[8,16,1152]{2,1,0:T(8,128)(2,1)S(1)} %all_to_all.21.refs_0_.refs_2_, bf16[8,16,1152]{2,1,0:T(8,128)(2,1)S(1)} %collective-permute-done.1.refs_1_.refs_3_, bf16[1024,2048]{1,0:T(8,128)(2,1)S(1)} %get-tuple-element.34.refs_1_.refs_2_.weight), custom_call_target="tpu_custom_call" | custom-call | flops 1000 | bytes 1000 | tf_op jit(solution)/shard_map/pallas_call | solution.py:22
  40.2 0.6 collective-permute-start.3
  40.8 0.0 copy-done.1
  40.8 2.9 %shard_map.81 = (f32[512,1]{1,0:T(8,128)S(1)}, bf16[1024,512]{1,0:T(8,128)(2,1)S(1)}) custom-call(s32[1,200]{1,0:T(1,128)S(1)} %bitcast.6, bf16[8,16,1152]{2,1,0:T(8,128)(2,1)S(1)} %all_to_all.20.refs_0_, bf16[8,16,1152]{2,1,0:T(8,128)(2,1)S(1)} %collective-permute-done.refs_0_.refs_1_, bf16[8,16,1152]{2,1,0:T(8,128)(2,1)S(1)} %all_to_all.21.refs_0_.refs_2_, ...), custom_call_target="tpu_custom_call" | custom-call | flops 1000 | bytes 1000 | tf_op jit(solution)/shard_map/pallas_call | solution.py:22
  43.7 0.0 copy-start
  43.7 5.1 %collective-permute-done.2.recv = bf16[256,2048]{1,0:T(8,128)(2,1)S(1)} collective-permute-done((bf16[256,2048]{1,0:T(8,128)(2,1)S(1)}, bf16[256,2048]{1,0:T(8,128)(2,1)S(1)}, u32[]{:S(2)}, u32[]{:S(2)}) %collective-permute-start.2) | collective-permute-done | bytes 1048608 | tf_op jit(solution)/shard_map/ppermute | solution.py:44
  48.8 2.1 %shard_map.82 = (bf16[256,2048]{1,0:T(8,128)(2,1)}, f32[128,1024]{1,0:T(8,128)S(1)}, bf16[128,512]{1,0:T(8,128)(2,1)S(1)}, bf16[128,512]{1,0:T(8,128)(2,1)S(1)}) custom-call(bf16[256,2048]{1,0:T(8,128)(2,1)S(1)} %collective-permute-done.2.recv, bf16[256,2048]{1,0:T(8,128)(2,1)S(1)} %shard_map.79.hand, ...), custom_call_target="tpu_custom_call" | custom-call | flops 1000 | bytes 1000 | tf_op jit(solution)/shard_map/pallas_call | solution.py:22
  50.9 0.0 copy-done
  50.9 0.1 collective-permute-start.4
  51.0 0.5 collective-permute-start.5
  51.5 0.8 collective-permute-done.4.left
  52.3 0.2 collective-permute-done.5.right
  52.5 0.8 shard_map.83
  53.3 3.4 %all-to-all-start.2 = ((bf16[8,16,1024]{2,1,0:T(8,128)(2,1)}), bf16[8,16,1024]{2,1,0:T(8,128)(2,1)S(1)}, u32[]{:S(2)}, u32[]{:S(2)}) async-start(bf16[8,16,1024]{2,1,0:T(8,128)(2,1)} %shard_map.83), calls=%async_computation.2 | async-start | bytes 524288 | tf_op jit(solution)/shard_map/all_to_all | solution.py:50
  56.7 1.5 %collective-permute-start.6 = (bf16[96,2048]{1,0:T(8,128)(2,1)S(1)}, bf16[96,2048]{1,0:T(8,128)(2,1)S(1)}, u32[]{:S(2)}, u32[]{:S(2)}) collective-permute-start(bf16[96,2048]{1,0:T(8,128)(2,1)S(1)} %get-tuple-element.37.hand), channel_id=1, source_target_pairs={{0,16},{16,0},{1,17},{17,1},{2,18},{18,2},{3,19},{19,3},{4,20},{20... | collective-permute-start | bytes 1179656 | tf_op jit(solution)/shard_map/ppermute | solution.py:44
  58.3 4.6 %collective-permute-done.3.recv = bf16[160,2048]{1,0:T(8,128)(2,1)S(1)} collective-permute-done((bf16[160,2048]{1,0:T(8,128)(2,1)S(1)}, bf16[160,2048]{1,0:T(8,128)(2,1)S(1)}, u32[]{:S(2)}, u32[]{:S(2)}) %collective-permute-start.3) | collective-permute-done | bytes 655392 | tf_op jit(solution)/shard_map/ppermute | solution.py:44
  62.9 3.4 %shard_map.84 = (bf16[160,2048]{1,0:T(8,128)(2,1)}, f32[32,1024]{1,0:T(8,128)S(1)}, bf16[128,512]{1,0:T(8,128)(2,1)S(1)}, bf16[128,512]{1,0:T(8,128)(2,1)S(1)}) custom-call(bf16[160,2048]{1,0:T(8,128)(2,1)S(1)} %collective-permute-done.3.recv, bf16[160,2048]{1,0:T(8,128)(2,1)S(1)} %get-tuple-element.36.hand, bf16[1024,2048]{1,0:T(8,128)(2,1)} %bitcast.8), custom_call_target="tpu_custom_call" | custom-call | flops 1000 | bytes 1000 | tf_op jit(solution)/shard_map/pallas_call | solution.py:22
  66.3 0.1 collective-permute-start.7
  66.4 0.5 collective-permute-start.8
  66.9 0.0 all-to-all-done.2.back
  66.9 0.3 shard_map.85
  67.2 2.2 %shard_map.86.weight = bf16[1024,2048]{1,0:T(8,128)(2,1)S(1)} custom-call(bf16[1024,2048]{1,0:T(8,128)(2,1)} %bitcast.9, s32[8,128]{1,0:T(8,128)S(1)} %get-tuple-element.56.info.token), custom_call_target="tpu_custom_call" | custom-call | flops 1000 | bytes 1000 | tf_op jit(solution)/shard_map/pallas_call | solution.py:22
  69.4 1.1 %collective-permute-done.6.recv = bf16[96,2048]{1,0:T(8,128)(2,1)S(1)} collective-permute-done((bf16[96,2048]{1,0:T(8,128)(2,1)S(1)}, bf16[96,2048]{1,0:T(8,128)(2,1)S(1)}, u32[]{:S(2)}, u32[]{:S(2)}) %collective-permute-start.6) | collective-permute-done | bytes 393248 | tf_op jit(solution)/shard_map/ppermute | solution.py:44
  70.5 0.0 collective-permute-done.7.left
  70.5 0.0 collective-permute-done.8.right
  70.5 2.0 %shard_map.87 = (bf16[96,2048]{1,0:T(8,128)(2,1)}, bf16[8,16,512]{2,1,0:T(8,128)(2,1)S(1)}, bf16[8,16,512]{2,1,0:T(8,128)(2,1)S(1)}) custom-call(bf16[96,2048]{1,0:T(8,128)(2,1)S(1)} %collective-permute-done.6.recv, bf16[96,2048]{1,0:T(8,128)(2,1)S(1)} %get-tuple-element.37.hand, bf16[1024,2048]{1,0:T(8,128)(2,1)S(1)} %shard_map.86.weight, ...), custom_call_target="tpu_custom_call" | custom-call | flops 1000 | bytes 1000 | tf_op jit(solution)/shard_map/pallas_call | solution.py:22
  72.5 1.6 %collective-permute-start.9 = (bf16[8,16,512]{2,1,0:T(8,128)(2,1)S(1)}, bf16[8,16,512]{2,1,0:T(8,128)(2,1)S(1)}, u32[]{:S(2)}, u32[]{:S(2)}) collective-permute-start(bf16[8,16,512]{2,1,0:T(8,128)(2,1)S(1)} %get-tuple-element.58), channel_id=1, source_target_pairs={{0,16},{16,0},{1,17},{17,1},{2,18},{18,2},{3,19},{19,3},{4,20},{20... | collective-permute-start | bytes 393224 | tf_op jit(solution)/shard_map/ppermute | solution.py:44
  74.1 3.3 %shard_map.88.refs_3_ = f32[1024,2048]{1,0:T(8,128)} custom-call(bf16[1024,512]{1,0:T(8,128)(2,1)} %copy-done, bf16[256,2048]{1,0:T(8,128)(2,1)} %get-tuple-element.42.refs_0_, bf16[160,2048]{1,0:T(8,128)(2,1)} %get-tuple-element.47.refs_1_, bf16[96,2048]{1,0:T(8,128)(2,1)} %get-tuple-element.55.refs_2_), custom_call_target="tpu_custom_call" | custom-call | flops 1000 | bytes 1000 | tf_op jit(solution)/shard_map/pallas_call | solution.py:455
  77.4 0.2 collective-permute-done.9.right
  77.5 0.7 shard_map.90
  78.2 3.4 %all-to-all-start.3 = ((bf16[8,16,512]{2,1,0:T(8,128)(2,1)}), bf16[8,16,512]{2,1,0:T(8,128)(2,1)S(1)}, u32[]{:S(2)}, u32[]{:S(2)}) async-start(bf16[8,16,512]{2,1,0:T(8,128)(2,1)} %shard_map.90), calls=%async_computation.3 | async-start | bytes 262144 | tf_op jit(solution)/shard_map/all_to_all | solution.py:50
  81.6 1.6 %collective-permute-start.10 = (bf16[128,512]{1,0:T(8,128)(2,1)S(1)}, bf16[128,512]{1,0:T(8,128)(2,1)S(1)}, u32[]{:S(2)}, u32[]{:S(2)}) collective-permute-start(bf16[128,512]{1,0:T(8,128)(2,1)S(1)} %get-tuple-element.61), channel_id=1, source_target_pairs={{0,16},{16,0},{1,17},{17,1},{2,18},{18,2},{3,19},{19,3},{4,20},{20... | collective-permute-start | bytes 393224 | tf_op jit(solution)/shard_map/ppermute | solution.py:44
  83.1 7.0 %shard_map.89 = f32[1024,2048]{1,0:T(8,128)} custom-call(bf16[1024,512]{1,0:T(8,128)(2,1)} %copy-done, bf16[256,2048]{1,0:T(8,128)(2,1)} %get-tuple-element.42.refs_0_, bf16[160,2048]{1,0:T(8,128)(2,1)} %get-tuple-element.47.refs_1_, bf16[96,2048]{1,0:T(8,128)(2,1)} %get-tuple-element.55.refs_2_, ...), custom_call_target="tpu_custom_call", output_to_operand_aliasing={{}: (4, {})} | custom-call | flops 1000 | bytes 1000 | tf_op jit(solution)/shard_map/pallas_call | solution.py:455
  90.1 0.0 collective-permute-done.10.right
  90.1 0.0 all-to-all-done.3.back
  90.1 0.9 shard_map.91
Async XLA Ops:
  20.4 1.6 %collective-permute-start = (bf16[8,16,1152]{2,1,0:T(8,128)(2,1)S(1)}, bf16[8,16,1152]{2,1,0:T(8,128)(2,1)S(1)}, u32[]{:S(2)}, u32[]{:S(2)}) collective-permute-start(bf16[8,16,1152]{2,1,0:T(8,128)(2,1)S(1)} %all_to_all.20.refs_0_), channel_id=1, source_target_pairs={{0,1},{1,0},{2,3},{3,2},{4,5},{5,4},{6,7},{7,6},{8,9},{9,8},{10,11... | collective-permute-start | bytes 884744 | tf_op jit(solution)/shard_map/ppermute | solution.py:40
  22.8 18.1 %copy-start.1 = (s32[200]{0:T(256)S(1)}, s32[200]{0:T(256)}, u32[]{:S(2)}) copy-start(s32[200]{0:T(256)} %param.10) | copy-start | bytes 2404
  22.8 26.1 %collective-permute-start.2 = (bf16[256,2048]{1,0:T(8,128)(2,1)S(1)}, bf16[256,2048]{1,0:T(8,128)(2,1)S(1)}, u32[]{:S(2)}, u32[]{:S(2)}) collective-permute-start(bf16[256,2048]{1,0:T(8,128)(2,1)S(1)} %shard_map.79.hand), channel_id=1, source_target_pairs={{0,16},{16,0},{1,17},{17,1},{2,18},{18,2},{3,19},{19,3},{4,20},{20... | collective-permute-start | bytes 3145736 | tf_op jit(solution)/shard_map/ppermute | solution.py:44
  37.3 1.6 %collective-permute-start.1 = (bf16[8,16,1152]{2,1,0:T(8,128)(2,1)S(1)}, bf16[8,16,1152]{2,1,0:T(8,128)(2,1)S(1)}, u32[]{:S(2)}, u32[]{:S(2)}) collective-permute-start(bf16[8,16,1152]{2,1,0:T(8,128)(2,1)S(1)} %all_to_all.21.refs_0_.refs_2_), channel_id=1, source_target_pairs={{0,1},{1,0},{2,3},{3,2},{4,5},{5,4},{6,7},{7,6},{8,9},{9,8},{10,11... | collective-permute-start | bytes 884744 | tf_op jit(solution)/shard_map/ppermute | solution.py:40
  40.2 22.7 %collective-permute-start.3 = (bf16[160,2048]{1,0:T(8,128)(2,1)S(1)}, bf16[160,2048]{1,0:T(8,128)(2,1)S(1)}, u32[]{:S(2)}, u32[]{:S(2)}) collective-permute-start(bf16[160,2048]{1,0:T(8,128)(2,1)S(1)} %get-tuple-element.36.hand), channel_id=1, source_target_pairs={{0,16},{16,0},{1,17},{17,1},{2,18},{18,2},{3,19},{19,3},{4,20},{20... | collective-permute-start | bytes 1966088 | tf_op jit(solution)/shard_map/ppermute | solution.py:44
  43.7 7.2 %copy-start = (bf16[1024,512]{1,0:T(8,128)(2,1)}, bf16[1024,512]{1,0:T(8,128)(2,1)S(1)}, u32[]{:S(2)}) copy-start(bf16[1024,512]{1,0:T(8,128)(2,1)S(1)} %get-tuple-element.39.turned) | copy-start | bytes 3145732
  50.9 1.4 %collective-permute-start.4 = (bf16[128,512]{1,0:T(8,128)(2,1)S(1)}, bf16[128,512]{1,0:T(8,128)(2,1)S(1)}, u32[]{:S(2)}, u32[]{:S(2)}) collective-permute-start(bf16[128,512]{1,0:T(8,128)(2,1)S(1)} %get-tuple-element.44), channel_id=1, source_target_pairs={{0,1},{1,0},{2,3},{3,2},{4,5},{5,4},{6,7},{7,6},{8,9},{9,8},{10,11... | collective-permute-start | bytes 393224 | tf_op jit(solution)/shard_map/ppermute | solution.py:40
  51.0 1.5 %collective-permute-start.5 = (bf16[128,512]{1,0:T(8,128)(2,1)S(1)}, bf16[128,512]{1,0:T(8,128)(2,1)S(1)}, u32[]{:S(2)}, u32[]{:S(2)}) collective-permute-start(bf16[128,512]{1,0:T(8,128)(2,1)S(1)} %get-tuple-element.45), channel_id=1, source_target_pairs={{0,1},{1,0},{2,3},{3,2},{4,5},{5,4},{6,7},{7,6},{8,9},{9,8},{10,11... | collective-permute-start | bytes 393224 | tf_op jit(solution)/shard_map/ppermute | solution.py:40
  53.3 13.6 %all-to-all-start.2 = ((bf16[8,16,1024]{2,1,0:T(8,128)(2,1)}), bf16[8,16,1024]{2,1,0:T(8,128)(2,1)S(1)}, u32[]{:S(2)}, u32[]{:S(2)}) async-start(bf16[8,16,1024]{2,1,0:T(8,128)(2,1)} %shard_map.83), calls=%async_computation.2 | async-start | bytes 524288 | tf_op jit(solution)/shard_map/all_to_all | solution.py:50
  56.7 13.8 %collective-permute-start.6 = (bf16[96,2048]{1,0:T(8,128)(2,1)S(1)}, bf16[96,2048]{1,0:T(8,128)(2,1)S(1)}, u32[]{:S(2)}, u32[]{:S(2)}) collective-permute-start(bf16[96,2048]{1,0:T(8,128)(2,1)S(1)} %get-tuple-element.37.hand), channel_id=1, source_target_pairs={{0,16},{16,0},{1,17},{17,1},{2,18},{18,2},{3,19},{19,3},{4,20},{20... | collective-permute-start | bytes 1179656 | tf_op jit(solution)/shard_map/ppermute | solution.py:44
  66.3 4.2 %collective-permute-start.7 = (bf16[128,512]{1,0:T(8,128)(2,1)S(1)}, bf16[128,512]{1,0:T(8,128)(2,1)S(1)}, u32[]{:S(2)}, u32[]{:S(2)}) collective-permute-start(bf16[128,512]{1,0:T(8,128)(2,1)S(1)} %get-tuple-element.53), channel_id=1, source_target_pairs={{0,1},{1,0},{2,3},{3,2},{4,5},{5,4},{6,7},{7,6},{8,9},{9,8},{10,11... | collective-permute-start | bytes 393224 | tf_op jit(solution)/shard_map/ppermute | solution.py:40
  66.4 4.1 %collective-permute-start.8 = (bf16[128,512]{1,0:T(8,128)(2,1)S(1)}, bf16[128,512]{1,0:T(8,128)(2,1)S(1)}, u32[]{:S(2)}, u32[]{:S(2)}) collective-permute-start(bf16[128,512]{1,0:T(8,128)(2,1)S(1)} %get-tuple-element.54), channel_id=1, source_target_pairs={{0,1},{1,0},{2,3},{3,2},{4,5},{5,4},{6,7},{7,6},{8,9},{9,8},{10,11... | collective-permute-start | bytes 393224 | tf_op jit(solution)/shard_map/ppermute | solution.py:40
  72.5 5.0 %collective-permute-start.9 = (bf16[8,16,512]{2,1,0:T(8,128)(2,1)S(1)}, bf16[8,16,512]{2,1,0:T(8,128)(2,1)S(1)}, u32[]{:S(2)}, u32[]{:S(2)}) collective-permute-start(bf16[8,16,512]{2,1,0:T(8,128)(2,1)S(1)} %get-tuple-element.58), channel_id=1, source_target_pairs={{0,16},{16,0},{1,17},{17,1},{2,18},{18,2},{3,19},{19,3},{4,20},{20... | collective-permute-start | bytes 393224 | tf_op jit(solution)/shard_map/ppermute | solution.py:44
  78.2 11.9 %all-to-all-start.3 = ((bf16[8,16,512]{2,1,0:T(8,128)(2,1)}), bf16[8,16,512]{2,1,0:T(8,128)(2,1)S(1)}, u32[]{:S(2)}, u32[]{:S(2)}) async-start(bf16[8,16,512]{2,1,0:T(8,128)(2,1)} %shard_map.90), calls=%async_computation.3 | async-start | bytes 262144 | tf_op jit(solution)/shard_map/all_to_all | solution.py:50
  81.6 8.6 %collective-permute-start.10 = (bf16[128,512]{1,0:T(8,128)(2,1)S(1)}, bf16[128,512]{1,0:T(8,128)(2,1)S(1)}, u32[]{:S(2)}, u32[]{:S(2)}) collective-permute-start(bf16[128,512]{1,0:T(8,128)(2,1)S(1)} %get-tuple-element.61), channel_id=1, source_target_pairs={{0,16},{16,0},{1,17},{17,1},{2,18},{18,2},{3,19},{19,3},{4,20},{20... | collective-permute-start | bytes 393224 | tf_op jit(solution)/shard_map/ppermute | solution.py:44

commit v7 on v6

--- a/solution.py
+++ b/solution.py
@@ -68,7 +68,7 @@
     ]
     for move in moves:
         move.start()
-    for move in moves[:4]:
+    for move in moves[:3]:
         move.wait()
     ids, table, counts, rows = copies[:4]
     chips, part, _ = packed[0].shape
@@ -105,6 +105,7 @@
             notes = notes + jnp.where(within == 0, head, 0.0) + jnp.where(within == 1, tail, 0.0)
         return moved, notes.astype(BF16)
 
+    moves[3].wait()
     for p, out in enumerate(packed):
         inside = (slot // part) == p
         target = jnp.where(inside, block * part + slot % part, -1)
@@ -448,7 +449,7 @@
         ],
     )
     (late_recv,) = across([late_right])
-    tile = 256
+    tile = 512
     first_tiles = ff_dev // tile // 4
 
     def weight_part(start, steps, sofar=()):

time: 91.6 us -> 90.4 us (0.987)
  Pallas kernels: 30.6 us -> 29.5 us
    pallas_call x2, Pallas kernels: 10.3 us -> 9.16 us  [weight_part(): pl.pallas_call(functools.partial(weight_kernel, len(partners)), out_shape...]
  transfers between devices with their start and end apart: 13 -> 13, of which waited for: 8 -> 8; matrix products, arithmetic and copies ran while one was open for 0% -> 0% of each run, Pallas kernels for 26% -> 25%
where the time goes in v7:
time: 90.4 us; the launch traced here: 89.8 us
  blocking collectives  30.4 us (34%)
  Pallas kernels  29.5 us (33%)
  starting transfers between devices  14.8 us (16%)
  waiting for transfers between devices  14.4 us (16%)
    all_to_all x2, blocking collectives, same_core_exchange(): lax.all_to_all(value, 'dp', split_axis=0, concat_axis=0, axis_index_group...  30.4 us
    pallas_call x12, Pallas kernels, call(): pl.pallas_call(kernel, out_shape=outs, in_specs=spec if isinstance(spec,...  19.4 us
    ppermute x5, waiting for transfers between devices, across(): lax.ppermute(value, 'section', [(0, 1), (1, 0)])  10.9 us
    pallas_call x2, Pallas kernels, weight_part(): pl.pallas_call(functools.partial(weight_kernel, len(partners)), out_shape...  9.16 us
    ppermute x5, starting transfers between devices, across(): lax.ppermute(value, 'section', [(0, 1), (1, 0)])  6.85 us
    all_to_all x2, starting transfers between devices, same_core_exchange(): lax.all_to_all(value, 'dp', split_axis=0, concat_axis=0, axis_index_group...  6.78 us
    ppermute x6, waiting for transfers between devices, sibling(): return lax.ppermute(value, 'dp', [(i, i ^ 1) for i in range(count)])  3.42 us
  transfers between devices with their start and end apart: 13, of which 8 were waited for; matrix products, arithmetic and copies ran while one was open for 0% of the time, Pallas kernels for 25%

profile of v7, /device:TPU:0, one launch (start us, length us, event | category | flops | bytes accessed | tf_op | source)
XLA Modules:
  0.0 89.8 jit_solution(16429681608194539617)
XLA Ops:
  0.6 2.4 %shard_map.77 = (bf16[8,16,1152]{2,1,0:T(8,128)(2,1)S(1)}, bf16[8,16,1152]{2,1,0:T(8,128)(2,1)S(1)}, s32[8,128]{1,0:T(8,128)S(1)}, bf16[1024,2048]{1,0:T(8,128)(2,1)S(1)}) custom-call(s32[1,128]{1,0:T(1,128)} %bitcast.13, s32[1,200]{1,0:T(1,128)} %bitcast.12, s32[1,200]{1,0:T(1,128)} %refs_2_.1, bf16[128,1024]{1,0:T(8,128)(2,1)} %bitcast.11, ...), custom_call_target="tpu_custom_call" | custom-call | flops 1000 | bytes 1000 | tf_op jit(solution)/shard_map/pallas_call | solution.py:22
  3.0 17.4 %all_to_all.20.refs_0_ = bf16[8,16,1152]{2,1,0:T(8,128)(2,1)S(1)} all-to-all(bf16[8,16,1152]{2,1,0:T(8,128)(2,1)S(1)} %get-tuple-element.33), channel_id=1, replica_groups={{0,2,4,6,8,10,12,14},{1,3,5,7,9,11,13,15},{16,18,20,22,24,26,28,30},{17..., dimensions={0} | all-to-all | bytes 589824 | tf_op jit(solution)/shard_map/all_to_all | solution.py:50
  20.4 0.0 collective-permute-start
  20.4 0.8 shard_map.78.refs_2_
  21.2 0.8 collective-permute-done.refs_0_.refs_1_
  22.0 0.7 shard_map.79.hand
  22.8 0.0 copy-start.1
  22.8 1.6 %collective-permute-start.2 = (bf16[256,2048]{1,0:T(8,128)(2,1)S(1)}, bf16[256,2048]{1,0:T(8,128)(2,1)S(1)}, u32[]{:S(2)}, u32[]{:S(2)}) collective-permute-start(bf16[256,2048]{1,0:T(8,128)(2,1)S(1)} %shard_map.79.hand), channel_id=1, source_target_pairs={{0,16},{16,0},{1,17},{17,1},{2,18},{18,2},{3,19},{19,3},{4,20},{20... | collective-permute-start | bytes 3145736 | tf_op jit(solution)/shard_map/ppermute | solution.py:44
  24.3 13.0 %all_to_all.21.refs_0_.refs_2_ = bf16[8,16,1152]{2,1,0:T(8,128)(2,1)S(1)} all-to-all(bf16[8,16,1152]{2,1,0:T(8,128)(2,1)S(1)} %get-tuple-element.35), channel_id=1, replica_groups={{0,2,4,6,8,10,12,14},{1,3,5,7,9,11,13,15},{16,18,20,22,24,26,28,30},{17..., dimensions={0} | all-to-all | bytes 589824 | tf_op jit(solution)/shard_map/all_to_all | solution.py:50
  37.3 0.0 collective-permute-start.1
  37.4 1.6 %collective-permute-done.1.refs_1_.refs_3_ = bf16[8,16,1152]{2,1,0:T(8,128)(2,1)S(1)} collective-permute-done((bf16[8,16,1152]{2,1,0:T(8,128)(2,1)S(1)}, bf16[8,16,1152]{2,1,0:T(8,128)(2,1)S(1)}, u32[]{:S(2)}, u32[]{:S(2)}) %collective-permute-start.1) | collective-permute-done | bytes 294944 | tf_op jit(solution)/shard_map/ppermute | solution.py:40
  38.9 1.3 %shard_map.80 = (bf16[160,2048]{1,0:T(8,128)(2,1)S(1)}, bf16[96,2048]{1,0:T(8,128)(2,1)S(1)}) custom-call(bf16[8,16,1152]{2,1,0:T(8,128)(2,1)S(1)} %all_to_all.21.refs_0_.refs_2_, bf16[8,16,1152]{2,1,0:T(8,128)(2,1)S(1)} %collective-permute-done.1.refs_1_.refs_3_, bf16[1024,2048]{1,0:T(8,128)(2,1)S(1)} %get-tuple-element.34.refs_1_.refs_2_.weight), custom_call_target="tpu_custom_call" | custom-call | flops 1000 | bytes 1000 | tf_op jit(solution)/shard_map/pallas_call | solution.py:22
  40.2 0.6 collective-permute-start.3
  40.8 0.0 copy-done.1
  40.8 2.9 %shard_map.81 = (f32[512,1]{1,0:T(8,128)S(1)}, bf16[1024,512]{1,0:T(8,128)(2,1)S(1)}) custom-call(s32[1,200]{1,0:T(1,128)S(1)} %bitcast.6, bf16[8,16,1152]{2,1,0:T(8,128)(2,1)S(1)} %all_to_all.20.refs_0_, bf16[8,16,1152]{2,1,0:T(8,128)(2,1)S(1)} %collective-permute-done.refs_0_.refs_1_, bf16[8,16,1152]{2,1,0:T(8,128)(2,1)S(1)} %all_to_all.21.refs_0_.refs_2_, ...), custom_call_target="tpu_custom_call" | custom-call | flops 1000 | bytes 1000 | tf_op jit(solution)/shard_map/pallas_call | solution.py:22
  43.7 0.0 copy-start
  43.7 5.1 %collective-permute-done.2.recv = bf16[256,2048]{1,0:T(8,128)(2,1)S(1)} collective-permute-done((bf16[256,2048]{1,0:T(8,128)(2,1)S(1)}, bf16[256,2048]{1,0:T(8,128)(2,1)S(1)}, u32[]{:S(2)}, u32[]{:S(2)}) %collective-permute-start.2) | collective-permute-done | bytes 1048608 | tf_op jit(solution)/shard_map/ppermute | solution.py:44
  48.8 2.1 %shard_map.82 = (bf16[256,2048]{1,0:T(8,128)(2,1)}, f32[128,1024]{1,0:T(8,128)S(1)}, bf16[128,512]{1,0:T(8,128)(2,1)S(1)}, bf16[128,512]{1,0:T(8,128)(2,1)S(1)}) custom-call(bf16[256,2048]{1,0:T(8,128)(2,1)S(1)} %collective-permute-done.2.recv, bf16[256,2048]{1,0:T(8,128)(2,1)S(1)} %shard_map.79.hand, ...), custom_call_target="tpu_custom_call" | custom-call | flops 1000 | bytes 1000 | tf_op jit(solution)/shard_map/pallas_call | solution.py:22
  50.9 0.0 copy-done
  50.9 0.1 collective-permute-start.4
  51.0 0.5 collective-permute-start.5
  51.5 0.8 collective-permute-done.4.left
  52.3 0.2 collective-permute-done.5.right
  52.5 0.8 shard_map.83
  53.3 3.4 %all-to-all-start.2 = ((bf16[8,16,1024]{2,1,0:T(8,128)(2,1)}), bf16[8,16,1024]{2,1,0:T(8,128)(2,1)S(1)}, u32[]{:S(2)}, u32[]{:S(2)}) async-start(bf16[8,16,1024]{2,1,0:T(8,128)(2,1)} %shard_map.83), calls=%async_computation.2 | async-start | bytes 524288 | tf_op jit(solution)/shard_map/all_to_all | solution.py:50
  56.7 1.5 %collective-permute-start.6 = (bf16[96,2048]{1,0:T(8,128)(2,1)S(1)}, bf16[96,2048]{1,0:T(8,128)(2,1)S(1)}, u32[]{:S(2)}, u32[]{:S(2)}) collective-permute-start(bf16[96,2048]{1,0:T(8,128)(2,1)S(1)} %get-tuple-element.37.hand), channel_id=1, source_target_pairs={{0,16},{16,0},{1,17},{17,1},{2,18},{18,2},{3,19},{19,3},{4,20},{20... | collective-permute-start | bytes 1179656 | tf_op jit(solution)/shard_map/ppermute | solution.py:44
  58.3 4.6 %collective-permute-done.3.recv = bf16[160,2048]{1,0:T(8,128)(2,1)S(1)} collective-permute-done((bf16[160,2048]{1,0:T(8,128)(2,1)S(1)}, bf16[160,2048]{1,0:T(8,128)(2,1)S(1)}, u32[]{:S(2)}, u32[]{:S(2)}) %collective-permute-start.3) | collective-permute-done | bytes 655392 | tf_op jit(solution)/shard_map/ppermute | solution.py:44
  62.9 3.4 %shard_map.84 = (bf16[160,2048]{1,0:T(8,128)(2,1)}, f32[32,1024]{1,0:T(8,128)S(1)}, bf16[128,512]{1,0:T(8,128)(2,1)S(1)}, bf16[128,512]{1,0:T(8,128)(2,1)S(1)}) custom-call(bf16[160,2048]{1,0:T(8,128)(2,1)S(1)} %collective-permute-done.3.recv, bf16[160,2048]{1,0:T(8,128)(2,1)S(1)} %get-tuple-element.36.hand, bf16[1024,2048]{1,0:T(8,128)(2,1)} %bitcast.8), custom_call_target="tpu_custom_call" | custom-call | flops 1000 | bytes 1000 | tf_op jit(solution)/shard_map/pallas_call | solution.py:22
  66.3 0.1 collective-permute-start.7
  66.4 0.5 collective-permute-start.8
  66.9 0.0 all-to-all-done.2.back
  66.9 0.3 shard_map.85
  67.2 2.2 %shard_map.86.weight = bf16[1024,2048]{1,0:T(8,128)(2,1)S(1)} custom-call(bf16[1024,2048]{1,0:T(8,128)(2,1)} %bitcast.9, s32[8,128]{1,0:T(8,128)S(1)} %get-tuple-element.56.info.token), custom_call_target="tpu_custom_call" | custom-call | flops 1000 | bytes 1000 | tf_op jit(solution)/shard_map/pallas_call | solution.py:22
  69.4 1.1 %collective-permute-done.6.recv = bf16[96,2048]{1,0:T(8,128)(2,1)S(1)} collective-permute-done((bf16[96,2048]{1,0:T(8,128)(2,1)S(1)}, bf16[96,2048]{1,0:T(8,128)(2,1)S(1)}, u32[]{:S(2)}, u32[]{:S(2)}) %collective-permute-start.6) | collective-permute-done | bytes 393248 | tf_op jit(solution)/shard_map/ppermute | solution.py:44
  70.5 0.0 collective-permute-done.7.left
  70.5 0.0 collective-permute-done.8.right
  70.5 2.0 %shard_map.87 = (bf16[96,2048]{1,0:T(8,128)(2,1)}, bf16[8,16,512]{2,1,0:T(8,128)(2,1)S(1)}, bf16[8,16,512]{2,1,0:T(8,128)(2,1)S(1)}) custom-call(bf16[96,2048]{1,0:T(8,128)(2,1)S(1)} %collective-permute-done.6.recv, bf16[96,2048]{1,0:T(8,128)(2,1)S(1)} %get-tuple-element.37.hand, bf16[1024,2048]{1,0:T(8,128)(2,1)S(1)} %shard_map.86.weight, ...), custom_call_target="tpu_custom_call" | custom-call | flops 1000 | bytes 1000 | tf_op jit(solution)/shard_map/pallas_call | solution.py:22
  72.5 1.6 %collective-permute-start.9 = (bf16[8,16,512]{2,1,0:T(8,128)(2,1)S(1)}, bf16[8,16,512]{2,1,0:T(8,128)(2,1)S(1)}, u32[]{:S(2)}, u32[]{:S(2)}) collective-permute-start(bf16[8,16,512]{2,1,0:T(8,128)(2,1)S(1)} %get-tuple-element.58), channel_id=1, source_target_pairs={{0,16},{16,0},{1,17},{17,1},{2,18},{18,2},{3,19},{19,3},{4,20},{20... | collective-permute-start | bytes 393224 | tf_op jit(solution)/shard_map/ppermute | solution.py:44
  74.1 3.4 %shard_map.88.refs_3_ = f32[1024,2048]{1,0:T(8,128)} custom-call(bf16[1024,512]{1,0:T(8,128)(2,1)} %copy-done, bf16[256,2048]{1,0:T(8,128)(2,1)} %get-tuple-element.42.refs_0_, bf16[160,2048]{1,0:T(8,128)(2,1)} %get-tuple-element.47.refs_1_, bf16[96,2048]{1,0:T(8,128)(2,1)} %get-tuple-element.55.refs_2_), custom_call_target="tpu_custom_call" | custom-call | flops 1000 | bytes 1000 | tf_op jit(solution)/shard_map/pallas_call | solution.py:456
  77.4 0.1 collective-permute-done.9.right
  77.5 0.7 shard_map.90
  78.2 3.4 %all-to-all-start.3 = ((bf16[8,16,512]{2,1,0:T(8,128)(2,1)}), bf16[8,16,512]{2,1,0:T(8,128)(2,1)S(1)}, u32[]{:S(2)}, u32[]{:S(2)}) async-start(bf16[8,16,512]{2,1,0:T(8,128)(2,1)} %shard_map.90), calls=%async_computation.3 | async-start | bytes 262144 | tf_op jit(solution)/shard_map/all_to_all | solution.py:50
  81.6 1.6 %collective-permute-start.10 = (bf16[128,512]{1,0:T(8,128)(2,1)S(1)}, bf16[128,512]{1,0:T(8,128)(2,1)S(1)}, u32[]{:S(2)}, u32[]{:S(2)}) collective-permute-start(bf16[128,512]{1,0:T(8,128)(2,1)S(1)} %get-tuple-element.61), channel_id=1, source_target_pairs={{0,16},{16,0},{1,17},{17,1},{2,18},{18,2},{3,19},{19,3},{4,20},{20... | collective-permute-start | bytes 393224 | tf_op jit(solution)/shard_map/ppermute | solution.py:44
  83.1 5.8 %shard_map.89 = f32[1024,2048]{1,0:T(8,128)} custom-call(bf16[1024,512]{1,0:T(8,128)(2,1)} %copy-done, bf16[256,2048]{1,0:T(8,128)(2,1)} %get-tuple-element.42.refs_0_, bf16[160,2048]{1,0:T(8,128)(2,1)} %get-tuple-element.47.refs_1_, bf16[96,2048]{1,0:T(8,128)(2,1)} %get-tuple-element.55.refs_2_, ...), custom_call_target="tpu_custom_call", output_to_operand_aliasing={{}: (4, {})} | custom-call | flops 1000 | bytes 1000 | tf_op jit(solution)/shard_map/pallas_call | solution.py:456
  88.9 0.0 collective-permute-done.10.right
  88.9 0.0 all-to-all-done.3.back
  89.0 0.9 shard_map.91
Async XLA Ops:
  20.4 1.6 %collective-permute-start = (bf16[8,16,1152]{2,1,0:T(8,128)(2,1)S(1)}, bf16[8,16,1152]{2,1,0:T(8,128)(2,1)S(1)}, u32[]{:S(2)}, u32[]{:S(2)}) collective-permute-start(bf16[8,16,1152]{2,1,0:T(8,128)(2,1)S(1)} %all_to_all.20.refs_0_), channel_id=1, source_target_pairs={{0,1},{1,0},{2,3},{3,2},{4,5},{5,4},{6,7},{7,6},{8,9},{9,8},{10,11... | collective-permute-start | bytes 884744 | tf_op jit(solution)/shard_map/ppermute | solution.py:40
  22.8 18.1 %copy-start.1 = (s32[200]{0:T(256)S(1)}, s32[200]{0:T(256)}, u32[]{:S(2)}) copy-start(s32[200]{0:T(256)} %param.10) | copy-start | bytes 2404
  22.8 26.1 %collective-permute-start.2 = (bf16[256,2048]{1,0:T(8,128)(2,1)S(1)}, bf16[256,2048]{1,0:T(8,128)(2,1)S(1)}, u32[]{:S(2)}, u32[]{:S(2)}) collective-permute-start(bf16[256,2048]{1,0:T(8,128)(2,1)S(1)} %shard_map.79.hand), channel_id=1, source_target_pairs={{0,16},{16,0},{1,17},{17,1},{2,18},{18,2},{3,19},{19,3},{4,20},{20... | collective-permute-start | bytes 3145736 | tf_op jit(solution)/shard_map/ppermute | solution.py:44
  37.3 1.6 %collective-permute-start.1 = (bf16[8,16,1152]{2,1,0:T(8,128)(2,1)S(1)}, bf16[8,16,1152]{2,1,0:T(8,128)(2,1)S(1)}, u32[]{:S(2)}, u32[]{:S(2)}) collective-permute-start(bf16[8,16,1152]{2,1,0:T(8,128)(2,1)S(1)} %all_to_all.21.refs_0_.refs_2_), channel_id=1, source_target_pairs={{0,1},{1,0},{2,3},{3,2},{4,5},{5,4},{6,7},{7,6},{8,9},{9,8},{10,11... | collective-permute-start | bytes 884744 | tf_op jit(solution)/shard_map/ppermute | solution.py:40
  40.2 22.7 %collective-permute-start.3 = (bf16[160,2048]{1,0:T(8,128)(2,1)S(1)}, bf16[160,2048]{1,0:T(8,128)(2,1)S(1)}, u32[]{:S(2)}, u32[]{:S(2)}) collective-permute-start(bf16[160,2048]{1,0:T(8,128)(2,1)S(1)} %get-tuple-element.36.hand), channel_id=1, source_target_pairs={{0,16},{16,0},{1,17},{17,1},{2,18},{18,2},{3,19},{19,3},{4,20},{20... | collective-permute-start | bytes 1966088 | tf_op jit(solution)/shard_map/ppermute | solution.py:44
  43.7 7.2 %copy-start = (bf16[1024,512]{1,0:T(8,128)(2,1)}, bf16[1024,512]{1,0:T(8,128)(2,1)S(1)}, u32[]{:S(2)}) copy-start(bf16[1024,512]{1,0:T(8,128)(2,1)S(1)} %get-tuple-element.39.turned) | copy-start | bytes 3145732
  50.9 1.4 %collective-permute-start.4 = (bf16[128,512]{1,0:T(8,128)(2,1)S(1)}, bf16[128,512]{1,0:T(8,128)(2,1)S(1)}, u32[]{:S(2)}, u32[]{:S(2)}) collective-permute-start(bf16[128,512]{1,0:T(8,128)(2,1)S(1)} %get-tuple-element.44), channel_id=1, source_target_pairs={{0,1},{1,0},{2,3},{3,2},{4,5},{5,4},{6,7},{7,6},{8,9},{9,8},{10,11... | collective-permute-start | bytes 393224 | tf_op jit(solution)/shard_map/ppermute | solution.py:40
  51.0 1.5 %collective-permute-start.5 = (bf16[128,512]{1,0:T(8,128)(2,1)S(1)}, bf16[128,512]{1,0:T(8,128)(2,1)S(1)}, u32[]{:S(2)}, u32[]{:S(2)}) collective-permute-start(bf16[128,512]{1,0:T(8,128)(2,1)S(1)} %get-tuple-element.45), channel_id=1, source_target_pairs={{0,1},{1,0},{2,3},{3,2},{4,5},{5,4},{6,7},{7,6},{8,9},{9,8},{10,11... | collective-permute-start | bytes 393224 | tf_op jit(solution)/shard_map/ppermute | solution.py:40
  53.3 13.6 %all-to-all-start.2 = ((bf16[8,16,1024]{2,1,0:T(8,128)(2,1)}), bf16[8,16,1024]{2,1,0:T(8,128)(2,1)S(1)}, u32[]{:S(2)}, u32[]{:S(2)}) async-start(bf16[8,16,1024]{2,1,0:T(8,128)(2,1)} %shard_map.83), calls=%async_computation.2 | async-start | bytes 524288 | tf_op jit(solution)/shard_map/all_to_all | solution.py:50
  56.7 13.8 %collective-permute-start.6 = (bf16[96,2048]{1,0:T(8,128)(2,1)S(1)}, bf16[96,2048]{1,0:T(8,128)(2,1)S(1)}, u32[]{:S(2)}, u32[]{:S(2)}) collective-permute-start(bf16[96,2048]{1,0:T(8,128)(2,1)S(1)} %get-tuple-element.37.hand), channel_id=1, source_target_pairs={{0,16},{16,0},{1,17},{17,1},{2,18},{18,2},{3,19},{19,3},{4,20},{20... | collective-permute-start | bytes 1179656 | tf_op jit(solution)/shard_map/ppermute | solution.py:44
  66.3 4.2 %collective-permute-start.7 = (bf16[128,512]{1,0:T(8,128)(2,1)S(1)}, bf16[128,512]{1,0:T(8,128)(2,1)S(1)}, u32[]{:S(2)}, u32[]{:S(2)}) collective-permute-start(bf16[128,512]{1,0:T(8,128)(2,1)S(1)} %get-tuple-element.53), channel_id=1, source_target_pairs={{0,1},{1,0},{2,3},{3,2},{4,5},{5,4},{6,7},{7,6},{8,9},{9,8},{10,11... | collective-permute-start | bytes 393224 | tf_op jit(solution)/shard_map/ppermute | solution.py:40
  66.4 4.1 %collective-permute-start.8 = (bf16[128,512]{1,0:T(8,128)(2,1)S(1)}, bf16[128,512]{1,0:T(8,128)(2,1)S(1)}, u32[]{:S(2)}, u32[]{:S(2)}) collective-permute-start(bf16[128,512]{1,0:T(8,128)(2,1)S(1)} %get-tuple-element.54), channel_id=1, source_target_pairs={{0,1},{1,0},{2,3},{3,2},{4,5},{5,4},{6,7},{7,6},{8,9},{9,8},{10,11... | collective-permute-start | bytes 393224 | tf_op jit(solution)/shard_map/ppermute | solution.py:40
  72.5 5.0 %collective-permute-start.9 = (bf16[8,16,512]{2,1,0:T(8,128)(2,1)S(1)}, bf16[8,16,512]{2,1,0:T(8,128)(2,1)S(1)}, u32[]{:S(2)}, u32[]{:S(2)}) collective-permute-start(bf16[8,16,512]{2,1,0:T(8,128)(2,1)S(1)} %get-tuple-element.58), channel_id=1, source_target_pairs={{0,16},{16,0},{1,17},{17,1},{2,18},{18,2},{3,19},{19,3},{4,20},{20... | collective-permute-start | bytes 393224 | tf_op jit(solution)/shard_map/ppermute | solution.py:44
  78.2 10.8 %all-to-all-start.3 = ((bf16[8,16,512]{2,1,0:T(8,128)(2,1)}), bf16[8,16,512]{2,1,0:T(8,128)(2,1)S(1)}, u32[]{:S(2)}, u32[]{:S(2)}) async-start(bf16[8,16,512]{2,1,0:T(8,128)(2,1)} %shard_map.90), calls=%async_computation.3 | async-start | bytes 262144 | tf_op jit(solution)/shard_map/all_to_all | solution.py:50
  81.6 7.4 %collective-permute-start.10 = (bf16[128,512]{1,0:T(8,128)(2,1)S(1)}, bf16[128,512]{1,0:T(8,128)(2,1)S(1)}, u32[]{:S(2)}, u32[]{:S(2)}) collective-permute-start(bf16[128,512]{1,0:T(8,128)(2,1)S(1)} %get-tuple-element.61), channel_id=1, source_target_pairs={{0,16},{16,0},{1,17},{17,1},{2,18},{18,2},{3,19},{19,3},{4,20},{20... | collective-permute-start | bytes 393224 | tf_op jit(solution)/shard_map/ppermute | solution.py:44
